TPU v7x, 32 devices: a whole 2x2x4 slice. The times are simulated.
32 devices in a mesh: grp: 2 (over x), lat: 8 (over z, y), lon: 2 (over core).
Axes of the slice: x: 2, y: 2, z: 4, core: 2. Of those that a mesh axis runs over, the one named last changes fastest.
Arguments:
- perturb: float32 [256, 256, 192], P(('grp', 'lat'), 'lon'), parts along dimension 0, may hold values from -110 to 110, as said below
- kernels: float32 [2, 7, 7, 192], replicated, may hold values from -0.875 to 0.875
- gains: float32 [2, 192], replicated, may hold values from 0.5 to 1.5
- w_in: bfloat16 [2, 192, 768], replicated, may hold values from -0.4375 to 0.4375
- w_out: bfloat16 [2, 768, 192], replicated, may hold values from -0.21875 to 0.21875
- scales: float32 [2, 192], replicated, may hold values from 0.3 to 1.5
- normed: bfloat16 [2, 256, 256, 192], P(None, ('grp', 'lat'), 'lon'), parts along dimension 1, may hold values from -6 to 6
- inv_std: float32 [2, 256, 256], P(None, ('grp', 'lat'), 'lon'), parts along dimension 1, may hold values from 0.5 to 2
- slope: bfloat16 [2, 256, 256, 768], P(None, ('grp', 'lat'), 'lon'), parts along dimension 1, may hold values from -0.099609375 to 1.09375
Outputs:
- new_vec: float32 [256, 256, 192], P(('grp', 'lat'), 'lon'), parts along dimension 0
- growth: float32 [2], P('grp'), parts along dimension 0
There are 2 independent parts, one for each index of `grp`. A program takes and returns all parts, laid end to end along the dimension named above; an argument that names none is the same for every part. Nothing has to cross between parts.
Inputs may be any that keep to these rules, and one draw needn't show every extreme that they name: `perturb`: the initial perturbation.
All inputs are finite; a program needn't handle non-finite values.
Results may differ from a plain program's by a relative error of at most 0.0075.
Values may be sent and summed in bfloat16 or wider, within the bound.
No kernel may reach another device: no remote copies, remote signals or barrier semaphores. Data moves between devices by JAX's collectives and lax.ppermute only.
A program may use at most 64 MiB of HBM per device.

v0:
```python
import math

import jax
import jax.numpy as jnp
from jax import lax
from jax.sharding import PartitionSpec as P

lat_span = 70.0 * math.pi / 180.0


def extended(x, sides, width, wrap):
    for axis, dim in sides:
        size, length = (lax.axis_size(axis), x.shape[dim])
        up = [(i, (i + 1) % size) for i in range(size if wrap else size - 1)]
        down = [(j, i) for i, j in up]
        last = lax.slice_in_dim(x, length - width, length, axis=dim)
        initial = lax.slice_in_dim(x, 0, width, axis=dim)
        before = lax.ppermute(last, axis, up)
        after = lax.ppermute(initial, axis, down)
        x = jnp.concatenate([before, x, after], axis=dim)
    return x


def tangent_pad(rounded):
    widened = extended(rounded, (("lon", 1),), 3, True)
    return extended(widened, (("lat", 0),), 3, False)


def adjoint_pad(rounded):
    widened = extended(rounded, (("lon", 1),), 3, True)
    return extended(widened, (("lat", 0),), 3, False)


def window_sum(padded, kernel, row_count, col_count, flipped):
    summed = jnp.zeros((row_count, col_count, padded.shape[2]), jnp.float32)
    for row_off in range(7):
        for col_off in range(7):
            row_start = 6 - row_off if flipped else row_off
            col_start = 6 - col_off if flipped else col_off
            window_part = padded[
                row_start : row_start + row_count, col_start : col_start + col_count
            ].astype(jnp.float32)
            summed = summed + kernel[row_off, col_off] * window_part
    return summed


def project(values, normed_layer, inv_layer):
    normal_f = normed_layer.astype(jnp.float32)
    centred = (
        values
        - jnp.mean(values, axis=-1, keepdims=True)
        - normal_f * jnp.mean(normal_f * values, axis=-1, keepdims=True)
    )
    return inv_layer[..., None] * centred


def on_device(perturb, kernels, gains, w_in, w_out, scales, normed, inv_std, slope):
    row_count, col_count, chans = perturb.shape
    lat_total = row_count * lax.axis_size("lat")
    lon_total = col_count * lax.axis_size("lon")
    local_rows = (lax.axis_index("lat") * row_count + jnp.arange(row_count)).astype(jnp.float32)
    area_rows = jnp.cos(lat_span * (local_rows + 0.5) / lat_total)
    area_w = area_rows[:, None, None]
    every_row = jnp.arange(lat_total).astype(jnp.float32)
    weight_total = jnp.sum(jnp.cos(lat_span * (every_row + 0.5) / lat_total)) * lon_total * chans
    layer_count = kernels.shape[0]
    tangent = perturb
    for layer_index in range(layer_count):
        rounded = tangent.astype(jnp.bfloat16)
        padded = tangent_pad(rounded)
        conv_out = window_sum(padded, kernels[layer_index], row_count, col_count, False)
        tangent_norm = project(conv_out, normed[layer_index], inv_std[layer_index])
        operand = (gains[layer_index] * tangent_norm).astype(jnp.bfloat16)
        hidden_pre = jnp.dot(operand, w_in[layer_index], preferred_element_type=jnp.float32)
        gated = (slope[layer_index] * hidden_pre).astype(jnp.bfloat16)
        branch_out = jnp.dot(gated, w_out[layer_index], preferred_element_type=jnp.float32)
        tangent = tangent + scales[layer_index] * branch_out
    start_local = jnp.sum(area_w * perturb * perturb)
    forward_local = jnp.sum(area_w * tangent * tangent)
    grad_field = area_w * tangent
    for layer_index in range(layer_count - 1, -1, -1):
        scaled = (scales[layer_index] * grad_field).astype(jnp.bfloat16)
        hidden_back = lax.dot_general(
            scaled, w_out[layer_index], (((2,), (1,)), ((), ())), preferred_element_type=jnp.float32
        )
        gated = (slope[layer_index] * hidden_back).astype(jnp.bfloat16)
        chan_back = lax.dot_general(
            gated, w_in[layer_index], (((2,), (1,)), ((), ())), preferred_element_type=jnp.float32
        )
        conv_grad = project(
            gains[layer_index] * chan_back, normed[layer_index], inv_std[layer_index]
        ).astype(jnp.bfloat16)
        padded = adjoint_pad(conv_grad)
        conv_back = window_sum(padded, kernels[layer_index], row_count, col_count, True)
        grad_field = grad_field + conv_back
    adjoint_out = grad_field / area_w
    adjoint_local = jnp.sum(area_w * adjoint_out * adjoint_out)
    start_sum, forward_sum, adjoint_sum = lax.psum(
        (start_local, forward_local, adjoint_local), ("lat", "lon")
    )
    start_sq = start_sum / weight_total
    forward_sq = forward_sum / weight_total
    adjoint_sq = adjoint_sum / weight_total
    growth = jnp.sqrt(forward_sq / (start_sq + 1e-06)).reshape(1)
    new_vec = adjoint_out / jnp.sqrt(adjoint_sq + 1e-06)
    return (new_vec, growth)


def solution(mesh):
    in_specs = (
        P(("grp", "lat"), "lon", None),
        P(),
        P(),
        P(),
        P(),
        P(),
        P(None, ("grp", "lat"), "lon", None),
        P(None, ("grp", "lat"), "lon"),
        P(None, ("grp", "lat"), "lon", None),
    )
    out_specs = (P(("grp", "lat"), "lon", None), P("grp"))
    return jax.shard_map(
        on_device, mesh=mesh, in_specs=in_specs, out_specs=out_specs, check_vma=False
    )
```

profile of v0, /device:TPU:0, one launch (start us, length us, event | category | flops | bytes accessed | tf_op | source)
XLA Modules:
  0.0 238.3 jit_solution(1238597391319515903)
XLA Ops:
  0.6 1.5 convert_element_type.665
  2.9 0.5 collective-permute-start
  4.5 0.6 fusion.150
  5.1 0.7 fusion.145
  5.8 0.6 fusion.151
  6.4 0.4 copy.16
  6.9 0.4 copy.17
  7.7 4.9 %collective-permute-start.2 = (bf16[3,134,192]{1,2,0:T(8,128)(2,1)S(1)}, bf16[3,134,192]{1,2,0:T(8,128)(2,1)S(1)}, u32[]{:S(2)}, u32[]{:S(2)}) collective-permute-start(bf16[3,134,192]{1,2,0:T(8,128)(2,1)S(1)} %get-tuple-element.33), channel_id=1, source_target_pairs={{0,2},{2,4},{4,6},{6,8},{8,10},{10,12},{12,14},{1,3},{3,5},{5,7},{... | collective-permute-start | bytes 463112 | tf_op jit(solution)/shard_map/ppermute | solution.py:18
  12.6 1.3 collective-permute-start.3
  13.9 0.6 fusion.152
  14.5 10.8 %collective-permute-done.2 = bf16[3,134,192]{1,2,0:T(8,128)(2,1)S(1)} collective-permute-done((bf16[3,134,192]{1,2,0:T(8,128)(2,1)S(1)}, bf16[3,134,192]{1,2,0:T(8,128)(2,1)S(1)}, u32[]{:S(2)}, u32[]{:S(2)}) %collective-permute-start.2) | collective-permute-done | bytes 154400 | tf_op jit(solution)/shard_map/ppermute | solution.py:18
  25.3 2.2 maximum_maximum_fusion
  28.0 18.3 %fusion.139 = (f32[16,128]{1,0:T(8,128)S(1)}, f32[16,128]{1,0:T(8,128)S(1)}, f32[16,128,192]{1,2,0:T(8,128)}) fusion(bf16[2,16,128,192]{2,3,1,0:T(8,128)(2,1)S(1)} %copy-done.5, bf16[19,134,192]{1,2,0:T(8,128)(2,1)S(1)} %get-tuple-element.32, f32[192]{0:T(256)S(1)} %bitcast.247, f32[192]{0:T(256)S(1)} %bitcast.249, f32[192]{0:T(256)S(1)} %bitcast.251, ...), kind=kLoop, calls=%fused_computation.193 | loop fusion | flops 66056192 | bytes 36266752 | tf_op jit(solution)/shard_map/reduce_sum | solution.py:51
  46.3 6.5 %fusion.153 = (bf16[16,128,192]{1,2,0:T(8,128)(2,1)S(1)}, f32[16,128,192]{1,2,0:T(8,128)}) fusion(f32[16,128,192]{1,2,0:T(8,128)} %param.9, bf16[2,768,192]{1,2,0:T(8,128)(2,1)S(1)} %copy-done.170, bf16[2,16,128,768]{3,2,1,0:T(8,128)(2,1)} %param.17, f32[16,128,192]{1,2,0:T(8,128)} %get-tuple-element.18, f32[16,128]{1,0:T(8,128)S(1)} %broadcast_multiply_fusion.6, ...), kind=kOutput, calls=%fused_computation.207 | convolution fusion | flops 1216610304 | bytes 10053632 | tf_op jit(solution)/shard_map/dot_general | solution.py:76
  54.0 0.6 collective-permute-start.5
  54.5 0.7 fusion.146
  55.2 0.4 copy.23
  55.6 0.4 copy.24
  56.4 4.4 %collective-permute-start.6 = (bf16[3,134,192]{1,2,0:T(8,128)(2,1)S(1)}, bf16[3,134,192]{1,2,0:T(8,128)(2,1)S(1)}, u32[]{:S(2)}, u32[]{:S(2)}) collective-permute-start(bf16[3,134,192]{1,2,0:T(8,128)(2,1)S(1)} %get-tuple-element.29), channel_id=1, source_target_pairs={{0,2},{2,4},{4,6},{6,8},{8,10},{10,12},{12,14},{1,3},{3,5},{5,7},{... | collective-permute-start | bytes 463112 | tf_op jit(solution)/shard_map/ppermute | solution.py:18
  60.9 1.5 collective-permute-start.7
  62.3 1.6 fusion.147
  63.9 0.6 multiply_cosine_fusion
  64.8 8.8 %collective-permute-done.6 = bf16[3,134,192]{1,2,0:T(8,128)(2,1)S(1)} collective-permute-done((bf16[3,134,192]{1,2,0:T(8,128)(2,1)S(1)}, bf16[3,134,192]{1,2,0:T(8,128)(2,1)S(1)}, u32[]{:S(2)}, u32[]{:S(2)}) %collective-permute-start.6) | collective-permute-done | bytes 154400 | tf_op jit(solution)/shard_map/ppermute | solution.py:18
  73.6 2.2 maximum_maximum_fusion.1
  76.3 18.0 %fusion.138 = (f32[16,128]{1,0:T(8,128)S(1)}, f32[16,128]{1,0:T(8,128)S(1)}, f32[16,128,192]{1,2,0:T(8,128)}) fusion(bf16[2,16,128,192]{2,3,1,0:T(8,128)(2,1)S(1)} %copy-done.6, bf16[19,134,192]{1,2,0:T(8,128)(2,1)S(1)} %get-tuple-element.28, f32[192]{0:T(256)S(1)} %bitcast.285, f32[192]{0:T(256)S(1)} %bitcast.287, f32[192]{0:T(256)S(1)} %bitcast.289, ...), kind=kLoop, calls=%fused_computation.192 | loop fusion | flops 66056192 | bytes 36266752 | tf_op jit(solution)/shard_map/reduce_sum | solution.py:51
  94.4 5.4 %multiply_add_fusion.1 = f32[16,128,192]{1,2,0:T(8,128)S(1)} fusion(f32[16,128,192]{1,2,0:T(8,128)} %get-tuple-element.150, bf16[2,16,128,768]{3,2,1,0:T(8,128)(2,1)} %param.17, f32[16,128,192]{1,2,0:T(8,128)} %get-tuple-element.17, f32[16,128]{1,0:T(8,128)S(1)} %broadcast_multiply_fusion.4, f32[16,128]{1,0:T(8,128)S(1)} %broadcast_multiply_fusion.5, ...), kind=kOutput, calls=%fused_computation.101 | convolution fusion | flops 1216217088 | bytes 9267200 | tf_op jit(solution)/shard_map/dot_general | solution.py:76
  99.9 6.0 %fusion.137 = (f32[16,128]{1,0:T(8,128)S(1)}, f32[16,128]{1,0:T(8,128)S(1)}, f32[16,128,192]{1,2,0:T(8,128)}) fusion(bf16[2,16,128,192]{2,3,1,0:T(8,128)(2,1)S(1)} %copy-done.7, bf16[2,192,768]{2,1,0:T(8,128)(2,1)} %param.12, bf16[2,16,128,768]{3,2,1,0:T(8,128)(2,1)} %param.17, f32[16,128,192]{1,2,0:T(8,128)S(1)} %multiply_add_fusion.1, ...), kind=kOutput, calls=%fused_computation.191 | convolution fusion | flops 1215819776 | bytes 7685696 | tf_op jit(solution)/shard_map/dot_general | solution.py:87
  105.9 1.7 fusion.49
  108.8 0.6 collective-permute-start.9
  109.6 0.4 copy.29
  111.0 1.3 collective-permute-start.10
  112.7 5.4 %collective-permute-start.11 = (bf16[3,134,192]{1,2,0:T(8,128)(2,1)S(1)}, bf16[3,134,192]{1,2,0:T(8,128)(2,1)S(1)}, u32[]{:S(2)}, u32[]{:S(2)}) collective-permute-start(bf16[3,134,192]{1,2,0:T(8,128)(2,1)S(1)} %get-tuple-element.26), channel_id=1, source_target_pairs={{0,2},{2,4},{4,6},{6,8},{8,10},{10,12},{12,14},{1,3},{3,5},{5,7},{... | collective-permute-start | bytes 463112 | tf_op jit(solution)/shard_map/ppermute | solution.py:18
  118.1 4.8 %collective-permute-done.10 = bf16[3,134,192]{1,2,0:T(8,128)(2,1)S(1)} collective-permute-done((bf16[3,134,192]{1,2,0:T(8,128)(2,1)S(1)}, bf16[3,134,192]{1,2,0:T(8,128)(2,1)S(1)}, u32[]{:S(2)}, u32[]{:S(2)}) %collective-permute-start.10) | collective-permute-done | bytes 154400 | tf_op jit(solution)/shard_map/ppermute | solution.py:19
  122.9 7.2 %collective-permute-done.11 = bf16[3,134,192]{1,2,0:T(8,128)(2,1)S(1)} collective-permute-done((bf16[3,134,192]{1,2,0:T(8,128)(2,1)S(1)}, bf16[3,134,192]{1,2,0:T(8,128)(2,1)S(1)}, u32[]{:S(2)}, u32[]{:S(2)}) %collective-permute-start.11) | collective-permute-done | bytes 154400 | tf_op jit(solution)/shard_map/ppermute | solution.py:18
  130.1 2.2 pad_maximum_fusion.2
  132.7 17.1 %multiply_add_fusion = f32[16,128,192]{1,2,0:T(8,128)} fusion(f32[16,128,192]{1,2,0:T(8,128)S(1)} %copy-done.1, bf16[16,128,192]{1,2,0:T(8,128)(2,1)S(1)} %fusion.49, bf16[16,3,192]{1,2,0:T(8,128)(2,1)S(1)} %copy.29, bf16[16,3,192]{1,2,0:T(8,128)(2,1)S(1)} %copy.30, bf16[19,134,192]{1,2,0:T(8,128)(2,1)S(1)} %get-tuple-element.24, ...), kind=kLoop, calls=%fused_computation.35 | loop fusion | flops 65273856 | bytes 37036864 | tf_op jit(solution)/shard_map/add | solution.py:95
  149.8 6.2 %fusion.136 = (f32[16,128]{1,0:T(8,128)S(1)}, f32[16,128]{1,0:T(8,128)S(1)}, f32[16,128,192]{1,2,0:T(8,128)}) fusion(bf16[2,16,128,192]{2,3,1,0:T(8,128)(2,1)} %param.15, bf16[2,192,768]{2,1,0:T(8,128)(2,1)} %param.12, bf16[2,16,128,768]{3,2,1,0:T(8,128)(2,1)} %param.17, f32[16,128,192]{1,2,0:T(8,128)} %multiply_add_fusion, f32[192]{0:T(256)} %bitcast, ...), kind=kOutput, calls=%fused_computation.190 | convolution fusion | flops 1215426560 | bytes 7686144 | tf_op jit(solution)/shard_map/dot_general | solution.py:87
  156.0 1.8 fusion.40
  158.9 0.5 collective-permute-start.13
  161.1 1.3 collective-permute-start.14
  162.4 5.3 %collective-permute-start.15 = (bf16[3,134,192]{1,2,0:T(8,128)(2,1)S(1)}, bf16[3,134,192]{1,2,0:T(8,128)(2,1)S(1)}, u32[]{:S(2)}, u32[]{:S(2)}) collective-permute-start(bf16[3,134,192]{1,2,0:T(8,128)(2,1)S(1)} %get-tuple-element.22), channel_id=1, source_target_pairs={{0,2},{2,4},{4,6},{6,8},{8,10},{10,12},{12,14},{1,3},{3,5},{5,7},{... | collective-permute-start | bytes 463112 | tf_op jit(solution)/shard_map/ppermute | solution.py:18
  167.7 0.7 cosine_reduce_fusion
  169.4 3.6 %collective-permute-done.14 = bf16[3,134,192]{1,2,0:T(8,128)(2,1)S(1)} collective-permute-done((bf16[3,134,192]{1,2,0:T(8,128)(2,1)S(1)}, bf16[3,134,192]{1,2,0:T(8,128)(2,1)S(1)}, u32[]{:S(2)}, u32[]{:S(2)}) %collective-permute-start.14) | collective-permute-done | bytes 154400 | tf_op jit(solution)/shard_map/ppermute | solution.py:19
  173.0 6.5 %collective-permute-done.15 = bf16[3,134,192]{1,2,0:T(8,128)(2,1)S(1)} collective-permute-done((bf16[3,134,192]{1,2,0:T(8,128)(2,1)S(1)}, bf16[3,134,192]{1,2,0:T(8,128)(2,1)S(1)}, u32[]{:S(2)}, u32[]{:S(2)}) %collective-permute-start.15) | collective-permute-done | bytes 154400 | tf_op jit(solution)/shard_map/ppermute | solution.py:18
  179.5 2.2 pad_maximum_fusion.3
  182.1 18.2 %fusion.31 = (f32[]{:T(128)}, f32[]{:T(128)}, f32[]{:T(128)}, f32[16,128,192]{1,2,0:T(8,128)}) fusion(f32[16,128,192]{1,2,0:T(8,128)S(1)} %copy-done.4, f32[16]{0:T(128)} %multiply_cosine_fusion, f32[16,128,192]{1,2,0:T(8,128)S(1)} %copy-done.2, f32[16,128,192]{1,2,0:T(8,128)S(1)} %copy-done.3, bf16[19,134,192]{1,2,0:T(8,128)(2,1)S(1)} %get-tuple-element.20, ...), kind=kLoop, calls=%fused_computation.80 | loop fusion | flops 68812800 | bytes 40182604 | tf_op jit(solution)/shard_map/reduce_sum | solution.py:78
  200.3 32.1 %all-reduce = (f32[]{:T(128)}, f32[]{:T(128)}, f32[]{:T(128)}) all-reduce(f32[]{:T(128)} %get-tuple-element.11, f32[]{:T(128)} %get-tuple-element.12, f32[]{:T(128)} %get-tuple-element.10), channel_id=1, replica_groups=mesh['grp'=2,'lat'=8,'lon'=2] {'lat','lon'}, use_global_device_ids=true, to_apply=%region_9.0 | all-reduce | flops 3 | bytes 24 | tf_op jit(solution)/shard_map/psum | solution.py:98
  234.4 2.8 %broadcast_divide_fusion = f32[16,128,192]{1,2,0:T(8,128)} fusion(f32[16,128,192]{1,2,0:T(8,128)} %get-tuple-element.16, f32[16]{0:T(128)S(1)} %broadcast_multiply_fusion.8), kind=kLoop, calls=%fused_computation.133 | loop fusion | flops 393216 | bytes 3145792 | tf_op jit(solution)/shard_map/div | solution.py:105
  (389 shorter events, 9.2 us)
Async XLA Ops:
  2.9 3.5 %collective-permute-start = (bf16[16,3,192]{2,0,1:T(8,128)(2,1)S(1)}, bf16[16,3,192]{2,0,1:T(8,128)(2,1)S(1)}, u32[]{:S(2)}, u32[]{:S(2)}) collective-permute-start(bf16[16,3,192]{2,0,1:T(8,128)(2,1)S(1)} %copy.14), channel_id=1, source_target_pairs={{0,1},{1,0},{2,3},{3,2},{4,5},{5,4},{6,7},{7,6},{8,9},{9,8},{10,11... | collective-permute-start | bytes 55304 | tf_op jit(solution)/shard_map/ppermute | solution.py:18
  3.8 3.0 %collective-permute-start.1 = (bf16[16,3,192]{2,0,1:T(8,128)(2,1)S(1)}, bf16[16,3,192]{2,0,1:T(8,128)(2,1)S(1)}, u32[]{:S(2)}, u32[]{:S(2)}) collective-permute-start(bf16[16,3,192]{2,0,1:T(8,128)(2,1)S(1)} %copy.15), channel_id=1, source_target_pairs={{1,0},{0,1},{3,2},{2,3},{5,4},{4,5},{7,6},{6,7},{9,8},{8,9},{11,10... | collective-permute-start | bytes 55304 | tf_op jit(solution)/shard_map/ppermute | solution.py:19
  4.1 50.5 %copy-start.9 = (f32[7,7,192]{2,1,0:T(8,128)}, f32[7,7,192]{2,1,0:T(8,128)S(1)}, u32[]{:S(2)}) copy-start(f32[7,7,192]{2,1,0:T(8,128)S(1)} %get-tuple-element.153) | copy-start | bytes 112900
  4.1 23.5 %copy-start.12 = (f32[1,1,192]{2,1,0:T(1,128)}, f32[1,1,192]{2,1,0:T(1,128)S(1)}, u32[]{:S(2)}) copy-start(f32[1,1,192]{2,1,0:T(1,128)S(1)} %get-tuple-element.113) | copy-start | bytes 2308
  4.1 23.5 %copy-start.14 = (f32[1,1,192]{2,1,0:T(1,128)}, f32[1,1,192]{2,1,0:T(1,128)S(1)}, u32[]{:S(2)}) copy-start(f32[1,1,192]{2,1,0:T(1,128)S(1)} %get-tuple-element.114) | copy-start | bytes 2308
  4.1 23.5 %copy-start.16 = (f32[1,1,192]{2,1,0:T(1,128)}, f32[1,1,192]{2,1,0:T(1,128)S(1)}, u32[]{:S(2)}) copy-start(f32[1,1,192]{2,1,0:T(1,128)S(1)} %get-tuple-element.115) | copy-start | bytes 2308
  4.1 23.5 %copy-start.18 = (f32[1,1,192]{2,1,0:T(1,128)}, f32[1,1,192]{2,1,0:T(1,128)S(1)}, u32[]{:S(2)}) copy-start(f32[1,1,192]{2,1,0:T(1,128)S(1)} %get-tuple-element.116) | copy-start | bytes 2308
  4.1 23.5 %copy-start.20 = (f32[1,1,192]{2,1,0:T(1,128)}, f32[1,1,192]{2,1,0:T(1,128)S(1)}, u32[]{:S(2)}) copy-start(f32[1,1,192]{2,1,0:T(1,128)S(1)} %get-tuple-element.117) | copy-start | bytes 2308
  4.1 23.5 %copy-start.22 = (f32[1,1,192]{2,1,0:T(1,128)}, f32[1,1,192]{2,1,0:T(1,128)S(1)}, u32[]{:S(2)}) copy-start(f32[1,1,192]{2,1,0:T(1,128)S(1)} %get-tuple-element.118) | copy-start | bytes 2308
  4.1 23.5 %copy-start.24 = (f32[1,1,192]{2,1,0:T(1,128)}, f32[1,1,192]{2,1,0:T(1,128)S(1)}, u32[]{:S(2)}) copy-start(f32[1,1,192]{2,1,0:T(1,128)S(1)} %get-tuple-element.119) | copy-start | bytes 2308
  4.2 23.5 %copy-start.26 = (f32[1,1,192]{2,1,0:T(1,128)}, f32[1,1,192]{2,1,0:T(1,128)S(1)}, u32[]{:S(2)}) copy-start(f32[1,1,192]{2,1,0:T(1,128)S(1)} %get-tuple-element.120) | copy-start | bytes 2308
  4.2 23.5 %copy-start.28 = (f32[1,1,192]{2,1,0:T(1,128)}, f32[1,1,192]{2,1,0:T(1,128)S(1)}, u32[]{:S(2)}) copy-start(f32[1,1,192]{2,1,0:T(1,128)S(1)} %get-tuple-element.121) | copy-start | bytes 2308
  4.2 23.5 %copy-start.30 = (f32[1,1,192]{2,1,0:T(1,128)}, f32[1,1,192]{2,1,0:T(1,128)S(1)}, u32[]{:S(2)}) copy-start(f32[1,1,192]{2,1,0:T(1,128)S(1)} %get-tuple-element.122) | copy-start | bytes 2308
  4.2 23.5 %copy-start.32 = (f32[1,1,192]{2,1,0:T(1,128)}, f32[1,1,192]{2,1,0:T(1,128)S(1)}, u32[]{:S(2)}) copy-start(f32[1,1,192]{2,1,0:T(1,128)S(1)} %get-tuple-element.123) | copy-start | bytes 2308
  4.2 23.5 %copy-start.34 = (f32[1,1,192]{2,1,0:T(1,128)}, f32[1,1,192]{2,1,0:T(1,128)S(1)}, u32[]{:S(2)}) copy-start(f32[1,1,192]{2,1,0:T(1,128)S(1)} %get-tuple-element.124) | copy-start | bytes 2308
  4.2 23.5 %copy-start.36 = (f32[1,1,192]{2,1,0:T(1,128)}, f32[1,1,192]{2,1,0:T(1,128)S(1)}, u32[]{:S(2)}) copy-start(f32[1,1,192]{2,1,0:T(1,128)S(1)} %get-tuple-element.125) | copy-start | bytes 2308
  4.2 23.5 %copy-start.38 = (f32[1,1,192]{2,1,0:T(1,128)}, f32[1,1,192]{2,1,0:T(1,128)S(1)}, u32[]{:S(2)}) copy-start(f32[1,1,192]{2,1,0:T(1,128)S(1)} %get-tuple-element.126) | copy-start | bytes 2308
  4.2 23.5 %copy-start.40 = (f32[1,1,192]{2,1,0:T(1,128)}, f32[1,1,192]{2,1,0:T(1,128)S(1)}, u32[]{:S(2)}) copy-start(f32[1,1,192]{2,1,0:T(1,128)S(1)} %get-tuple-element.127) | copy-start | bytes 2308
  4.2 23.5 %copy-start.42 = (f32[1,1,192]{2,1,0:T(1,128)}, f32[1,1,192]{2,1,0:T(1,128)S(1)}, u32[]{:S(2)}) copy-start(f32[1,1,192]{2,1,0:T(1,128)S(1)} %get-tuple-element.128) | copy-start | bytes 2308
  4.2 23.5 %copy-start.44 = (f32[1,1,192]{2,1,0:T(1,128)}, f32[1,1,192]{2,1,0:T(1,128)S(1)}, u32[]{:S(2)}) copy-start(f32[1,1,192]{2,1,0:T(1,128)S(1)} %get-tuple-element.129) | copy-start | bytes 2308
  4.3 23.5 %copy-start.46 = (f32[1,1,192]{2,1,0:T(1,128)}, f32[1,1,192]{2,1,0:T(1,128)S(1)}, u32[]{:S(2)}) copy-start(f32[1,1,192]{2,1,0:T(1,128)S(1)} %get-tuple-element.130) | copy-start | bytes 2308
  4.3 23.5 %copy-start.48 = (f32[1,1,192]{2,1,0:T(1,128)}, f32[1,1,192]{2,1,0:T(1,128)S(1)}, u32[]{:S(2)}) copy-start(f32[1,1,192]{2,1,0:T(1,128)S(1)} %get-tuple-element.131) | copy-start | bytes 2308
  4.3 23.4 %copy-start.50 = (f32[1,1,192]{2,1,0:T(1,128)}, f32[1,1,192]{2,1,0:T(1,128)S(1)}, u32[]{:S(2)}) copy-start(f32[1,1,192]{2,1,0:T(1,128)S(1)} %get-tuple-element.94) | copy-start | bytes 2308
  4.3 23.4 %copy-start.52 = (f32[1,1,192]{2,1,0:T(1,128)}, f32[1,1,192]{2,1,0:T(1,128)S(1)}, u32[]{:S(2)}) copy-start(f32[1,1,192]{2,1,0:T(1,128)S(1)} %get-tuple-element.95) | copy-start | bytes 2308
  4.3 23.4 %copy-start.54 = (f32[1,1,192]{2,1,0:T(1,128)}, f32[1,1,192]{2,1,0:T(1,128)S(1)}, u32[]{:S(2)}) copy-start(f32[1,1,192]{2,1,0:T(1,128)S(1)} %get-tuple-element.96) | copy-start | bytes 2308
  4.3 23.4 %copy-start.56 = (f32[1,1,192]{2,1,0:T(1,128)}, f32[1,1,192]{2,1,0:T(1,128)S(1)}, u32[]{:S(2)}) copy-start(f32[1,1,192]{2,1,0:T(1,128)S(1)} %get-tuple-element.97) | copy-start | bytes 2308
  4.3 23.4 %copy-start.58 = (f32[1,1,192]{2,1,0:T(1,128)}, f32[1,1,192]{2,1,0:T(1,128)S(1)}, u32[]{:S(2)}) copy-start(f32[1,1,192]{2,1,0:T(1,128)S(1)} %get-tuple-element.98) | copy-start | bytes 2308
  4.4 23.4 %copy-start.60 = (f32[1,1,192]{2,1,0:T(1,128)}, f32[1,1,192]{2,1,0:T(1,128)S(1)}, u32[]{:S(2)}) copy-start(f32[1,1,192]{2,1,0:T(1,128)S(1)} %get-tuple-element.99) | copy-start | bytes 2308
  4.4 23.4 %copy-start.62 = (f32[1,1,192]{2,1,0:T(1,128)}, f32[1,1,192]{2,1,0:T(1,128)S(1)}, u32[]{:S(2)}) copy-start(f32[1,1,192]{2,1,0:T(1,128)S(1)} %get-tuple-element.100) | copy-start | bytes 2308
  4.4 23.4 %copy-start.64 = (f32[1,1,192]{2,1,0:T(1,128)}, f32[1,1,192]{2,1,0:T(1,128)S(1)}, u32[]{:S(2)}) copy-start(f32[1,1,192]{2,1,0:T(1,128)S(1)} %get-tuple-element.101) | copy-start | bytes 2308
  4.4 23.4 %copy-start.66 = (f32[1,1,192]{2,1,0:T(1,128)}, f32[1,1,192]{2,1,0:T(1,128)S(1)}, u32[]{:S(2)}) copy-start(f32[1,1,192]{2,1,0:T(1,128)S(1)} %get-tuple-element.102) | copy-start | bytes 2308
  4.4 23.4 %copy-start.68 = (f32[1,1,192]{2,1,0:T(1,128)}, f32[1,1,192]{2,1,0:T(1,128)S(1)}, u32[]{:S(2)}) copy-start(f32[1,1,192]{2,1,0:T(1,128)S(1)} %get-tuple-element.103) | copy-start | bytes 2308
  4.4 23.4 %copy-start.70 = (f32[1,1,192]{2,1,0:T(1,128)}, f32[1,1,192]{2,1,0:T(1,128)S(1)}, u32[]{:S(2)}) copy-start(f32[1,1,192]{2,1,0:T(1,128)S(1)} %get-tuple-element.104) | copy-start | bytes 2308
  4.4 23.4 %copy-start.72 = (f32[1,1,192]{2,1,0:T(1,128)}, f32[1,1,192]{2,1,0:T(1,128)S(1)}, u32[]{:S(2)}) copy-start(f32[1,1,192]{2,1,0:T(1,128)S(1)} %get-tuple-element.105) | copy-start | bytes 2308
  7.7 17.6 %collective-permute-start.2 = (bf16[3,134,192]{1,2,0:T(8,128)(2,1)S(1)}, bf16[3,134,192]{1,2,0:T(8,128)(2,1)S(1)}, u32[]{:S(2)}, u32[]{:S(2)}) collective-permute-start(bf16[3,134,192]{1,2,0:T(8,128)(2,1)S(1)} %get-tuple-element.33), channel_id=1, source_target_pairs={{0,2},{2,4},{4,6},{6,8},{8,10},{10,12},{12,14},{1,3},{3,5},{5,7},{... | collective-permute-start | bytes 463112 | tf_op jit(solution)/shard_map/ppermute | solution.py:18
  12.6 12.7 %collective-permute-start.3 = (bf16[3,134,192]{1,2,0:T(8,128)(2,1)S(1)}, bf16[3,134,192]{1,2,0:T(8,128)(2,1)S(1)}, u32[]{:S(2)}, u32[]{:S(2)}) collective-permute-start(bf16[3,134,192]{1,2,0:T(8,128)(2,1)S(1)} %get-tuple-element.34), channel_id=1, source_target_pairs={{2,0},{4,2},{6,4},{8,6},{10,8},{12,10},{14,12},{3,1},{5,3},{7,5},{... | collective-permute-start | bytes 463112 | tf_op jit(solution)/shard_map/ppermute | solution.py:19
  53.5 1.7 collective-permute-start.4
  54.0 1.7 collective-permute-start.5
  56.4 17.2 %collective-permute-start.6 = (bf16[3,134,192]{1,2,0:T(8,128)(2,1)S(1)}, bf16[3,134,192]{1,2,0:T(8,128)(2,1)S(1)}, u32[]{:S(2)}, u32[]{:S(2)}) collective-permute-start(bf16[3,134,192]{1,2,0:T(8,128)(2,1)S(1)} %get-tuple-element.29), channel_id=1, source_target_pairs={{0,2},{2,4},{4,6},{6,8},{8,10},{10,12},{12,14},{1,3},{3,5},{5,7},{... | collective-permute-start | bytes 463112 | tf_op jit(solution)/shard_map/ppermute | solution.py:18
  60.9 12.8 %collective-permute-start.7 = (bf16[3,134,192]{1,2,0:T(8,128)(2,1)S(1)}, bf16[3,134,192]{1,2,0:T(8,128)(2,1)S(1)}, u32[]{:S(2)}, u32[]{:S(2)}) collective-permute-start(bf16[3,134,192]{1,2,0:T(8,128)(2,1)S(1)} %get-tuple-element.30), channel_id=1, source_target_pairs={{2,0},{4,2},{6,4},{8,6},{10,8},{12,10},{14,12},{3,1},{5,3},{7,5},{... | collective-permute-start | bytes 463112 | tf_op jit(solution)/shard_map/ppermute | solution.py:19
  108.4 1.3 collective-permute-start.8
  108.8 1.4 collective-permute-start.9
  111.0 11.9 %collective-permute-start.10 = (bf16[3,134,192]{1,2,0:T(8,128)(2,1)S(1)}, bf16[3,134,192]{1,2,0:T(8,128)(2,1)S(1)}, u32[]{:S(2)}, u32[]{:S(2)}) collective-permute-start(bf16[3,134,192]{1,2,0:T(8,128)(2,1)S(1)} %get-tuple-element.25), channel_id=1, source_target_pairs={{2,0},{4,2},{6,4},{8,6},{10,8},{12,10},{14,12},{3,1},{5,3},{7,5},{... | collective-permute-start | bytes 463112 | tf_op jit(solution)/shard_map/ppermute | solution.py:19
  112.7 17.4 %collective-permute-start.11 = (bf16[3,134,192]{1,2,0:T(8,128)(2,1)S(1)}, bf16[3,134,192]{1,2,0:T(8,128)(2,1)S(1)}, u32[]{:S(2)}, u32[]{:S(2)}) collective-permute-start(bf16[3,134,192]{1,2,0:T(8,128)(2,1)S(1)} %get-tuple-element.26), channel_id=1, source_target_pairs={{0,2},{2,4},{4,6},{6,8},{8,10},{10,12},{12,14},{1,3},{3,5},{5,7},{... | collective-permute-start | bytes 463112 | tf_op jit(solution)/shard_map/ppermute | solution.py:18
  158.5 1.3 collective-permute-start.12
  158.9 1.4 collective-permute-start.13
  161.1 11.9 %collective-permute-start.14 = (bf16[3,134,192]{1,2,0:T(8,128)(2,1)S(1)}, bf16[3,134,192]{1,2,0:T(8,128)(2,1)S(1)}, u32[]{:S(2)}, u32[]{:S(2)}) collective-permute-start(bf16[3,134,192]{1,2,0:T(8,128)(2,1)S(1)} %get-tuple-element.21), channel_id=1, source_target_pairs={{2,0},{4,2},{6,4},{8,6},{10,8},{12,10},{14,12},{3,1},{5,3},{7,5},{... | collective-permute-start | bytes 463112 | tf_op jit(solution)/shard_map/ppermute | solution.py:19
  162.4 17.1 %collective-permute-start.15 = (bf16[3,134,192]{1,2,0:T(8,128)(2,1)S(1)}, bf16[3,134,192]{1,2,0:T(8,128)(2,1)S(1)}, u32[]{:S(2)}, u32[]{:S(2)}) collective-permute-start(bf16[3,134,192]{1,2,0:T(8,128)(2,1)S(1)} %get-tuple-element.22), channel_id=1, source_target_pairs={{0,2},{2,4},{4,6},{6,8},{8,10},{10,12},{12,14},{1,3},{3,5},{5,7},{... | collective-permute-start | bytes 463112 | tf_op jit(solution)/shard_map/ppermute | solution.py:18
  (139 other events, 2011.8 us)
where the time goes:
time: 239 us; the launch traced here: 238 us
  other arithmetic  91.1 us (38%)
  waiting for transfers between devices  42.6 us (18%)
  blocking collectives  32.1 us (13%)
  starting transfers between devices  27.8 us (12%)
  matrix products  24.1 us (10%)
  local copies, waits for them, and re-layouts  13.4 us (6%)
  between operations  7.26 us (3%)
    reduce_sum x2, other arithmetic, project(): jnp.mean(values, axis=-1, keepdims=True)  36.4 us
    ppermute x8, waiting for transfers between devices, extended(): before = lax.ppermute(last, axis, up)  33.8 us
    psum x1, blocking collectives, on_device(): lax.psum((start_local, forward_local, adjoint_local), ('lat', 'lon'))  32.1 us
    ppermute x8, starting transfers between devices, extended(): before = lax.ppermute(last, axis, up)  20.7 us
    reduce_sum x1, other arithmetic, on_device(): start_local = jnp.sum(area_w * perturb * perturb)  18.2 us
    add x1, other arithmetic, on_device(): grad_field = grad_field + conv_back  17.1 us
    dot_general x2, matrix products, on_device(): lax.dot_general(gated, w_in[layer_index], (((2,), (1,)), ((), ())), prefe...  12.2 us
    dot_general x2, matrix products, on_device(): jnp.dot(gated, w_out[layer_index], preferred_element_type=jnp.float32)  11.9 us
  transfers between devices with their start and end apart: 16, of which 10 were waited for; matrix products, arithmetic and copies ran while one was open for 4% of the time, Pallas kernels for 0%

commit v1 on v0

v1 whole, which is shorter than its diff:
```python
import functools
import math

import jax
import jax.numpy as jnp
import numpy as np
from jax import lax
from jax.experimental import pallas as pl
from jax.experimental.pallas import tpu as pltpu
from jax.sharding import PartitionSpec as P

F32 = jnp.float32
BF16 = jnp.bfloat16
LAT_SPAN = 70.0 * math.pi / 180.0
MARGIN = 8
EXT = 8
VMEM = pltpu.VMEM
IN_VMEM = pl.BlockSpec(memory_space=pltpu.VMEM)
IN_SMEM = pl.BlockSpec(memory_space=pltpu.SMEM)


def in_vmem(x):
    return pltpu.with_memory_space_constraint(x, pltpu.VMEM)


def tap_index(a, b, flipped):
    return (6 - a) * 7 + (6 - b) if flipped else a * 7 + b


def fill_taps(taps_ref, layer, low_scr, high_scr):
    for i in range(49):
        row = taps_ref[layer, i // 7, i % 7 : i % 7 + 1, :]
        low_scr[i] = jnp.broadcast_to(row[:, :128], (8, 128))
        high = jnp.broadcast_to(row[:, 128:], (8, row.shape[1] - 128))
        high_scr[i] = jnp.concatenate([high, high], axis=1)


def conv_local(load_row, lon_ref, taps_ref, layer, out_ref, xs0, xs1, k0, k1, flipped):
    rows, cols, _ = out_ref.shape
    half = rows // 2
    fill_taps(taps_ref, layer, k0, k1)
    zero = jnp.zeros((cols + 2 * MARGIN, 64), F32)

    @pl.loop(0, rows)
    def _(r):
        xs0[r, MARGIN : MARGIN + cols, :] = load_row(r)[:, :128]
        side = lon_ref[r].astype(F32)
        xs0[r, MARGIN - 3 : MARGIN, :] = side[0:3, :128]
        xs0[r, MARGIN + cols : MARGIN + cols + 3, :] = side[3:6, :128]

    def high_part(r):
        side = lon_ref[r].astype(F32)
        return load_row(r)[:, 128:], side[0:3, 128:], side[3:6, 128:]

    @pl.loop(0, half)
    def _(r):
        low, high = high_part(r), high_part(r + half)
        both = [jnp.concatenate([x, y], axis=1) for x, y in zip(low, high)]
        xs1[r + 3, MARGIN : MARGIN + cols, :] = both[0]
        xs1[r + 3, MARGIN - 3 : MARGIN, :] = both[1]
        xs1[r + 3, MARGIN + cols : MARGIN + cols + 3, :] = both[2]

    @pl.loop(0, 3)
    def _(q):
        mid, left, right = high_part(q + half - 3)
        xs1[q, MARGIN : MARGIN + cols, :] = jnp.concatenate([zero[:cols], mid], axis=1)
        xs1[q, MARGIN - 3 : MARGIN, :] = jnp.concatenate([zero[:3], left], axis=1)
        xs1[q, MARGIN + cols : MARGIN + cols + 3, :] = jnp.concatenate([zero[:3], right], axis=1)
        mid, left, right = high_part(q + half)
        p = q + half + 3
        xs1[p, MARGIN : MARGIN + cols, :] = jnp.concatenate([mid, zero[:cols]], axis=1)
        xs1[p, MARGIN - 3 : MARGIN, :] = jnp.concatenate([left, zero[:3]], axis=1)
        xs1[p, MARGIN + cols : MARGIN + cols + 3, :] = jnp.concatenate([right, zero[:3]], axis=1)

    @pl.loop(0, cols // 8)
    def _(j):
        base = pl.multiple_of(j * 8, 8)
        acc = [None] * rows
        for b in range(7):
            taps = [k0[tap_index(a, b, flipped)] for a in range(7)]
            for r in range(rows):
                x = xs0[r, pl.ds(base + (MARGIN - 3 + b), 8), :]
                for a in range(7):
                    o = r + 3 - a
                    if 0 <= o < rows:
                        term = taps[a] * x
                        acc[o] = term if acc[o] is None else acc[o] + term
        for o in range(rows):
            out_ref[o, pl.ds(base, 8), :128] = acc[o]
        acc = [None] * half
        for b in range(7):
            taps = [k1[tap_index(a, b, flipped)] for a in range(7)]
            for q in range(half + 6):
                x = xs1[q, pl.ds(base + (MARGIN - 3 + b), 8), :]
                for a in range(7):
                    o = q - a
                    if 0 <= o < half:
                        term = taps[a] * x
                        acc[o] = term if acc[o] is None else acc[o] + term
        for o in range(half):
            out_ref[o, pl.ds(base, 8), 128:] = acc[o][:, :64]
            out_ref[o + half, pl.ds(base, 8), 128:] = acc[o][:, 64:]


def conv_scratch(rows, cols):
    return [
        pltpu.VMEM((rows, cols + 2 * MARGIN, 128), F32),
        pltpu.VMEM((rows // 2 + 6, cols + 2 * MARGIN, 128), F32),
        pltpu.VMEM((49, 8, 128), F32),
        pltpu.VMEM((49, 8, 128), F32),
    ]


def conv_kernel(layer, flipped, f_ref, lon_ref, taps_ref, out_ref, *scratch):
    def load_row(r):
        return f_ref[r].astype(BF16).astype(F32)

    conv_local(load_row, lon_ref, taps_ref, layer, out_ref, *scratch, flipped)


def first_conv_kernel(
    area_ref, f_ref, lon_ref, taps_ref, inv_ref, turned_ref, out_ref, sum_ref, inv_out, normed_out, *scratch
):
    rows, cols, _ = f_ref.shape
    start = lax.axis_index("lat") * rows

    def load_row(r):
        return f_ref[r].astype(BF16).astype(F32)

    sum_ref[...] = jnp.zeros_like(sum_ref)

    @pl.loop(0, rows)
    def _(r):
        x = f_ref[r]
        sum_ref[...] += area_ref[0, start + r] * jnp.sum(x * x, axis=0, keepdims=True)

    for layer in range(inv_ref.shape[0]):
        turned = jnp.transpose(inv_ref[layer])
        for r in range(rows):
            inv_out[layer, r] = jnp.broadcast_to(turned[:, r : r + 1], (cols, 128))

        @pl.loop(0, rows)
        def _(r):
            normed_out[layer, r] = jnp.transpose(turned_ref[layer, r].astype(F32)).astype(BF16)

    conv_local(load_row, lon_ref, taps_ref, 0, out_ref, *scratch, False)


def place_halo(parity, a_ref, b_ref, hx):
    cols = a_ref.shape[1] - EXT
    for ref, first in ((a_ref, (1 - parity) * 3), (b_ref, parity * 3)):
        for e in range(3):
            row = ref[e].astype(F32)
            for lanes, plane in ((slice(0, 128), 0), (slice(128, 192), 1)):
                part = row[:, lanes]
                width = part.shape[1]
                hx[plane, first + e, MARGIN : MARGIN + cols, :width] = part[:cols]
                hx[plane, first + e, MARGIN - 3 : MARGIN, :width] = part[cols : cols + 3]
                hx[plane, first + e, MARGIN + cols : MARGIN + cols + 3, :width] = part[cols + 3 : cols + 6]


def conv_halo(hx, acc_ref, taps_ref, layer, edge, k0, k1, flipped):
    rows, cols, _ = acc_ref.shape
    fill_taps(taps_ref, layer, k0, k1)

    @pl.loop(0, cols // 8)
    def _(j):
        base = pl.multiple_of(j * 8, 8)
        for plane, taps_scr, lanes in ((0, k0, slice(0, 128)), (1, k1, slice(128, 192))):
            acc = [None] * 6
            for b in range(7):
                for e in range(3):
                    upper = hx[plane, e, pl.ds(base + (MARGIN - 3 + b), 8), :]
                    for o in range(e + 1):
                        term = taps_scr[tap_index(e - o, b, flipped)] * upper
                        acc[o] = term if acc[o] is None else acc[o] + term
                    lower = hx[plane, 3 + e, pl.ds(base + (MARGIN - 3 + b), 8), :]
                    for p in range(e, 3):
                        term = taps_scr[tap_index(6 + e - p, b, flipped)] * lower
                        acc[3 + p] = term if acc[3 + p] is None else acc[3 + p] + term
            for o in range(6):
                own = o if o < 3 else rows - 6 + o
                width = lanes.stop - lanes.start
                edge[o, pl.ds(base, 8), lanes] = acc_ref[own, pl.ds(base, 8), lanes] + acc[o][:, :width]


def halo_scratch(cols, chans):
    return [
        pltpu.VMEM((2, 6, cols + 2 * MARGIN, 128), F32),
        pltpu.VMEM((6, cols, chans), F32),
        pltpu.VMEM((49, 8, 128), F32),
        pltpu.VMEM((49, 8, 128), F32),
    ]


def wide(inv, chans):
    return jnp.concatenate([inv, inv[:, : chans - 128]], axis=1)


def project(y, normed, inv):
    chans = y.shape[1]
    normal = normed.astype(F32)
    first = jnp.sum(y, axis=1, keepdims=True) * (1.0 / chans)
    second = jnp.sum(normal * y, axis=1, keepdims=True) * (1.0 / chans)
    return wide(inv, chans) * (y - first - normal * second)


ACROSS = (((1,), (1,)), ((), ()))


def forward_net(y, normed, inv, slope, gain, w_in, w_out_turned, scale):
    operand = (gain * project(y, normed, inv)).astype(BF16)
    hidden = jnp.dot(operand, w_in, preferred_element_type=F32)
    gated = (slope.astype(F32) * hidden).astype(BF16)
    return scale * lax.dot_general(gated, w_out_turned, ACROSS, preferred_element_type=F32)


def adjoint_net(g, normed, inv, slope, gain, w_in, w_out_turned, scale):
    scaled = (scale * g).astype(BF16)
    hidden = jnp.dot(scaled, w_out_turned, preferred_element_type=F32)
    gated = (slope.astype(F32) * hidden).astype(BF16)
    back = lax.dot_general(gated, w_in, ACROSS, preferred_element_type=F32)
    return project(gain * back, normed, inv).astype(BF16)


def send_rows(parity, field, lon_ref, a_ref, b_ref):
    rows, cols = lon_ref.shape[0], a_ref.shape[1] - EXT
    for e in range(3):
        top, bottom = field(e), field(rows - 3 + e)
        a_ref[e, :cols, :] = jnp.where(parity == 1, top.astype(F32), bottom.astype(F32)).astype(BF16)
        b_ref[e, :cols, :] = jnp.where(parity == 1, bottom.astype(F32), top.astype(F32)).astype(BF16)
    pad = jnp.zeros((2, lon_ref.shape[2]), BF16)

    @pl.loop(0, rows)
    def _(r):
        row = field(r)
        lon_ref[r] = jnp.concatenate([row[cols - 3 :], row[:3], pad], axis=0)


def flat(x):
    return x.reshape(x.shape[0] * x.shape[1], x.shape[2])


def each_block(rows, fn):
    fn(0, 3, 0)
    fn(rows - 3, 3, 3)

    @pl.loop(0, (rows - 6) // 2)
    def _(i):
        fn(3 + 2 * i, 2, None)


def sums_of(acc_ref, edge, first, count, slot):
    return flat(acc_ref[pl.ds(first, count)]) if slot is None else flat(edge[slot : slot + count])


def net_operands(layer, first, count, refs):
    normed_ref, inv_ref, slope_ref, gain_ref, win_ref, wout_ref, scale_ref = refs
    per_cell = [flat(ref[layer, pl.ds(first, count)]) for ref in (normed_ref, inv_ref, slope_ref)]
    return per_cell + [
        gain_ref[layer : layer + 1, :], win_ref[layer], wout_ref[layer], scale_ref[layer : layer + 1, :]
    ]


def tangent_kernel(layer, last, area_ref, acc_ref, a_ref, b_ref, taps_ref, t_ref, *rest):
    net, rest = rest[:7], rest[7:]
    rows, cols, chans = acc_ref.shape
    lat = lax.axis_index("lat")
    parity = lat % 2
    if last:
        g_ref, db_ref, sum_ref, lon_ref, sa_ref, sb_ref, hx, edge, k0, k1 = rest
        sum_ref[...] = jnp.zeros_like(sum_ref)
    else:
        t_out, lon_ref, sa_ref, sb_ref, hx, edge, k0, k1 = rest
    place_halo(parity, a_ref, b_ref, hx)
    conv_halo(hx, acc_ref, taps_ref, layer, edge, k0, k1, False)

    def block(first, count, slot):
        y = sums_of(acc_ref, edge, first, count, slot)
        operands = net_operands(layer, first, count, net)
        t = flat(t_ref[pl.ds(first, count)]) + forward_net(y, *operands)
        if not last:
            t_out[pl.ds(first, count)] = t.reshape(count, cols, chans)
            return
        parts = []
        for i in range(count):
            u = t[i * cols : (i + 1) * cols]
            g = area_ref[0, lat * rows + first + i] * u
            sum_ref[...] += jnp.sum(g * u, axis=0, keepdims=True)
            parts.append(g)
        g = jnp.concatenate(parts, axis=0)
        g_ref[pl.ds(first, count)] = g.reshape(count, cols, chans)
        db_ref[pl.ds(first, count)] = adjoint_net(g, *operands).reshape(count, cols, chans)

    each_block(rows, block)
    send_rows(parity, (lambda r: db_ref[r]) if last else (lambda r: t_out[r].astype(BF16)), lon_ref, sa_ref, sb_ref)


def adjoint_kernel(layer, acc_ref, a_ref, b_ref, taps_ref, g_ref, *rest):
    net, (g_out, db_ref, lon_ref, sa_ref, sb_ref, hx, edge, k0, k1) = rest[:7], rest[7:]
    rows, cols, chans = acc_ref.shape
    parity = lax.axis_index("lat") % 2
    place_halo(parity, a_ref, b_ref, hx)
    conv_halo(hx, acc_ref, taps_ref, layer + 1, edge, k0, k1, True)

    def block(first, count, slot):
        g = flat(g_ref[pl.ds(first, count)]) + sums_of(acc_ref, edge, first, count, slot)
        g_out[pl.ds(first, count)] = g.reshape(count, cols, chans)
        db = adjoint_net(g, *net_operands(layer, first, count, net))
        db_ref[pl.ds(first, count)] = db.reshape(count, cols, chans)

    each_block(rows, block)
    send_rows(parity, lambda r: db_ref[r], lon_ref, sa_ref, sb_ref)


def final_kernel(
    area_ref, acc_ref, a_ref, b_ref, taps_ref, g_ref, vv_ref, uu_ref, w_ref, tile_ref, hx, edge, k0, k1, ww
):
    rows = acc_ref.shape[0]
    lat = lax.axis_index("lat")
    place_halo(lat % 2, a_ref, b_ref, hx)
    conv_halo(hx, acc_ref, taps_ref, 0, edge, k0, k1, True)
    ww[...] = jnp.zeros_like(ww)

    def row(r, y):
        g = g_ref[r] + y
        w = g * area_ref[1, lat * rows + r]
        w_ref[r] = jnp.transpose(w)
        ww[...] += jnp.sum(g * w, axis=0, keepdims=True)

    for e in range(3):
        row(e, edge[e])
        row(rows - 3 + e, edge[3 + e])

    @pl.loop(3, rows - 3)
    def _(r):
        row(r, acc_ref[r])

    which = lax.broadcasted_iota(jnp.int32, (8, 128), 0)
    vv, uu, wv = (jnp.sum(ref[...]) for ref in (vv_ref, uu_ref, ww))
    tile = jnp.where(which == 0, vv, jnp.where(which == 1, uu, jnp.where(which == 2, wv, 0.0)))
    for i in range(tile_ref.shape[0]):
        tile_ref[i] = tile


def scale_kernel(total, tile_ref, w_ref, out_ref, growth_ref):
    sums = jnp.sum(tile_ref[...], axis=0) * (1.0 / total)
    vv, uu, ww = sums[0:1, :], sums[1:2, :], sums[2:3, :]
    growth_ref[...] = jnp.sqrt(uu / (vv + 1e-06))
    factor = 1.0 / jnp.sqrt(ww + 1e-06)
    i = pl.program_id(0)
    count = out_ref.shape[0]
    for r in range(count):
        out_ref[r] = w_ref[i * count + r] * factor


def extend_kernel(lon_ref, sa_in, sb_in, sa_ref, sb_ref):
    rows, cols = lon_ref.shape[0], sa_ref.shape[1] - EXT
    parity = lax.axis_index("lat") % 2
    for e in range(3):
        sa_ref[e, :cols, :] = sa_in[e, :cols, :]
        sb_ref[e, :cols, :] = sb_in[e, :cols, :]
        sa_ref[e, cols:, :] = lon_ref[(1 - parity) * (rows - 3) + e]
        sb_ref[e, cols:, :] = lon_ref[parity * (rows - 3) + e]


def edges_kernel(turned_ref, t_ref, lon_ref, sa_ref, sb_ref):
    rows = turned_ref.shape[0]

    @pl.loop(0, rows)
    def _(r):
        t_ref[r] = jnp.transpose(turned_ref[r])

    send_rows(lax.axis_index("lat") % 2, lambda r: t_ref[r].astype(BF16), lon_ref, sa_ref, sb_ref)


def params():
    return pltpu.CompilerParams(vmem_limit_bytes=16 * 1024 * 1024)


def on_device(lat_size, lon_size, perturb, kernels, gains, w_in, w_out, scales, normed, inv_std, slope):
    rows, cols, chans = perturb.shape
    hidden = w_in.shape[2]
    layers = kernels.shape[0]
    lat_total = rows * lat_size
    angles = LAT_SPAN * (np.arange(lat_total) + 0.5) / lat_total
    total = float(np.sum(np.cos(angles))) * cols * lon_size * chans
    table = np.stack([np.cos(angles), 1.0 / np.cos(angles)]).astype(np.float32)
    area = jnp.asarray(table)
    across_cells = jnp.transpose(w_out, (0, 2, 1))
    swap_a = [(i, i ^ 1) for i in range(lat_size) if i ^ 1 < lat_size]
    swap_b = [pair for i in range(1, lat_size - 1, 2) for pair in ((i, i + 1), (i + 1, i))]
    swap_lon = [(i, (i + 1) % lon_size) for i in range(lon_size)]

    lon_shape = VMEM((rows, EXT, chans), BF16)
    send_shape = VMEM((3, cols + EXT, chans), BF16)
    full32 = VMEM((rows, cols, chans), F32)
    full16 = VMEM((rows, cols, chans), BF16)
    sums = VMEM((1, chans), F32)

    def call(kernel, out_shape, in_specs, args, scratch=(), flops=0, name=None):
        args = [in_vmem(x) if spec is IN_VMEM else x for spec, x in zip(in_specs, args)]
        return pl.pallas_call(
            kernel,
            out_shape=out_shape,
            in_specs=in_specs,
            out_specs=[IN_VMEM] * len(out_shape),
            scratch_shapes=list(scratch),
            compiler_params=params(),
            cost_estimate=pl.CostEstimate(flops=flops, bytes_accessed=4_000_000, transcendentals=0),
            name=name,
        )(*args)

    def exchange(lon, send_a, send_b):
        side = lax.ppermute(lon, "lon", swap_lon)
        send_a, send_b = call(
            extend_kernel, [send_shape] * 2, [IN_VMEM] * 3, (side, send_a, send_b), name="extend"
        )
        halo_b = lax.ppermute(send_b, "lat", swap_b)
        halo_a = lax.ppermute(send_a, "lat", swap_a)
        return side, halo_a, halo_b

    conv_flops = 2 * 49 * rows * cols * chans
    net_flops = 4 * rows * cols * chans * hidden
    kscr = conv_scratch(rows, cols)
    hscr = halo_scratch(cols, chans)

    tangent, lon, send_a, send_b = call(
        edges_kernel, [full32, lon_shape, send_shape, send_shape], [IN_VMEM], (jnp.transpose(perturb, (0, 2, 1)),),
        name="edges",
    )
    side, halo_a, halo_b = exchange(lon, send_a, send_b)
    acc, vv, inv_wide, normed_cells = call(
        first_conv_kernel,
        [full32, sums, VMEM((layers, rows, cols, 128), F32), VMEM((layers, rows, cols, chans), BF16)],
        [IN_SMEM] + [IN_VMEM] * 5,
        (area, tangent, side, kernels, inv_std, jnp.transpose(normed, (0, 1, 3, 2))), kscr, conv_flops, "conv_first",
    )
    net = (normed_cells, inv_wide, slope, gains, w_in, across_cells, scales)
    for layer in range(layers):
        last = layer == layers - 1
        outs = [full32, full16, sums] if last else [full32]
        outs = outs + [lon_shape, send_shape, send_shape]
        got = call(
            functools.partial(tangent_kernel, layer, last), outs, [IN_SMEM] + [IN_VMEM] * 12,
            (area, acc, halo_a, halo_b, kernels, tangent) + net, hscr, net_flops, f"tangent{layer}",
        )
        side, halo_a, halo_b = exchange(*got[-3:])
        if last:
            grad, back, uu = got[:3]
        else:
            tangent = got[0]
            (acc,) = call(
                functools.partial(conv_kernel, layer + 1, False), [full32], [IN_VMEM] * 3, (tangent, side, kernels),
                kscr, conv_flops, f"conv{layer + 1}",
            )
    for layer in range(layers - 1, -1, -1):
        (acc,) = call(
            functools.partial(conv_kernel, layer, True), [full32], [IN_VMEM] * 3, (back, side, kernels),
            kscr, conv_flops, f"convt{layer}",
        )
        if layer > 0:
            grad, back, lon, send_a, send_b = call(
                functools.partial(adjoint_kernel, layer - 1), [full32, full16, lon_shape, send_shape, send_shape],
                [IN_VMEM] * 12, (acc, halo_a, halo_b, kernels, grad) + net, hscr, net_flops, f"adjoint{layer - 1}",
            )
            side, halo_a, halo_b = exchange(lon, send_a, send_b)
    members = lat_size * lon_size
    w, tile = call(
        final_kernel, [VMEM((rows, chans, cols), F32), VMEM((members, 8, 128), F32)], [IN_SMEM] + [IN_VMEM] * 7,
        (area, acc, halo_a, halo_b, kernels, grad, vv, uu), hscr + [pltpu.VMEM((1, chans), F32)], 0, "final",
    )
    tile = lax.all_to_all(tile, ("lat", "lon"), 0, 0, tiled=True)
    steps = 4
    new_vec, growth = pl.pallas_call(
        functools.partial(scale_kernel, total),
        grid=(steps,),
        out_shape=[jax.ShapeDtypeStruct((rows, chans, cols), F32), jax.ShapeDtypeStruct((1, 128), F32)],
        in_specs=[IN_VMEM, IN_VMEM],
        out_specs=[
            pl.BlockSpec((rows // steps, chans, cols), lambda i: (i, 0, 0)),
            pl.BlockSpec((1, 128), lambda i: (0, 0)),
        ],
        compiler_params=params(),
        name="scale",
    )(in_vmem(tile), in_vmem(w))
    return jnp.transpose(new_vec, (0, 2, 1)), growth[0, :1]


def solution(mesh):
    in_specs = (
        P(("grp", "lat"), "lon", None),
        P(),
        P(),
        P(),
        P(),
        P(),
        P(None, ("grp", "lat"), "lon", None),
        P(None, ("grp", "lat"), "lon"),
        P(None, ("grp", "lat"), "lon", None),
    )
    out_specs = (P(("grp", "lat"), "lon", None), P("grp"))
    fn = functools.partial(on_device, mesh.shape["lat"], mesh.shape["lon"])
    return jax.shard_map(fn, mesh=mesh, in_specs=in_specs, out_specs=out_specs, check_vma=False)
```

time: 239 us -> 103 us (0.43)
  other arithmetic: 91.1 us -> 0 us
  Pallas kernels: 0 us -> 60.4 us
  waiting for transfers between devices: 42.6 us -> 8.55 us
  matrix products: 24.1 us -> 0 us
  blocking collectives: 32.1 us -> 11.5 us
  starting transfers between devices: 27.8 us -> 16.8 us
  local copies, waits for them, and re-layouts: 13.4 us -> 4.25 us
  between operations: 7.26 us -> 0.92 us
    pallas_call x0 -> x14, Pallas kernels: none -> 60.4 us  [the longest x13 58.6 us: call(): pl.pallas_call(kernel, out_shape=out_shape, in_specs=in_specs, out_specs=...]
    reduce_sum x4 -> x0, other arithmetic: 55.2 us -> none  [the longest x2 36.4 us: project(): jnp.mean(values, axis=-1, keepdims=True)]
    ppermute x16 -> x12, waiting for transfers between devices: 42.6 us -> 8.55 us  [the longest x4 4.63 us: exchange(): side = lax.ppermute(lon, 'lon', swap_lon)]
    psum x1 -> x0, blocking collectives: 32.1 us -> none  [on_device(): lax.psum((start_local, forward_local, adjoint_local), ('lat', 'lon'))]
    dot_general x4 -> x0, matrix products: 24.1 us -> none  [the longest x2 12.2 us: on_device(): lax.dot_general(gated, w_in[layer_index], (((2,), (1,)), ((), ())), prefe...]
    add x1 -> x0, other arithmetic: 17.1 us -> none  [on_device(): grad_field = grad_field + conv_back]
    all_to_all x0 -> x1, blocking collectives: none -> 11.5 us  [on_device(): tile = lax.all_to_all(tile, ('lat', 'lon'), 0, 0, tiled=True)]
    ppermute x16 -> x12, starting transfers between devices: 27.8 us -> 16.8 us  [the longest x4 13.4 us: exchange(): halo_a = lax.ppermute(send_a, 'lat', swap_a)]
  transfers between devices with their start and end apart: 16 -> 12, of which waited for: 10 -> 7; matrix products, arithmetic and copies ran while one was open for 4% -> 0% of each run, Pallas kernels for 0% -> 33%
where the time goes in v1:
time: 103 us; the launch traced here: 102 us
  Pallas kernels  60.4 us (59%)
  starting transfers between devices  16.8 us (16%)
  blocking collectives  11.5 us (11%)
  waiting for transfers between devices  8.55 us (8%)
  local copies, waits for them, and re-layouts  4.25 us (4%)
    pallas_call x13, Pallas kernels, call(): pl.pallas_call(kernel, out_shape=out_shape, in_specs=in_specs, out_specs=...  58.6 us
    ppermute x4, starting transfers between devices, exchange(): halo_a = lax.ppermute(send_a, 'lat', swap_a)  13.4 us
    all_to_all x1, blocking collectives, on_device(): tile = lax.all_to_all(tile, ('lat', 'lon'), 0, 0, tiled=True)  11.5 us
    ppermute x4, waiting for transfers between devices, exchange(): side = lax.ppermute(lon, 'lon', swap_lon)  4.63 us
    unnamed x23, local copies, waits for them, and re-layouts  4.25 us
    ppermute x4, waiting for transfers between devices, exchange(): halo_a = lax.ppermute(send_a, 'lat', swap_a)  3.92 us
    ppermute x4, starting transfers between devices, exchange(): halo_b = lax.ppermute(send_b, 'lat', swap_b)  2.65 us
  transfers between devices with their start and end apart: 12, of which 7 were waited for; matrix products, arithmetic and copies ran while one was open for 0% of the time, Pallas kernels for 33%

profile of v1, /device:TPU:0, one launch (start us, length us, event | category | flops | bytes accessed | tf_op | source)
XLA Modules:
  0.0 102.4 jit_solution(3084643534864604374)
XLA Ops:
  0.6 0.0 copy-start.9
  0.6 0.0 copy-start.4
  0.7 1.4 %copy-done.4 = f32[16,128,192]{1,2,0:T(8,128)S(1)} copy-done((f32[16,128,192]{1,2,0:T(8,128)S(1)}, f32[16,128,192]{1,2,0:T(8,128)}, u32[]{:S(2)}) %copy-start.4) | copy-done | bytes 1572888
  2.1 1.8 %edges.1 = (f32[16,128,192]{2,1,0:T(8,128)S(1)}, bf16[16,8,192]{2,1,0:T(8,128)(2,1)S(1)}, bf16[3,136,192]{2,1,0:T(8,128)(2,1)S(1)}, bf16[3,136,192]{2,1,0:T(8,128)(2,1)S(1)}) custom-call(f32[16,192,128]{2,1,0:T(8,128)S(1)} %bitcast.9), custom_call_target="tpu_custom_call" | custom-call | bytes 4000000 | tf_op jit(solution)/shard_map/edges/pallas_call | solution.py:403
  3.9 0.5 collective-permute-start
  4.4 0.9 collective-permute-done.lon_ref
  5.4 0.0 copy-start.2
  5.4 0.0 copy-start.3
  5.4 0.0 copy-start.6
  5.4 0.0 copy-start.7
  5.4 2.9 %collective-permute-start.1 = (bf16[3,136,192]{2,1,0:T(8,128)(2,1)S(1)}, bf16[3,136,192]{2,1,0:T(8,128)(2,1)S(1)}, u32[]{:S(2)}, u32[]{:S(2)}) collective-permute-start(bf16[3,136,192]{2,1,0:T(8,128)(2,1)S(1)} %get-tuple-element.42), channel_id=1, source_target_pairs={{0,2},{2,0},{4,6},{6,4},{8,10},{10,8},{12,14},{14,12},{1,3},{3,1},... | collective-permute-start | bytes 470024 | tf_op jit(solution)/shard_map/ppermute | solution.py:420
  8.3 0.7 collective-permute-start.2
  9.0 0.0 copy-done.9
  9.0 0.0 copy-done.5
  9.1 0.0 copy-done.8
  9.1 12.5 %conv_first.1 = (f32[16,128,192]{2,1,0:T(8,128)S(1)}, f32[1,192]{1,0:T(1,128)S(1)}, f32[2,16,128,128]{3,2,1,0:T(8,128)S(1)}, bf16[2,16,128,192]{3,2,1,0:T(8,128)(2,1)S(1)}) custom-call(f32[2,128]{1,0:T(2,128)S(1)} %copy-done.9, f32[16,128,192]{2,1,0:T(8,128)S(1)} %get-tuple-element.37.f_ref.t_ref, bf16[16,8,192]{2,1,0:T(8,128)(2,1)S(1)} %collective-permute-done.lon_ref, ...), custom_call_target="tpu_custom_call" | custom-call | flops 38535168 | bytes 4000000 | tf_op jit(solution)/shard_map/conv_first/pallas_call | solution.py:403
  21.6 0.0 collective-permute-done.1.a_ref
  21.6 0.0 collective-permute-done.2.b_ref
  21.6 0.0 copy-done.2
  21.6 0.0 copy-start
  21.7 2.8 %copy-done = bf16[2,16,128,768]{3,2,1,0:T(8,128)(2,1)S(1)} copy-done((bf16[2,16,128,768]{3,2,1,0:T(8,128)(2,1)S(1)}, bf16[2,16,128,768]{3,2,1,0:T(8,128)(2,1)}, u32[]{:S(2)}) %copy-start) | copy-done | bytes 6291480
  24.4 5.5 %tangent0.1 = (f32[16,128,192]{2,1,0:T(8,128)S(1)}, bf16[16,8,192]{2,1,0:T(8,128)(2,1)S(1)}, bf16[3,136,192]{2,1,0:T(8,128)(2,1)S(1)}, bf16[3,136,192]{2,1,0:T(8,128)(2,1)S(1)}) custom-call(f32[2,128]{1,0:T(2,128)S(1)} %copy-done.9, f32[16,128,192]{2,1,0:T(8,128)S(1)} %get-tuple-element.39.acc_ref, bf16[3,136,192]{2,1,0:T(8,128)(2,1)S(1)} %collective-permute-done.1.a_ref, ...), custom_call_target="tpu_custom_call" | custom-call | flops 1207959552 | bytes 4000000 | tf_op jit(solution)/shard_map/tangent0/pallas_call | solution.py:403
  29.9 0.1 collective-permute-start.3
  30.0 1.2 %collective-permute-done.3.lon_ref = bf16[16,8,192]{2,1,0:T(8,128)(2,1)S(1)} collective-permute-done((bf16[16,8,192]{2,1,0:T(8,128)(2,1)S(1)}, bf16[16,8,192]{2,1,0:T(8,128)(2,1)S(1)}, u32[]{:S(2)}, u32[]{:S(2)}) %collective-permute-start.3) | collective-permute-done | bytes 49184 | tf_op jit(solution)/shard_map/ppermute | solution.py:415
  31.3 4.3 %collective-permute-start.4 = (bf16[3,136,192]{2,1,0:T(8,128)(2,1)S(1)}, bf16[3,136,192]{2,1,0:T(8,128)(2,1)S(1)}, u32[]{:S(2)}, u32[]{:S(2)}) collective-permute-start(bf16[3,136,192]{2,1,0:T(8,128)(2,1)S(1)} %get-tuple-element.50), channel_id=1, source_target_pairs={{0,2},{2,0},{4,6},{6,4},{8,10},{10,8},{12,14},{14,12},{1,3},{3,1},... | collective-permute-start | bytes 470024 | tf_op jit(solution)/shard_map/ppermute | solution.py:420
  35.6 0.7 collective-permute-start.5
  36.3 7.3 %conv1.1.acc_ref = f32[16,128,192]{2,1,0:T(8,128)S(1)} custom-call(f32[16,128,192]{2,1,0:T(8,128)S(1)} %get-tuple-element.46.f_ref.t_ref, bf16[16,8,192]{2,1,0:T(8,128)(2,1)S(1)} %collective-permute-done.3.lon_ref, f32[2,7,7,192]{3,2,1,0:T(8,128)S(1)} %copy.12.taps_ref), custom_call_target="tpu_custom_call" | custom-call | flops 38535168 | bytes 4000000 | tf_op jit(solution)/shard_map/conv1/pallas_call | solution.py:403
  43.6 1.3 %collective-permute-done.4.a_ref = bf16[3,136,192]{2,1,0:T(8,128)(2,1)S(1)} collective-permute-done((bf16[3,136,192]{2,1,0:T(8,128)(2,1)S(1)}, bf16[3,136,192]{2,1,0:T(8,128)(2,1)S(1)}, u32[]{:S(2)}, u32[]{:S(2)}) %collective-permute-start.4) | collective-permute-done | bytes 156704 | tf_op jit(solution)/shard_map/ppermute | solution.py:420
  44.8 0.0 collective-permute-done.5.b_ref
  44.8 8.7 %tangent1.1 = (f32[16,128,192]{2,1,0:T(8,128)S(1)}, bf16[16,128,192]{2,1,0:T(8,128)(2,1)S(1)}, f32[1,192]{1,0:T(1,128)S(1)}, bf16[16,8,192]{2,1,0:T(8,128)(2,1)S...) custom-call(f32[2,128]{1,0:T(2,128)S(1)} %copy-done.9, f32[16,128,192]{2,1,0:T(8,128)S(1)} %conv1.1.acc_ref, ...), custom_call_target="tpu_custom_call" | custom-call | flops 1207959552 | bytes 4000000 | tf_op jit(solution)/shard_map/tangent1/pallas_call | solution.py:403
  53.6 0.1 collective-permute-start.6
  53.6 1.2 %collective-permute-done.6.lon_ref = bf16[16,8,192]{2,1,0:T(8,128)(2,1)S(1)} collective-permute-done((bf16[16,8,192]{2,1,0:T(8,128)(2,1)S(1)}, bf16[16,8,192]{2,1,0:T(8,128)(2,1)S(1)}, u32[]{:S(2)}, u32[]{:S(2)}) %collective-permute-start.6) | collective-permute-done | bytes 49184 | tf_op jit(solution)/shard_map/ppermute | solution.py:415
  54.9 3.1 %collective-permute-start.7 = (bf16[3,136,192]{2,1,0:T(8,128)(2,1)S(1)}, bf16[3,136,192]{2,1,0:T(8,128)(2,1)S(1)}, u32[]{:S(2)}, u32[]{:S(2)}) collective-permute-start(bf16[3,136,192]{2,1,0:T(8,128)(2,1)S(1)} %get-tuple-element.56), channel_id=1, source_target_pairs={{0,2},{2,0},{4,6},{6,4},{8,10},{10,8},{12,14},{14,12},{1,3},{3,1},... | collective-permute-start | bytes 470024 | tf_op jit(solution)/shard_map/ppermute | solution.py:420
  58.0 0.7 collective-permute-start.8
  58.7 7.2 %convt1.1.acc_ref = f32[16,128,192]{2,1,0:T(8,128)S(1)} custom-call(bf16[16,128,192]{2,1,0:T(8,128)(2,1)S(1)} %get-tuple-element.52.f_ref, bf16[16,8,192]{2,1,0:T(8,128)(2,1)S(1)} %collective-permute-done.6.lon_ref, f32[2,7,7,192]{3,2,1,0:T(8,128)S(1)} %copy.12.taps_ref), custom_call_target="tpu_custom_call" | custom-call | flops 38535168 | bytes 4000000 | tf_op jit(solution)/shard_map/convt1/pallas_call | solution.py:403
  65.9 1.3 %collective-permute-done.7.a_ref = bf16[3,136,192]{2,1,0:T(8,128)(2,1)S(1)} collective-permute-done((bf16[3,136,192]{2,1,0:T(8,128)(2,1)S(1)}, bf16[3,136,192]{2,1,0:T(8,128)(2,1)S(1)}, u32[]{:S(2)}, u32[]{:S(2)}) %collective-permute-start.7) | collective-permute-done | bytes 156704 | tf_op jit(solution)/shard_map/ppermute | solution.py:420
  67.2 0.0 collective-permute-done.8.b_ref
  67.2 5.0 %adjoint0.1 = (f32[16,128,192]{2,1,0:T(8,128)S(1)}, bf16[16,128,192]{2,1,0:T(8,128)(2,1)S(1)}, bf16[16,8,192]{2,1,0:T(8,128)(2,1)S(1)}, bf16[3,136,192]{2,1,0:T(8,128)(2,1)S(1)}, bf16[3,136,192]{2,1,0:T(8,128)(2,1)S(1)}) custom-call(f32[16,128,192]{2,1,0:T(8,128)S(1)} %convt1.1.acc_ref, bf16[3,136,192]{2,1,0:T(8,128)(2,1)S(1)} %collective-permute-done.7.a_ref, ...), custom_call_target="tpu_custom_call" | custom-call | flops 1207959552 | bytes 4000000 | tf_op jit(solution)/shard_map/adjoint0/pallas_call | solution.py:403
  72.3 0.1 collective-permute-start.9
  72.4 1.2 %collective-permute-done.9.lon_ref = bf16[16,8,192]{2,1,0:T(8,128)(2,1)S(1)} collective-permute-done((bf16[16,8,192]{2,1,0:T(8,128)(2,1)S(1)}, bf16[16,8,192]{2,1,0:T(8,128)(2,1)S(1)}, u32[]{:S(2)}, u32[]{:S(2)}) %collective-permute-start.9) | collective-permute-done | bytes 49184 | tf_op jit(solution)/shard_map/ppermute | solution.py:415
  73.6 3.0 %collective-permute-start.10 = (bf16[3,136,192]{2,1,0:T(8,128)(2,1)S(1)}, bf16[3,136,192]{2,1,0:T(8,128)(2,1)S(1)}, u32[]{:S(2)}, u32[]{:S(2)}) collective-permute-start(bf16[3,136,192]{2,1,0:T(8,128)(2,1)S(1)} %get-tuple-element.63), channel_id=1, source_target_pairs={{0,2},{2,0},{4,6},{6,4},{8,10},{10,8},{12,14},{14,12},{1,3},{3,1},... | collective-permute-start | bytes 470024 | tf_op jit(solution)/shard_map/ppermute | solution.py:420
  76.7 0.7 collective-permute-start.11
  77.3 7.2 %convt0.1.acc_ref = f32[16,128,192]{2,1,0:T(8,128)S(1)} custom-call(bf16[16,128,192]{2,1,0:T(8,128)(2,1)S(1)} %get-tuple-element.59.f_ref, bf16[16,8,192]{2,1,0:T(8,128)(2,1)S(1)} %collective-permute-done.9.lon_ref, f32[2,7,7,192]{3,2,1,0:T(8,128)S(1)} %copy.12.taps_ref), custom_call_target="tpu_custom_call" | custom-call | flops 38535168 | bytes 4000000 | tf_op jit(solution)/shard_map/convt0/pallas_call | solution.py:403
  84.6 1.3 %collective-permute-done.10.a_ref = bf16[3,136,192]{2,1,0:T(8,128)(2,1)S(1)} collective-permute-done((bf16[3,136,192]{2,1,0:T(8,128)(2,1)S(1)}, bf16[3,136,192]{2,1,0:T(8,128)(2,1)S(1)}, u32[]{:S(2)}, u32[]{:S(2)}) %collective-permute-start.10) | collective-permute-done | bytes 156704 | tf_op jit(solution)/shard_map/ppermute | solution.py:420
  85.9 0.0 collective-permute-done.11.b_ref
  85.9 3.2 %final.1 = (f32[16,192,128]{2,1,0:T(8,128)S(1)}, f32[16,8,128]{2,1,0:T(8,128)S(1)}) custom-call(f32[2,128]{1,0:T(2,128)S(1)} %copy-done.9, f32[16,128,192]{2,1,0:T(8,128)S(1)} %convt0.1.acc_ref, bf16[3,136,192]{2,1,0:T(8,128)(2,1)S(1)} %collective-permute-done.10.a_ref, bf16[3,136,192]{2,1,0:T(8,128)(2,1)S(1)} %collective-permute-done.11.b_ref, ...), custom_call_target="tpu_custom_call" | custom-call | bytes 4000000 | tf_op jit(solution)/shard_map/final/pallas_call | solution.py:403
  89.1 11.5 %all_to_all.5.tile_ref = f32[16,8,128]{2,1,0:T(8,128)S(1)} all-to-all(f32[16,8,128]{2,1,0:T(8,128)S(1)} %get-tuple-element.68), channel_id=1, replica_groups=mesh['grp'=2,'lat'=8,'lon'=2] {'lat','lon'}, dimensions={0} | all-to-all | bytes 131072 | tf_op jit(solution)/shard_map/all_to_all | solution.py:473
  100.7 1.7 %scale.1 = (f32[16,192,128]{2,1,0:T(8,128)}, f32[1,128]{1,0:T(1,128)}) custom-call(f32[16,8,128]{2,1,0:T(8,128)S(1)} %all_to_all.5.tile_ref, f32[16,192,128]{2,1,0:T(8,128)S(1)} %get-tuple-element.69.w_ref), custom_call_target="tpu_custom_call" | custom-call | tf_op jit(solution)/shard_map/scale/pallas_call | solution.py:475
  (14 shorter events, 0.1 us)
Async XLA Ops:
  0.6 8.4 %copy-start.9 = (f32[2,128]{1,0:T(2,128)S(1)}, f32[2,128]{1,0:T(2,128)}, u32[]{:S(2)}) copy-start(f32[2,128]{1,0:T(2,128)} %constant.2.clone.area_ref) | copy-start | bytes 3076
  0.6 1.4 %copy-start.4 = (f32[16,128,192]{1,2,0:T(8,128)S(1)}, f32[16,128,192]{1,2,0:T(8,128)}, u32[]{:S(2)}) copy-start(f32[16,128,192]{1,2,0:T(8,128)} %param.10) | copy-start | bytes 4718596
  2.1 6.9 %copy-start.10 = (f32[2,7,7,192]{3,0,2,1:T(2,128)S(1)}, f32[2,7,7,192]{3,0,2,1:T(2,128)}, u32[]{:S(2)}) copy-start(f32[2,7,7,192]{3,0,2,1:T(2,128)} %param.11) | copy-start | bytes 225796
  2.1 7.0 %copy-start.5 = (bf16[2,16,128,192]{2,3,1,0:T(8,128)(2,1)S(1)}, bf16[2,16,128,192]{2,3,1,0:T(8,128)(2,1)}, u32[]{:S(2)}) copy-start(bf16[2,16,128,192]{2,3,1,0:T(8,128)(2,1)} %param.16) | copy-start | bytes 4718596
  2.1 7.0 %copy-start.8 = (f32[2,16,128]{2,1,0:T(8,128)S(1)}, f32[2,16,128]{2,1,0:T(8,128)}, u32[]{:S(2)}) copy-start(f32[2,16,128]{2,1,0:T(8,128)} %inv_ref.1) | copy-start | bytes 49156
  3.9 1.4 %collective-permute-start = (bf16[16,8,192]{2,1,0:T(8,128)(2,1)S(1)}, bf16[16,8,192]{2,1,0:T(8,128)(2,1)S(1)}, u32[]{:S(2)}, u32[]{:S(2)}) collective-permute-start(bf16[16,8,192]{2,1,0:T(8,128)(2,1)S(1)} %get-tuple-element.38), channel_id=1, source_target_pairs={{0,1},{1,0},{2,3},{3,2},{4,5},{5,4},{6,7},{7,6},{8,9},{9,8},{10,11... | collective-permute-start | bytes 147464 | tf_op jit(solution)/shard_map/ppermute | solution.py:415
  5.4 16.3 %copy-start.2 = (bf16[2,192,768]{2,1,0:T(8,128)(2,1)S(1)}, bf16[2,192,768]{2,1,0:T(8,128)(2,1)}, u32[]{:S(2)}) copy-start(bf16[2,192,768]{2,1,0:T(8,128)(2,1)} %rest_4_.5) | copy-start | bytes 1769476
  5.4 16.3 %copy-start.3 = (bf16[2,768,192]{1,2,0:T(8,128)(2,1)S(1)}, bf16[2,768,192]{1,2,0:T(8,128)(2,1)}, u32[]{:S(2)}) copy-start(bf16[2,768,192]{1,2,0:T(8,128)(2,1)} %param.14) | copy-start | bytes 1769476
  5.4 16.3 %copy-start.6 = (f32[2,192]{1,0:T(2,128)S(1)}, f32[2,192]{1,0:T(2,128)}, u32[]{:S(2)}) copy-start(f32[2,192]{1,0:T(2,128)} %rest_3_.5) | copy-start | bytes 4612
  5.4 16.3 %copy-start.7 = (f32[2,192]{1,0:T(2,128)S(1)}, f32[2,192]{1,0:T(2,128)}, u32[]{:S(2)}) copy-start(f32[2,192]{1,0:T(2,128)} %rest_6_.5) | copy-start | bytes 4612
  5.4 16.2 %collective-permute-start.1 = (bf16[3,136,192]{2,1,0:T(8,128)(2,1)S(1)}, bf16[3,136,192]{2,1,0:T(8,128)(2,1)S(1)}, u32[]{:S(2)}, u32[]{:S(2)}) collective-permute-start(bf16[3,136,192]{2,1,0:T(8,128)(2,1)S(1)} %get-tuple-element.42), channel_id=1, source_target_pairs={{0,2},{2,0},{4,6},{6,4},{8,10},{10,8},{12,14},{14,12},{1,3},{3,1},... | collective-permute-start | bytes 470024 | tf_op jit(solution)/shard_map/ppermute | solution.py:420
  8.3 13.3 %collective-permute-start.2 = (bf16[3,136,192]{2,1,0:T(8,128)(2,1)S(1)}, bf16[3,136,192]{2,1,0:T(8,128)(2,1)S(1)}, u32[]{:S(2)}, u32[]{:S(2)}) collective-permute-start(bf16[3,136,192]{2,1,0:T(8,128)(2,1)S(1)} %get-tuple-element.43), channel_id=1, source_target_pairs={{2,4},{4,2},{6,8},{8,6},{10,12},{12,10},{3,5},{5,3},{7,9},{9,7},{1... | collective-permute-start | bytes 470024 | tf_op jit(solution)/shard_map/ppermute | solution.py:419
  21.6 2.8 %copy-start = (bf16[2,16,128,768]{3,2,1,0:T(8,128)(2,1)S(1)}, bf16[2,16,128,768]{3,2,1,0:T(8,128)(2,1)}, u32[]{:S(2)}) copy-start(bf16[2,16,128,768]{3,2,1,0:T(8,128)(2,1)} %rest_2_.5) | copy-start | bytes 18874372
  24.4 20.4 %copy-start.1 = (bf16[2,16,128,768]{3,2,1,0:T(8,128)(2,1)S(1)}, bf16[2,16,128,768]{3,2,1,0:T(8,128)(2,1)}, u32[]{:S(2)}) copy-start(bf16[2,16,128,768]{3,2,1,0:T(8,128)(2,1)} %rest_2_.5) | copy-start | bytes 18874372
  29.9 1.3 %collective-permute-start.3 = (bf16[16,8,192]{2,1,0:T(8,128)(2,1)S(1)}, bf16[16,8,192]{2,1,0:T(8,128)(2,1)S(1)}, u32[]{:S(2)}, u32[]{:S(2)}) collective-permute-start(bf16[16,8,192]{2,1,0:T(8,128)(2,1)S(1)} %get-tuple-element.47), channel_id=1, source_target_pairs={{0,1},{1,0},{2,3},{3,2},{4,5},{5,4},{6,7},{7,6},{8,9},{9,8},{10,11... | collective-permute-start | bytes 147464 | tf_op jit(solution)/shard_map/ppermute | solution.py:415
  31.3 13.6 %collective-permute-start.4 = (bf16[3,136,192]{2,1,0:T(8,128)(2,1)S(1)}, bf16[3,136,192]{2,1,0:T(8,128)(2,1)S(1)}, u32[]{:S(2)}, u32[]{:S(2)}) collective-permute-start(bf16[3,136,192]{2,1,0:T(8,128)(2,1)S(1)} %get-tuple-element.50), channel_id=1, source_target_pairs={{0,2},{2,0},{4,6},{6,4},{8,10},{10,8},{12,14},{14,12},{1,3},{3,1},... | collective-permute-start | bytes 470024 | tf_op jit(solution)/shard_map/ppermute | solution.py:420
  35.6 9.2 %collective-permute-start.5 = (bf16[3,136,192]{2,1,0:T(8,128)(2,1)S(1)}, bf16[3,136,192]{2,1,0:T(8,128)(2,1)S(1)}, u32[]{:S(2)}, u32[]{:S(2)}) collective-permute-start(bf16[3,136,192]{2,1,0:T(8,128)(2,1)S(1)} %get-tuple-element.51), channel_id=1, source_target_pairs={{2,4},{4,2},{6,8},{8,6},{10,12},{12,10},{3,5},{5,3},{7,9},{9,7},{1... | collective-permute-start | bytes 470024 | tf_op jit(solution)/shard_map/ppermute | solution.py:419
  53.6 1.3 %collective-permute-start.6 = (bf16[16,8,192]{2,1,0:T(8,128)(2,1)S(1)}, bf16[16,8,192]{2,1,0:T(8,128)(2,1)S(1)}, u32[]{:S(2)}, u32[]{:S(2)}) collective-permute-start(bf16[16,8,192]{2,1,0:T(8,128)(2,1)S(1)} %get-tuple-element.53), channel_id=1, source_target_pairs={{0,1},{1,0},{2,3},{3,2},{4,5},{5,4},{6,7},{7,6},{8,9},{9,8},{10,11... | collective-permute-start | bytes 147464 | tf_op jit(solution)/shard_map/ppermute | solution.py:415
  54.9 12.3 %collective-permute-start.7 = (bf16[3,136,192]{2,1,0:T(8,128)(2,1)S(1)}, bf16[3,136,192]{2,1,0:T(8,128)(2,1)S(1)}, u32[]{:S(2)}, u32[]{:S(2)}) collective-permute-start(bf16[3,136,192]{2,1,0:T(8,128)(2,1)S(1)} %get-tuple-element.56), channel_id=1, source_target_pairs={{0,2},{2,0},{4,6},{6,4},{8,10},{10,8},{12,14},{14,12},{1,3},{3,1},... | collective-permute-start | bytes 470024 | tf_op jit(solution)/shard_map/ppermute | solution.py:420
  58.0 9.2 %collective-permute-start.8 = (bf16[3,136,192]{2,1,0:T(8,128)(2,1)S(1)}, bf16[3,136,192]{2,1,0:T(8,128)(2,1)S(1)}, u32[]{:S(2)}, u32[]{:S(2)}) collective-permute-start(bf16[3,136,192]{2,1,0:T(8,128)(2,1)S(1)} %get-tuple-element.57), channel_id=1, source_target_pairs={{2,4},{4,2},{6,8},{8,6},{10,12},{12,10},{3,5},{5,3},{7,9},{9,7},{1... | collective-permute-start | bytes 470024 | tf_op jit(solution)/shard_map/ppermute | solution.py:419
  72.3 1.3 %collective-permute-start.9 = (bf16[16,8,192]{2,1,0:T(8,128)(2,1)S(1)}, bf16[16,8,192]{2,1,0:T(8,128)(2,1)S(1)}, u32[]{:S(2)}, u32[]{:S(2)}) collective-permute-start(bf16[16,8,192]{2,1,0:T(8,128)(2,1)S(1)} %get-tuple-element.60), channel_id=1, source_target_pairs={{0,1},{1,0},{2,3},{3,2},{4,5},{5,4},{6,7},{7,6},{8,9},{9,8},{10,11... | collective-permute-start | bytes 147464 | tf_op jit(solution)/shard_map/ppermute | solution.py:415
  73.6 12.3 %collective-permute-start.10 = (bf16[3,136,192]{2,1,0:T(8,128)(2,1)S(1)}, bf16[3,136,192]{2,1,0:T(8,128)(2,1)S(1)}, u32[]{:S(2)}, u32[]{:S(2)}) collective-permute-start(bf16[3,136,192]{2,1,0:T(8,128)(2,1)S(1)} %get-tuple-element.63), channel_id=1, source_target_pairs={{0,2},{2,0},{4,6},{6,4},{8,10},{10,8},{12,14},{14,12},{1,3},{3,1},... | collective-permute-start | bytes 470024 | tf_op jit(solution)/shard_map/ppermute | solution.py:420
  76.7 9.2 %collective-permute-start.11 = (bf16[3,136,192]{2,1,0:T(8,128)(2,1)S(1)}, bf16[3,136,192]{2,1,0:T(8,128)(2,1)S(1)}, u32[]{:S(2)}, u32[]{:S(2)}) collective-permute-start(bf16[3,136,192]{2,1,0:T(8,128)(2,1)S(1)} %get-tuple-element.64), channel_id=1, source_target_pairs={{2,4},{4,2},{6,8},{8,6},{10,12},{12,10},{3,5},{5,3},{7,9},{9,7},{1... | collective-permute-start | bytes 470024 | tf_op jit(solution)/shard_map/ppermute | solution.py:419

commit v2 on v1

v2 whole, which is shorter than its diff:
```python
import functools
import math

import jax
import jax.numpy as jnp
import numpy as np
from jax import lax
from jax.experimental import pallas as pl
from jax.experimental.pallas import tpu as pltpu
from jax.sharding import PartitionSpec as P

F32 = jnp.float32
BF16 = jnp.bfloat16
LAT_SPAN = 70.0 * math.pi / 180.0
MARGIN = 8
EXT = 16
VMEM = pltpu.VMEM
ACROSS = (((1,), (1,)), ((), ()))
IN_VMEM = pl.BlockSpec(memory_space=pltpu.VMEM)
IN_HBM = pl.BlockSpec(memory_space=pltpu.HBM)
IN_SMEM = pl.BlockSpec(memory_space=pltpu.SMEM)


def in_vmem(x):
    return pltpu.with_memory_space_constraint(x, pltpu.VMEM)


def tap_index(a, b, flipped):
    return (6 - a) * 7 + (6 - b) if flipped else a * 7 + b


def spread_taps(taps_ref, k0, k1, k2):
    for layer in range(taps_ref.shape[0]):
        for a in range(7):
            rows = taps_ref[layer, a]
            for b in range(7):
                row = rows[b : b + 1, :]
                k0[layer, a * 7 + b] = jnp.broadcast_to(row[:, :128], (8, 128))
                high = jnp.broadcast_to(row[:, 128:], (8, row.shape[1] - 128))
                k1[layer, a * 7 + b] = jnp.concatenate([high, high], axis=1)
        lane = lax.broadcasted_iota(jnp.int32, (8, 128), 1)
        for a in range(3):
            for b in range(7):
                for flipped in (0, 1):
                    low = k1[layer, tap_index(a, b, flipped)]
                    high = k1[layer, tap_index(6 - a, b, flipped)]
                    k2[layer, flipped, a * 7 + b] = jnp.where(lane < 64, low, high)


def fill_row(xs, index, mid, side):
    cols = mid.shape[0]
    xs[index, :MARGIN, :] = side[:MARGIN]
    xs[index, MARGIN : MARGIN + cols, :] = mid
    xs[index, MARGIN + cols :, :] = side[MARGIN:]


def conv_local(load_row, lon_ref, k0, k1, layer, out_ref, xs0, xs1, flipped, beside=None):
    rows, cols, _ = out_ref.shape
    half = rows // 2

    @pl.loop(0, half)
    def _(r):
        low, high = load_row(r), load_row(r + half)
        low_side, high_side = lon_ref[r].astype(F32), lon_ref[r + half].astype(F32)
        fill_row(xs0, r, low[:, :128], low_side[:, :128])
        fill_row(xs0, r + half, high[:, :128], high_side[:, :128])
        mid = jnp.concatenate([low[:, 128:], high[:, 128:]], axis=1)
        side = jnp.concatenate([low_side[:, 128:], high_side[:, 128:]], axis=1)
        fill_row(xs1, r + 3, mid, side)

    lane = lax.broadcasted_iota(jnp.int32, (cols + 2 * MARGIN, 128), 1)
    for q in range(3):
        above, below = xs1[q + half], xs1[q + 3]
        xs1[q] = jnp.where(lane < 64, 0.0, pltpu.roll(above, 64, 1))
        xs1[q + half + 3] = jnp.where(lane < 64, pltpu.roll(below, 64, 1), 0.0)

    @pl.loop(0, cols // 8)
    def _(j):
        base = pl.multiple_of(j * 8, 8)
        acc = [None] * rows
        for b in range(7):
            taps = [k0[layer, tap_index(a, b, flipped)] for a in range(7)]
            for r in range(rows):
                x = xs0[r, pl.ds(base + (MARGIN - 3 + b), 8), :]
                for a in range(7):
                    o = r + 3 - a
                    if 0 <= o < rows:
                        term = taps[a] * x
                        acc[o] = term if acc[o] is None else acc[o] + term
        for o in range(rows):
            out_ref[o, pl.ds(base, 8), :128] = acc[o]
        acc = [None] * half
        for b in range(7):
            taps = [k1[layer, tap_index(a, b, flipped)] for a in range(7)]
            for q in range(half + 6):
                x = xs1[q, pl.ds(base + (MARGIN - 3 + b), 8), :]
                for a in range(7):
                    o = q - a
                    if 0 <= o < half:
                        term = taps[a] * x
                        acc[o] = term if acc[o] is None else acc[o] + term
        for o in range(half):
            out_ref[o, pl.ds(base, 8), 128:] = acc[o][:, :64]
            out_ref[o + half, pl.ds(base, 8), 128:] = acc[o][:, 64:]
        if beside is not None:
            beside(j)


def conv_scratch(rows, cols):
    return [
        pltpu.VMEM((rows, cols + 2 * MARGIN, 128), F32),
        pltpu.VMEM((rows // 2 + 6, cols + 2 * MARGIN, 128), F32),
    ]


def conv_kernel(layer, flipped, f_ref, lon_ref, k0, k1, out_ref, *scratch):
    def load_row(r):
        return f_ref[r].astype(BF16).astype(F32)

    conv_local(load_row, lon_ref, k0, k1, layer, out_ref, *scratch, flipped)


def first_conv_kernel(
    area_ref, f_ref, lon_ref, taps_ref, inv_ref, turned_ref, slope_hbm, out_ref, sum_ref, inv_out, normed_out,
    k0, k1, k2, slope_out, xs0, xs1, sems,
):
    rows, cols, _ = f_ref.shape
    start = lax.axis_index("lat") * rows
    fetches = [
        pltpu.make_async_copy(slope_hbm.at[layer], slope_out.at[layer], sems.at[layer])
        for layer in range(slope_hbm.shape[0])
    ]
    for fetch in fetches:
        fetch.start()
    spread_taps(taps_ref, k0, k1, k2)
    one = lax.broadcasted_iota(jnp.int32, (cols, cols), 0) == lax.broadcasted_iota(jnp.int32, (cols, cols), 1)
    eye = jnp.where(one, 1.0, 0.0).astype(BF16)

    def turn_row(r):
        x = f_ref[r]
        sum_ref[...] += area_ref[0, start + r] * jnp.sum(x * x, axis=0, keepdims=True)
        for layer in range(inv_ref.shape[0]):
            turned = lax.dot_general(eye, turned_ref[layer, r], ACROSS, preferred_element_type=F32)
            normed_out[layer, r] = turned.astype(BF16)
            inv = inv_ref[layer, pl.ds(r, 1), :]
            inv_out[layer, r] = jnp.transpose(jnp.broadcast_to(inv, (128, cols)))

    def load_row(r):
        return f_ref[r].astype(BF16).astype(F32)

    sum_ref[...] = jnp.zeros_like(sum_ref)
    steps = cols // 8
    for j in range(steps, rows):
        turn_row(j)

    def beside(j):
        if rows >= steps:
            turn_row(j)
        else:
            pl.when(j < rows)(lambda: turn_row(j))

    conv_local(load_row, lon_ref, k0, k1, 0, out_ref, xs0, xs1, False, beside)
    for fetch in fetches:
        fetch.wait()


def place_halo(parity, a_ref, b_ref, h0, h1):
    cols = a_ref.shape[1] - EXT

    def put(ref, index, row):
        ref[index, :MARGIN, :] = row[cols : cols + MARGIN]
        ref[index, MARGIN : MARGIN + cols, :] = row[:cols]
        ref[index, MARGIN + cols :, :] = row[cols + MARGIN :]

    for e in range(3):
        put(h0, (1 - parity) * 3 + e, a_ref[e, :, :128].astype(F32))
        put(h0, parity * 3 + e, b_ref[e, :, :128].astype(F32))
        a_up, a_down = a_ref[e, :, 128:].astype(F32), a_ref[2 - e, :, 128:].astype(F32)
        b_up, b_down = b_ref[e, :, 128:].astype(F32), b_ref[2 - e, :, 128:].astype(F32)
        up, down = jnp.where(parity == 1, a_up, b_up), jnp.where(parity == 1, b_down, a_down)
        put(h1, e, jnp.concatenate([up, down], axis=1))


def conv_halo(h0, h1, acc_ref, k0, k2, layer, edge, flipped):
    rows, cols, _ = acc_ref.shape
    unroll = 2

    def add(acc, index, term):
        acc[index] = term if acc[index] is None else acc[index] + term

    @pl.loop(0, cols // (8 * unroll))
    def _(block):
        bases = [pl.multiple_of(block * (8 * unroll) + 8 * i, 8) for i in range(unroll)]
        acc = [[None] * 6 for _ in bases]
        for b in range(7):
            taps = {a: k0[layer, tap_index(a, b, flipped)] for a in (0, 1, 2, 4, 5, 6)}
            for i, base in enumerate(bases):
                for e in range(3):
                    upper = h0[e, pl.ds(base + (MARGIN - 3 + b), 8), :]
                    for o in range(e + 1):
                        add(acc[i], o, taps[e - o] * upper)
                    lower = h0[3 + e, pl.ds(base + (MARGIN - 3 + b), 8), :]
                    for p in range(e, 3):
                        add(acc[i], 3 + p, taps[6 + e - p] * lower)
        for i, base in enumerate(bases):
            for o in range(6):
                own = o if o < 3 else rows - 6 + o
                edge[o, pl.ds(base, 8), :128] = acc_ref[own, pl.ds(base, 8), :128] + acc[i][o]
        acc = [[None] * 3 for _ in bases]
        for b in range(7):
            taps = [k2[layer, int(flipped), a * 7 + b] for a in range(3)]
            for i, base in enumerate(bases):
                for e in range(3):
                    both = h1[e, pl.ds(base + (MARGIN - 3 + b), 8), :]
                    for o in range(e + 1):
                        add(acc[i], o, taps[e - o] * both)
        for i, base in enumerate(bases):
            for o in range(3):
                edge[o, pl.ds(base, 8), 128:] = acc_ref[o, pl.ds(base, 8), 128:] + acc[i][o][:, :64]
                own = acc_ref[rows - 1 - o, pl.ds(base, 8), 128:]
                edge[5 - o, pl.ds(base, 8), 128:] = own + acc[i][o][:, 64:]


def halo_scratch(cols, chans):
    return [
        pltpu.VMEM((6, cols + 2 * MARGIN, 128), F32),
        pltpu.VMEM((3, cols + 2 * MARGIN, 128), F32),
        pltpu.VMEM((6, cols, chans), F32),
    ]


def wide(inv, chans):
    return jnp.concatenate([inv, inv[:, : chans - 128]], axis=1)


def project(y, normed, inv):
    chans = y.shape[1]
    normal = normed.astype(F32)
    first = jnp.sum(y, axis=1, keepdims=True) * (1.0 / chans)
    second = jnp.sum(normal * y, axis=1, keepdims=True) * (1.0 / chans)
    return inv * (y - first - normal * second)


def forward_net(y, normed, inv, slope, gain, w_in, w_out_turned, scale):
    operand = (gain * project(y, normed, inv)).astype(BF16)
    hidden = jnp.dot(operand, w_in, preferred_element_type=F32)
    gated = (slope.astype(F32) * hidden).astype(BF16)
    return scale * lax.dot_general(gated, w_out_turned, ACROSS, preferred_element_type=F32)


def adjoint_net(g, normed, inv, slope, gain, w_in, w_out_turned, scale):
    scaled = (scale * g).astype(BF16)
    hidden = jnp.dot(scaled, w_out_turned, preferred_element_type=F32)
    gated = (slope.astype(F32) * hidden).astype(BF16)
    back = lax.dot_general(gated, w_in, ACROSS, preferred_element_type=F32)
    return project(gain * back, normed, inv).astype(BF16)


def send_rows(parity, field, lon_ref, a_ref, b_ref):
    rows, cols = field.shape[0], field.shape[1]
    for e in range(3):
        a_ref[e, :cols, :] = field[(1 - parity) * (rows - 3) + e].astype(BF16)
        b_ref[e, :cols, :] = field[parity * (rows - 3) + e].astype(BF16)
    for r in range(rows):
        lon_ref[r, :MARGIN, :] = field[r, cols - MARGIN :, :].astype(BF16)
        lon_ref[r, MARGIN:, :] = field[r, :MARGIN, :].astype(BF16)


def flat(x):
    return x.reshape(x.shape[0] * x.shape[1], x.shape[2])


class Rows:
    def __init__(self, rows, outer):
        self.spans = [(0, 3), (rows - 3, 3)] if outer else [(3, rows - 6)]

    def get(self, ref, *lead):
        return jnp.concatenate([flat(ref[(*lead, slice(a, a + n))]) for a, n in self.spans], axis=0)

    def put(self, ref, value):
        cols, done = ref.shape[1], 0
        for a, n in self.spans:
            ref[a : a + n] = value[done * cols : (done + n) * cols].reshape(n, cols, value.shape[1])
            done += n

    def numbers(self):
        return [a + i for a, n in self.spans for i in range(n)]


def both_blocks(acc_ref, edge, fn):
    rows = acc_ref.shape[0]
    inner, outer = Rows(rows, False), Rows(rows, True)
    fn(outer, flat(edge[...]))
    fn(inner, inner.get(acc_ref))


def net_operands(layer, block, refs):
    normed_ref, inv_ref, slope_ref, gain_ref, win_ref, wout_ref, scale_ref = refs
    return [
        block.get(normed_ref, layer), wide(block.get(inv_ref, layer), normed_ref.shape[3]), block.get(slope_ref, layer),
        gain_ref[layer : layer + 1, :], win_ref[layer], wout_ref[layer], scale_ref[layer : layer + 1, :],
    ]


def tangent_kernel(layer, last, area_ref, acc_ref, a_ref, b_ref, k0, k2, t_ref, *rest):
    net, rest = rest[:7], rest[7:]
    rows, cols, chans = acc_ref.shape
    lat = lax.axis_index("lat")
    if last:
        g_ref, db_ref, sum_ref, lon_ref, sa_ref, sb_ref, h0, h1, edge = rest
        sum_ref[...] = jnp.zeros_like(sum_ref)
    else:
        t_out, lon_ref, sa_ref, sb_ref, h0, h1, edge = rest
    place_halo(lat % 2, a_ref, b_ref, h0, h1)
    conv_halo(h0, h1, acc_ref, k0, k2, layer, edge, False)

    def work(block, y):
        operands = net_operands(layer, block, net)
        t = block.get(t_ref) + forward_net(y, *operands)
        if not last:
            block.put(t_out, t)
            return
        parts = []
        for i, r in enumerate(block.numbers()):
            u = t[i * cols : (i + 1) * cols]
            g = area_ref[0, lat * rows + r] * u
            sum_ref[...] += jnp.sum(g * u, axis=0, keepdims=True)
            parts.append(g)
        g = jnp.concatenate(parts, axis=0)
        block.put(g_ref, g)
        block.put(db_ref, adjoint_net(g, *operands))

    both_blocks(acc_ref, edge, work)
    send_rows(lat % 2, db_ref if last else t_out, lon_ref, sa_ref, sb_ref)


def adjoint_kernel(layer, acc_ref, a_ref, b_ref, k0, k2, g_ref, *rest):
    net, (g_out, db_ref, lon_ref, sa_ref, sb_ref, h0, h1, edge) = rest[:7], rest[7:]
    parity = lax.axis_index("lat") % 2
    place_halo(parity, a_ref, b_ref, h0, h1)
    conv_halo(h0, h1, acc_ref, k0, k2, layer + 1, edge, True)

    def work(block, y):
        g = block.get(g_ref) + y
        block.put(g_out, g)
        block.put(db_ref, adjoint_net(g, *net_operands(layer, block, net)))

    both_blocks(acc_ref, edge, work)
    send_rows(parity, db_ref, lon_ref, sa_ref, sb_ref)


def final_kernel(
    area_ref, acc_ref, a_ref, b_ref, k0, k2, g_ref, vv_ref, uu_ref, w_ref, tile_ref, h0, h1, edge, ww
):
    rows = acc_ref.shape[0]
    lat = lax.axis_index("lat")
    place_halo(lat % 2, a_ref, b_ref, h0, h1)
    conv_halo(h0, h1, acc_ref, k0, k2, 0, edge, True)
    ww[...] = jnp.zeros_like(ww)

    def row(r, y):
        g = g_ref[r] + y
        w = g * area_ref[1, lat * rows + r]
        w_ref[r] = jnp.transpose(w)
        ww[...] += jnp.sum(g * w, axis=0, keepdims=True)

    for e in range(3):
        row(e, edge[e])
        row(rows - 3 + e, edge[3 + e])

    for r in range(3, rows - 3):
        row(r, acc_ref[r])

    which = lax.broadcasted_iota(jnp.int32, (8, 128), 0)
    vv, uu, wv = (jnp.sum(ref[...]) for ref in (vv_ref, uu_ref, ww))
    tile = jnp.where(which == 0, vv, jnp.where(which == 1, uu, jnp.where(which == 2, wv, 0.0)))
    for i in range(tile_ref.shape[0]):
        tile_ref[i] = tile


def scale_kernel(total, tile_ref, w_ref, out_hbm, growth_ref, scaled, sems):
    sums = jnp.sum(tile_ref[...], axis=0) * (1.0 / total)
    vv, uu, ww = sums[0:1, :], sums[1:2, :], sums[2:3, :]
    growth_ref[...] = jnp.sqrt(uu / (vv + 1e-06))
    factor = 1.0 / jnp.sqrt(ww + 1e-06)
    copies = []
    for r in range(w_ref.shape[0]):
        scaled[r] = w_ref[r] * factor
        copies.append(pltpu.make_async_copy(scaled.at[r], out_hbm.at[r], sems.at[r]))
        copies[-1].start()
    for copy in copies:
        copy.wait()


def extend_kernel(lon_ref, sa_in, sb_in, sa_ref, sb_ref):
    rows, cols = lon_ref.shape[0], sa_ref.shape[1] - EXT
    parity = lax.axis_index("lat") % 2
    for e in range(3):
        sa_ref[e, :cols, :] = sa_in[e, :cols, :]
        sb_ref[e, :cols, :] = sb_in[e, :cols, :]
        sa_ref[e, cols:, :] = lon_ref[(1 - parity) * (rows - 3) + e]
        sb_ref[e, cols:, :] = lon_ref[parity * (rows - 3) + e]


def edges_kernel(turned_hbm, t_ref, lon_ref, sa_ref, sb_ref, turned, sems):
    rows = turned.shape[0]
    copies = [pltpu.make_async_copy(turned_hbm.at[r], turned.at[r], sems.at[r]) for r in range(rows)]
    for copy in copies:
        copy.start()
    for r, copy in enumerate(copies):
        copy.wait()
        t_ref[r] = jnp.transpose(turned[r])
    send_rows(lax.axis_index("lat") % 2, t_ref, lon_ref, sa_ref, sb_ref)


def params():
    return pltpu.CompilerParams(vmem_limit_bytes=16 * 1024 * 1024)


def on_device(lat_size, lon_size, perturb, kernels, gains, w_in, w_out, scales, normed, inv_std, slope):
    rows, cols, chans = perturb.shape
    hidden = w_in.shape[2]
    layers = kernels.shape[0]
    lat_total = rows * lat_size
    angles = LAT_SPAN * (np.arange(lat_total) + 0.5) / lat_total
    total = float(np.sum(np.cos(angles))) * cols * lon_size * chans
    table = np.stack([np.cos(angles), 1.0 / np.cos(angles)]).astype(np.float32)
    area = jnp.asarray(table)
    across_cells = jnp.transpose(w_out, (0, 2, 1))
    swap_a = [(i, i ^ 1) for i in range(lat_size) if i ^ 1 < lat_size]
    swap_b = [pair for i in range(1, lat_size - 1, 2) for pair in ((i, i + 1), (i + 1, i))]
    swap_lon = [(i, (i + 1) % lon_size) for i in range(lon_size)]

    lon_shape = VMEM((rows, EXT, chans), BF16)
    send_shape = VMEM((3, cols + EXT, chans), BF16)
    full32 = VMEM((rows, cols, chans), F32)
    full16 = VMEM((rows, cols, chans), BF16)
    sums = VMEM((1, chans), F32)

    def call(kernel, out_shape, in_specs, args, scratch=(), flops=0, name=None):
        args = [pltpu.with_memory_space_constraint(x, spec.memory_space) if spec is not IN_SMEM else x for spec, x in zip(in_specs, args)]
        return pl.pallas_call(
            kernel,
            out_shape=out_shape,
            in_specs=in_specs,
            out_specs=[IN_VMEM] * len(out_shape),
            scratch_shapes=list(scratch),
            compiler_params=params(),
            cost_estimate=pl.CostEstimate(flops=flops, bytes_accessed=4_000_000, transcendentals=0),
            name=name,
        )(*args)

    def exchange(lon, send_a, send_b):
        side = lax.ppermute(lon, "lon", swap_lon)
        send_a, send_b = call(
            extend_kernel, [send_shape] * 2, [IN_VMEM] * 3, (side, send_a, send_b), name="extend"
        )
        halo_a = lax.ppermute(send_a, "lat", swap_a)
        halo_b = lax.ppermute(send_b, "lat", swap_b)
        return side, halo_a, halo_b

    conv_flops = 2 * 49 * rows * cols * chans
    net_flops = 4 * rows * cols * chans * hidden
    kscr = conv_scratch(rows, cols)
    hscr = halo_scratch(cols, chans)

    tangent, lon, send_a, send_b = call(
        edges_kernel, [full32, lon_shape, send_shape, send_shape], [IN_HBM], (jnp.transpose(perturb, (0, 2, 1)),),
        [pltpu.VMEM((rows, chans, cols), F32), pltpu.SemaphoreType.DMA((rows,))], name="edges",
    )
    side, halo_a, halo_b = exchange(lon, send_a, send_b)
    acc, vv, inv_cells, normed_cells, k0, k1, k2, slope_cells = call(
        first_conv_kernel,
        [
            full32, sums, VMEM((layers, rows, cols, 128), F32), VMEM((layers, rows, cols, chans), BF16),
            VMEM((layers, 49, 8, 128), F32), VMEM((layers, 49, 8, 128), F32), VMEM((layers, 2, 21, 8, 128), F32),
            VMEM(slope.shape, BF16),
        ],
        [IN_SMEM] + [IN_VMEM] * 5 + [IN_HBM],
        (area, tangent, side, kernels, inv_std, jnp.transpose(normed, (0, 1, 3, 2)), slope),
        kscr + [pltpu.SemaphoreType.DMA((layers,))], conv_flops, "conv_first",
    )
    net = (normed_cells, inv_cells, slope_cells, gains, w_in, across_cells, scales)
    for layer in range(layers):
        last = layer == layers - 1
        outs = [full32, full16, sums] if last else [full32]
        outs = outs + [lon_shape, send_shape, send_shape]
        got = call(
            functools.partial(tangent_kernel, layer, last), outs, [IN_SMEM] + [IN_VMEM] * 13,
            (area, acc, halo_a, halo_b, k0, k2, tangent) + net, hscr, net_flops, f"tangent{layer}",
        )
        side, halo_a, halo_b = exchange(*got[-3:])
        if last:
            grad, back, uu = got[:3]
        else:
            tangent = got[0]
            (acc,) = call(
                functools.partial(conv_kernel, layer + 1, False), [full32], [IN_VMEM] * 4, (tangent, side, k0, k1),
                kscr, conv_flops, f"conv{layer + 1}",
            )
    for layer in range(layers - 1, -1, -1):
        (acc,) = call(
            functools.partial(conv_kernel, layer, True), [full32], [IN_VMEM] * 4, (back, side, k0, k1),
            kscr, conv_flops, f"convt{layer}",
        )
        if layer > 0:
            grad, back, lon, send_a, send_b = call(
                functools.partial(adjoint_kernel, layer - 1), [full32, full16, lon_shape, send_shape, send_shape],
                [IN_VMEM] * 13, (acc, halo_a, halo_b, k0, k2, grad) + net, hscr, net_flops, f"adjoint{layer - 1}",
            )
            side, halo_a, halo_b = exchange(lon, send_a, send_b)
    members = lat_size * lon_size
    w, tile = call(
        final_kernel, [VMEM((rows, chans, cols), F32), VMEM((members, 8, 128), F32)], [IN_SMEM] + [IN_VMEM] * 8,
        (area, acc, halo_a, halo_b, k0, k2, grad, vv, uu), hscr + [pltpu.VMEM((1, chans), F32)], 0, "final",
    )
    tile = lax.all_to_all(tile, ("lat", "lon"), 0, 0, tiled=True)
    new_vec, growth = pl.pallas_call(
        functools.partial(scale_kernel, total),
        out_shape=[jax.ShapeDtypeStruct((rows, chans, cols), F32), jax.ShapeDtypeStruct((1, 128), F32)],
        in_specs=[IN_VMEM, IN_VMEM],
        out_specs=[IN_HBM, IN_VMEM],
        scratch_shapes=[pltpu.VMEM((rows, chans, cols), F32), pltpu.SemaphoreType.DMA((rows,))],
        compiler_params=params(),
        name="scale",
    )(in_vmem(tile), in_vmem(w))
    return jnp.transpose(new_vec, (0, 2, 1)), growth[0, :1]


def solution(mesh):
    in_specs = (
        P(("grp", "lat"), "lon", None),
        P(),
        P(),
        P(),
        P(),
        P(),
        P(None, ("grp", "lat"), "lon", None),
        P(None, ("grp", "lat"), "lon"),
        P(None, ("grp", "lat"), "lon", None),
    )
    out_specs = (P(("grp", "lat"), "lon", None), P("grp"))
    fn = functools.partial(on_device, mesh.shape["lat"], mesh.shape["lon"])
    return jax.shard_map(fn, mesh=mesh, in_specs=in_specs, out_specs=out_specs, check_vma=False)
```

time: 103 us -> 94.4 us (0.917)
  Pallas kernels: 60.4 us -> 53.3 us
  local copies, waits for them, and re-layouts: 4.25 us -> 0.06 us
  waiting for transfers between devices: 8.55 us -> 11.2 us
  blocking collectives: 11.5 us -> 12.6 us
    pallas_call x13, Pallas kernels: 58.6 us -> 51.5 us  [call(): pl.pallas_call(kernel, out_shape=out_shape, in_specs=in_specs, out_specs=...]
    unnamed x23 -> x17, local copies, waits for them, and re-layouts: 4.25 us -> 0.06 us
    ppermute x4, waiting for transfers between devices: 3.92 us -> 6.24 us  [exchange(): halo_a = lax.ppermute(send_a, 'lat', swap_a)]
    ppermute x4, starting transfers between devices: 13.4 us -> 12.4 us  [exchange(): halo_a = lax.ppermute(send_a, 'lat', swap_a)]
    all_to_all x1, blocking collectives: 11.5 us -> 12.6 us  [on_device(): tile = lax.all_to_all(tile, ('lat', 'lon'), 0, 0, tiled=True)]
where the time goes in v2:
time: 94.4 us; the launch traced here: 94.1 us
  Pallas kernels  53.3 us (56%)
  starting transfers between devices  15.9 us (17%)
  blocking collectives  12.6 us (13%)
  waiting for transfers between devices  11.2 us (12%)
  between operations  1.07 us (1%)
    pallas_call x13, Pallas kernels, call(): pl.pallas_call(kernel, out_shape=out_shape, in_specs=in_specs, out_specs=...  51.5 us
    all_to_all x1, blocking collectives, on_device(): tile = lax.all_to_all(tile, ('lat', 'lon'), 0, 0, tiled=True)  12.6 us
    ppermute x4, starting transfers between devices, exchange(): halo_a = lax.ppermute(send_a, 'lat', swap_a)  12.4 us
    ppermute x4, waiting for transfers between devices, exchange(): halo_a = lax.ppermute(send_a, 'lat', swap_a)  6.24 us
    ppermute x4, waiting for transfers between devices, exchange(): side = lax.ppermute(lon, 'lon', swap_lon)  4.99 us
    ppermute x4, starting transfers between devices, exchange(): halo_b = lax.ppermute(send_b, 'lat', swap_b)  2.83 us
  transfers between devices with their start and end apart: 12, of which 7 were waited for; matrix products, arithmetic and copies ran while one was open for 0% of the time, Pallas kernels for 33%

profile of v2, /device:TPU:0, one launch (start us, length us, event | category | flops | bytes accessed | tf_op | source)
XLA Modules:
  0.0 94.1 jit_solution(7378418719151725217)
XLA Ops:
  0.6 0.0 copy-start.6
  0.6 0.0 copy-start.7
  0.7 0.0 copy-start.5
  0.7 0.0 copy-start.2
  0.7 2.8 %edges.1 = (f32[16,128,192]{2,1,0:T(8,128)S(1)}, bf16[16,16,192]{2,1,0:T(8,128)(2,1)S(1)}, bf16[3,144,192]{2,1,0:T(8,128)(2,1)S(1)}, bf16[3,144,192]{2,1,0:T(8,128)(2,1)S(1)}) custom-call(f32[16,192,128]{2,1,0:T(8,128)} %bitcast.10), custom_call_target="tpu_custom_call" | custom-call | bytes 4000000 | tf_op jit(solution)/shard_map/edges/pallas_call | solution.py:442
  3.5 0.5 collective-permute-start
  4.0 1.0 %collective-permute-done.lon_ref = bf16[16,16,192]{2,1,0:T(8,128)(2,1)S(1)} collective-permute-done((bf16[16,16,192]{2,1,0:T(8,128)(2,1)S(1)}, bf16[16,16,192]{2,1,0:T(8,128)(2,1)S(1)}, u32[]{:S(2)}, u32[]{:S(2)}) %collective-permute-start) | collective-permute-done | bytes 98336 | tf_op jit(solution)/shard_map/ppermute | solution.py:454
  5.1 2.9 %collective-permute-start.1 = (bf16[3,144,192]{2,1,0:T(8,128)(2,1)S(1)}, bf16[3,144,192]{2,1,0:T(8,128)(2,1)S(1)}, u32[]{:S(2)}, u32[]{:S(2)}) collective-permute-start(bf16[3,144,192]{2,1,0:T(8,128)(2,1)S(1)} %get-tuple-element.46), channel_id=1, source_target_pairs={{0,2},{2,0},{4,6},{6,4},{8,10},{10,8},{12,14},{14,12},{1,3},{3,1},... | collective-permute-start | bytes 497672 | tf_op jit(solution)/shard_map/ppermute | solution.py:458
  8.0 0.7 collective-permute-start.2
  8.7 0.0 copy-done.6
  8.7 0.0 copy-done.5
  8.7 0.0 copy-done.2
  8.7 0.0 copy-start
  8.7 0.0 copy-start.1
  8.8 0.0 copy-start.3
  8.8 0.0 copy-start.4
  8.8 10.0 %conv_first.1 = (f32[16,128,192]{2,1,0:T(8,128)S(1)}, f32[1,192]{1,0:T(1,128)S(1)}, f32[2,16,128,128]{3,2,1,0:T(8,128)S(1)}, bf16[2,16,128,192]{3,2,1,0:T(8,128)...) custom-call(f32[2,128]{1,0:T(2,128)S(1)} %copy-done.6, ...), custom_call_target="tpu_custom_call" | custom-call | flops 38535168 | bytes 4000000 | tf_op jit(solution)/shard_map/conv_first/pallas_call | solution.py:442
  18.8 0.0 collective-permute-done.1.a_ref
  18.8 0.0 collective-permute-done.2.b_ref
  18.8 0.0 copy-done
  18.8 0.0 copy-done.1
  18.8 4.4 %tangent0.1 = (f32[16,128,192]{2,1,0:T(8,128)S(1)}, bf16[16,16,192]{2,1,0:T(8,128)(2,1)S(1)}, bf16[3,144,192]{2,1,0:T(8,128)(2,1)S(1)}, bf16[3,144,192]{2,1,0:T(8,128)(2,1)S(1)}) custom-call(f32[2,128]{1,0:T(2,128)S(1)} %copy-done.6, f32[16,128,192]{2,1,0:T(8,128)S(1)} %get-tuple-element.43.acc_ref, bf16[3,144,192]{2,1,0:T(8,128)(2,1)S(1)} %collective-permute-done.1.a_ref, ...), custom_call_target="tpu_custom_call" | custom-call | flops 1207959552 | bytes 4000000 | tf_op jit(solution)/shard_map/tangent0/pallas_call | solution.py:442
  23.3 0.1 collective-permute-start.3
  23.4 1.3 %collective-permute-done.3.lon_ref = bf16[16,16,192]{2,1,0:T(8,128)(2,1)S(1)} collective-permute-done((bf16[16,16,192]{2,1,0:T(8,128)(2,1)S(1)}, bf16[16,16,192]{2,1,0:T(8,128)(2,1)S(1)}, u32[]{:S(2)}, u32[]{:S(2)}) %collective-permute-start.3) | collective-permute-done | bytes 98336 | tf_op jit(solution)/shard_map/ppermute | solution.py:454
  24.7 4.3 %collective-permute-start.4 = (bf16[3,144,192]{2,1,0:T(8,128)(2,1)S(1)}, bf16[3,144,192]{2,1,0:T(8,128)(2,1)S(1)}, u32[]{:S(2)}, u32[]{:S(2)}) collective-permute-start(bf16[3,144,192]{2,1,0:T(8,128)(2,1)S(1)} %get-tuple-element.58), channel_id=1, source_target_pairs={{0,2},{2,0},{4,6},{6,4},{8,10},{10,8},{12,14},{14,12},{1,3},{3,1},... | collective-permute-start | bytes 497672 | tf_op jit(solution)/shard_map/ppermute | solution.py:458
  29.1 0.7 collective-permute-start.5
  29.7 6.9 %conv1.1.acc_ref = f32[16,128,192]{2,1,0:T(8,128)S(1)} custom-call(f32[16,128,192]{2,1,0:T(8,128)S(1)} %get-tuple-element.53.f_ref.t_ref, bf16[16,16,192]{2,1,0:T(8,128)(2,1)S(1)} %collective-permute-done.3.lon_ref, f32[2,49,8,128]{3,2,1,0:T(8,128)S(1)} %get-tuple-element.48.k0, f32[2,49,8,128]{3,2,1,0:T(8,128)S(1)} %get-tuple-element.55.k1), custom_call_target="tpu_custom_call" | custom-call | flops 38535168 | bytes 4000000 | tf_op jit(solution)/shard_map/conv1/pallas_call | solution.py:442
  36.7 2.1 %collective-permute-done.4.a_ref = bf16[3,144,192]{2,1,0:T(8,128)(2,1)S(1)} collective-permute-done((bf16[3,144,192]{2,1,0:T(8,128)(2,1)S(1)}, bf16[3,144,192]{2,1,0:T(8,128)(2,1)S(1)}, u32[]{:S(2)}, u32[]{:S(2)}) %collective-permute-start.4) | collective-permute-done | bytes 165920 | tf_op jit(solution)/shard_map/ppermute | solution.py:458
  38.8 0.0 collective-permute-done.5.b_ref
  38.8 6.8 %tangent1.1 = (f32[16,128,192]{2,1,0:T(8,128)S(1)}, bf16[16,128,192]{2,1,0:T(8,128)(2,1)S(1)}, f32[1,192]{1,0:T(1,128)S(1)}, bf16[16,16,192]{2,1,0:T(8,128)(2,1)...) custom-call(f32[2,128]{1,0:T(2,128)S(1)} %copy-done.6, f32[16,128,192]{2,1,0:T(8,128)S(1)} %conv1.1.acc_ref, ...), custom_call_target="tpu_custom_call" | custom-call | flops 1207959552 | bytes 4000000 | tf_op jit(solution)/shard_map/tangent1/pallas_call | solution.py:442
  45.6 0.1 collective-permute-start.6
  45.7 1.3 %collective-permute-done.6.lon_ref = bf16[16,16,192]{2,1,0:T(8,128)(2,1)S(1)} collective-permute-done((bf16[16,16,192]{2,1,0:T(8,128)(2,1)S(1)}, bf16[16,16,192]{2,1,0:T(8,128)(2,1)S(1)}, u32[]{:S(2)}, u32[]{:S(2)}) %collective-permute-start.6) | collective-permute-done | bytes 98336 | tf_op jit(solution)/shard_map/ppermute | solution.py:454
  47.0 2.5 %collective-permute-start.7 = (bf16[3,144,192]{2,1,0:T(8,128)(2,1)S(1)}, bf16[3,144,192]{2,1,0:T(8,128)(2,1)S(1)}, u32[]{:S(2)}, u32[]{:S(2)}) collective-permute-start(bf16[3,144,192]{2,1,0:T(8,128)(2,1)S(1)} %get-tuple-element.64), channel_id=1, source_target_pairs={{0,2},{2,0},{4,6},{6,4},{8,10},{10,8},{12,14},{14,12},{1,3},{3,1},... | collective-permute-start | bytes 497672 | tf_op jit(solution)/shard_map/ppermute | solution.py:458
  49.6 0.8 collective-permute-start.8
  50.4 6.9 %convt1.1.acc_ref = f32[16,128,192]{2,1,0:T(8,128)S(1)} custom-call(bf16[16,128,192]{2,1,0:T(8,128)(2,1)S(1)} %get-tuple-element.60.f_ref, bf16[16,16,192]{2,1,0:T(8,128)(2,1)S(1)} %collective-permute-done.6.lon_ref, f32[2,49,8,128]{3,2,1,0:T(8,128)S(1)} %get-tuple-element.48.k0, f32[2,49,8,128]{3,2,1,0:T(8,128)S(1)} %get-tuple-element.55.k1), custom_call_target="tpu_custom_call" | custom-call | flops 38535168 | bytes 4000000 | tf_op jit(solution)/shard_map/convt1/pallas_call | solution.py:442
  57.3 2.0 %collective-permute-done.7.a_ref = bf16[3,144,192]{2,1,0:T(8,128)(2,1)S(1)} collective-permute-done((bf16[3,144,192]{2,1,0:T(8,128)(2,1)S(1)}, bf16[3,144,192]{2,1,0:T(8,128)(2,1)S(1)}, u32[]{:S(2)}, u32[]{:S(2)}) %collective-permute-start.7) | collective-permute-done | bytes 165920 | tf_op jit(solution)/shard_map/ppermute | solution.py:458
  59.3 0.0 collective-permute-done.8.b_ref
  59.3 4.0 %adjoint0.1 = (f32[16,128,192]{2,1,0:T(8,128)S(1)}, bf16[16,128,192]{2,1,0:T(8,128)(2,1)S(1)}, bf16[16,16,192]{2,1,0:T(8,128)(2,1)S(1)}, bf16[3,144,192]{2,1,0:T(8,128)(2,1)S(1)}, bf16[3,144,192]{2,1,0:T(8,128)(2,1)S(1)}) custom-call(f32[16,128,192]{2,1,0:T(8,128)S(1)} %convt1.1.acc_ref, bf16[3,144,192]{2,1,0:T(8,128)(2,1)S(1)} %collective-permute-done.7.a_ref, ...), custom_call_target="tpu_custom_call" | custom-call | flops 1207959552 | bytes 4000000 | tf_op jit(solution)/shard_map/adjoint0/pallas_call | solution.py:442
  63.3 0.1 collective-permute-start.9
  63.4 1.3 %collective-permute-done.9.lon_ref = bf16[16,16,192]{2,1,0:T(8,128)(2,1)S(1)} collective-permute-done((bf16[16,16,192]{2,1,0:T(8,128)(2,1)S(1)}, bf16[16,16,192]{2,1,0:T(8,128)(2,1)S(1)}, u32[]{:S(2)}, u32[]{:S(2)}) %collective-permute-start.9) | collective-permute-done | bytes 98336 | tf_op jit(solution)/shard_map/ppermute | solution.py:454
  64.8 2.5 %collective-permute-start.10 = (bf16[3,144,192]{2,1,0:T(8,128)(2,1)S(1)}, bf16[3,144,192]{2,1,0:T(8,128)(2,1)S(1)}, u32[]{:S(2)}, u32[]{:S(2)}) collective-permute-start(bf16[3,144,192]{2,1,0:T(8,128)(2,1)S(1)} %get-tuple-element.71), channel_id=1, source_target_pairs={{0,2},{2,0},{4,6},{6,4},{8,10},{10,8},{12,14},{14,12},{1,3},{3,1},... | collective-permute-start | bytes 497672 | tf_op jit(solution)/shard_map/ppermute | solution.py:458
  67.3 0.7 collective-permute-start.11
  68.0 6.9 %convt0.1.acc_ref = f32[16,128,192]{2,1,0:T(8,128)S(1)} custom-call(bf16[16,128,192]{2,1,0:T(8,128)(2,1)S(1)} %get-tuple-element.67.f_ref, bf16[16,16,192]{2,1,0:T(8,128)(2,1)S(1)} %collective-permute-done.9.lon_ref, f32[2,49,8,128]{3,2,1,0:T(8,128)S(1)} %get-tuple-element.48.k0, f32[2,49,8,128]{3,2,1,0:T(8,128)S(1)} %get-tuple-element.55.k1), custom_call_target="tpu_custom_call" | custom-call | flops 38535168 | bytes 4000000 | tf_op jit(solution)/shard_map/convt0/pallas_call | solution.py:442
  74.9 2.1 %collective-permute-done.10.a_ref = bf16[3,144,192]{2,1,0:T(8,128)(2,1)S(1)} collective-permute-done((bf16[3,144,192]{2,1,0:T(8,128)(2,1)S(1)}, bf16[3,144,192]{2,1,0:T(8,128)(2,1)S(1)}, u32[]{:S(2)}, u32[]{:S(2)}) %collective-permute-start.10) | collective-permute-done | bytes 165920 | tf_op jit(solution)/shard_map/ppermute | solution.py:458
  77.1 0.0 collective-permute-done.11.b_ref
  77.1 2.5 %final.1 = (f32[16,192,128]{2,1,0:T(8,128)S(1)}, f32[16,8,128]{2,1,0:T(8,128)S(1)}) custom-call(f32[2,128]{1,0:T(2,128)S(1)} %copy-done.6, f32[16,128,192]{2,1,0:T(8,128)S(1)} %convt0.1.acc_ref, bf16[3,144,192]{2,1,0:T(8,128)(2,1)S(1)} %collective-permute-done.10.a_ref, bf16[3,144,192]{2,1,0:T(8,128)(2,1)S(1)} %collective-permute-done.11.b_ref, ...), custom_call_target="tpu_custom_call" | custom-call | bytes 4000000 | tf_op jit(solution)/shard_map/final/pallas_call | solution.py:442
  79.6 12.6 %all_to_all.5.tile_ref = f32[16,8,128]{2,1,0:T(8,128)S(1)} all-to-all(f32[16,8,128]{2,1,0:T(8,128)S(1)} %get-tuple-element.76), channel_id=1, replica_groups=mesh['grp'=2,'lat'=8,'lon'=2] {'lat','lon'}, dimensions={0} | all-to-all | bytes 131072 | tf_op jit(solution)/shard_map/all_to_all | solution.py:517
  92.2 1.8 %scale.1 = (f32[16,192,128]{2,1,0:T(8,128)}, f32[1,128]{1,0:T(1,128)}) custom-call(f32[16,8,128]{2,1,0:T(8,128)S(1)} %all_to_all.5.tile_ref, f32[16,192,128]{2,1,0:T(8,128)S(1)} %get-tuple-element.77.w_ref), custom_call_target="tpu_custom_call" | custom-call | tf_op jit(solution)/shard_map/scale/pallas_call | solution.py:518
  (8 shorter events, 0.2 us)
Async XLA Ops:
  0.6 8.1 %copy-start.6 = (f32[2,128]{1,0:T(2,128)S(1)}, f32[2,128]{1,0:T(2,128)}, u32[]{:S(2)}) copy-start(f32[2,128]{1,0:T(2,128)} %constant.2.clone.area_ref) | copy-start | bytes 3076
  0.6 8.0 %copy-start.7 = (f32[2,7,7,192]{3,0,2,1:T(2,128)S(1)}, f32[2,7,7,192]{3,0,2,1:T(2,128)}, u32[]{:S(2)}) copy-start(f32[2,7,7,192]{3,0,2,1:T(2,128)} %param.11) | copy-start | bytes 225796
  0.7 8.1 %copy-start.5 = (f32[2,16,128]{2,1,0:T(8,128)S(1)}, f32[2,16,128]{2,1,0:T(8,128)}, u32[]{:S(2)}) copy-start(f32[2,16,128]{2,1,0:T(8,128)} %inv_ref.1) | copy-start | bytes 49156
  0.7 8.1 %copy-start.2 = (bf16[2,16,128,192]{2,3,1,0:T(8,128)(2,1)S(1)}, bf16[2,16,128,192]{2,3,1,0:T(8,128)(2,1)}, u32[]{:S(2)}) copy-start(bf16[2,16,128,192]{2,3,1,0:T(8,128)(2,1)} %param.16) | copy-start | bytes 4718596
  3.5 1.5 %collective-permute-start = (bf16[16,16,192]{2,1,0:T(8,128)(2,1)S(1)}, bf16[16,16,192]{2,1,0:T(8,128)(2,1)S(1)}, u32[]{:S(2)}, u32[]{:S(2)}) collective-permute-start(bf16[16,16,192]{2,1,0:T(8,128)(2,1)S(1)} %get-tuple-element.42), channel_id=1, source_target_pairs={{0,1},{1,0},{2,3},{3,2},{4,5},{5,4},{6,7},{7,6},{8,9},{9,8},{10,11... | collective-permute-start | bytes 294920 | tf_op jit(solution)/shard_map/ppermute | solution.py:454
  5.1 13.7 %collective-permute-start.1 = (bf16[3,144,192]{2,1,0:T(8,128)(2,1)S(1)}, bf16[3,144,192]{2,1,0:T(8,128)(2,1)S(1)}, u32[]{:S(2)}, u32[]{:S(2)}) collective-permute-start(bf16[3,144,192]{2,1,0:T(8,128)(2,1)S(1)} %get-tuple-element.46), channel_id=1, source_target_pairs={{0,2},{2,0},{4,6},{6,4},{8,10},{10,8},{12,14},{14,12},{1,3},{3,1},... | collective-permute-start | bytes 497672 | tf_op jit(solution)/shard_map/ppermute | solution.py:458
  8.0 10.8 %collective-permute-start.2 = (bf16[3,144,192]{2,1,0:T(8,128)(2,1)S(1)}, bf16[3,144,192]{2,1,0:T(8,128)(2,1)S(1)}, u32[]{:S(2)}, u32[]{:S(2)}) collective-permute-start(bf16[3,144,192]{2,1,0:T(8,128)(2,1)S(1)} %get-tuple-element.47), channel_id=1, source_target_pairs={{2,4},{4,2},{6,8},{8,6},{10,12},{12,10},{3,5},{5,3},{7,9},{9,7},{1... | collective-permute-start | bytes 497672 | tf_op jit(solution)/shard_map/ppermute | solution.py:459
  8.7 10.1 %copy-start = (bf16[2,192,768]{2,1,0:T(8,128)(2,1)S(1)}, bf16[2,192,768]{2,1,0:T(8,128)(2,1)}, u32[]{:S(2)}) copy-start(bf16[2,192,768]{2,1,0:T(8,128)(2,1)} %rest_4_.5) | copy-start | bytes 1769476
  8.7 10.1 %copy-start.1 = (bf16[2,768,192]{1,2,0:T(8,128)(2,1)S(1)}, bf16[2,768,192]{1,2,0:T(8,128)(2,1)}, u32[]{:S(2)}) copy-start(bf16[2,768,192]{1,2,0:T(8,128)(2,1)} %param.14) | copy-start | bytes 1769476
  8.8 10.1 %copy-start.3 = (f32[2,192]{1,0:T(2,128)S(1)}, f32[2,192]{1,0:T(2,128)}, u32[]{:S(2)}) copy-start(f32[2,192]{1,0:T(2,128)} %rest_3_.5) | copy-start | bytes 4612
  8.8 10.1 %copy-start.4 = (f32[2,192]{1,0:T(2,128)S(1)}, f32[2,192]{1,0:T(2,128)}, u32[]{:S(2)}) copy-start(f32[2,192]{1,0:T(2,128)} %rest_6_.5) | copy-start | bytes 4612
  23.3 1.4 %collective-permute-start.3 = (bf16[16,16,192]{2,1,0:T(8,128)(2,1)S(1)}, bf16[16,16,192]{2,1,0:T(8,128)(2,1)S(1)}, u32[]{:S(2)}, u32[]{:S(2)}) collective-permute-start(bf16[16,16,192]{2,1,0:T(8,128)(2,1)S(1)} %get-tuple-element.54), channel_id=1, source_target_pairs={{0,1},{1,0},{2,3},{3,2},{4,5},{5,4},{6,7},{7,6},{8,9},{9,8},{10,11... | collective-permute-start | bytes 294920 | tf_op jit(solution)/shard_map/ppermute | solution.py:454
  24.7 14.1 %collective-permute-start.4 = (bf16[3,144,192]{2,1,0:T(8,128)(2,1)S(1)}, bf16[3,144,192]{2,1,0:T(8,128)(2,1)S(1)}, u32[]{:S(2)}, u32[]{:S(2)}) collective-permute-start(bf16[3,144,192]{2,1,0:T(8,128)(2,1)S(1)} %get-tuple-element.58), channel_id=1, source_target_pairs={{0,2},{2,0},{4,6},{6,4},{8,10},{10,8},{12,14},{14,12},{1,3},{3,1},... | collective-permute-start | bytes 497672 | tf_op jit(solution)/shard_map/ppermute | solution.py:458
  29.1 9.7 %collective-permute-start.5 = (bf16[3,144,192]{2,1,0:T(8,128)(2,1)S(1)}, bf16[3,144,192]{2,1,0:T(8,128)(2,1)S(1)}, u32[]{:S(2)}, u32[]{:S(2)}) collective-permute-start(bf16[3,144,192]{2,1,0:T(8,128)(2,1)S(1)} %get-tuple-element.59), channel_id=1, source_target_pairs={{2,4},{4,2},{6,8},{8,6},{10,12},{12,10},{3,5},{5,3},{7,9},{9,7},{1... | collective-permute-start | bytes 497672 | tf_op jit(solution)/shard_map/ppermute | solution.py:459
  45.6 1.4 %collective-permute-start.6 = (bf16[16,16,192]{2,1,0:T(8,128)(2,1)S(1)}, bf16[16,16,192]{2,1,0:T(8,128)(2,1)S(1)}, u32[]{:S(2)}, u32[]{:S(2)}) collective-permute-start(bf16[16,16,192]{2,1,0:T(8,128)(2,1)S(1)} %get-tuple-element.61), channel_id=1, source_target_pairs={{0,1},{1,0},{2,3},{3,2},{4,5},{5,4},{6,7},{7,6},{8,9},{9,8},{10,11... | collective-permute-start | bytes 294920 | tf_op jit(solution)/shard_map/ppermute | solution.py:454
  47.0 12.3 %collective-permute-start.7 = (bf16[3,144,192]{2,1,0:T(8,128)(2,1)S(1)}, bf16[3,144,192]{2,1,0:T(8,128)(2,1)S(1)}, u32[]{:S(2)}, u32[]{:S(2)}) collective-permute-start(bf16[3,144,192]{2,1,0:T(8,128)(2,1)S(1)} %get-tuple-element.64), channel_id=1, source_target_pairs={{0,2},{2,0},{4,6},{6,4},{8,10},{10,8},{12,14},{14,12},{1,3},{3,1},... | collective-permute-start | bytes 497672 | tf_op jit(solution)/shard_map/ppermute | solution.py:458
  49.6 9.7 %collective-permute-start.8 = (bf16[3,144,192]{2,1,0:T(8,128)(2,1)S(1)}, bf16[3,144,192]{2,1,0:T(8,128)(2,1)S(1)}, u32[]{:S(2)}, u32[]{:S(2)}) collective-permute-start(bf16[3,144,192]{2,1,0:T(8,128)(2,1)S(1)} %get-tuple-element.65), channel_id=1, source_target_pairs={{2,4},{4,2},{6,8},{8,6},{10,12},{12,10},{3,5},{5,3},{7,9},{9,7},{1... | collective-permute-start | bytes 497672 | tf_op jit(solution)/shard_map/ppermute | solution.py:459
  63.3 1.4 %collective-permute-start.9 = (bf16[16,16,192]{2,1,0:T(8,128)(2,1)S(1)}, bf16[16,16,192]{2,1,0:T(8,128)(2,1)S(1)}, u32[]{:S(2)}, u32[]{:S(2)}) collective-permute-start(bf16[16,16,192]{2,1,0:T(8,128)(2,1)S(1)} %get-tuple-element.68), channel_id=1, source_target_pairs={{0,1},{1,0},{2,3},{3,2},{4,5},{5,4},{6,7},{7,6},{8,9},{9,8},{10,11... | collective-permute-start | bytes 294920 | tf_op jit(solution)/shard_map/ppermute | solution.py:454
  64.8 12.3 %collective-permute-start.10 = (bf16[3,144,192]{2,1,0:T(8,128)(2,1)S(1)}, bf16[3,144,192]{2,1,0:T(8,128)(2,1)S(1)}, u32[]{:S(2)}, u32[]{:S(2)}) collective-permute-start(bf16[3,144,192]{2,1,0:T(8,128)(2,1)S(1)} %get-tuple-element.71), channel_id=1, source_target_pairs={{0,2},{2,0},{4,6},{6,4},{8,10},{10,8},{12,14},{14,12},{1,3},{3,1},... | collective-permute-start | bytes 497672 | tf_op jit(solution)/shard_map/ppermute | solution.py:458
  67.3 9.7 %collective-permute-start.11 = (bf16[3,144,192]{2,1,0:T(8,128)(2,1)S(1)}, bf16[3,144,192]{2,1,0:T(8,128)(2,1)S(1)}, u32[]{:S(2)}, u32[]{:S(2)}) collective-permute-start(bf16[3,144,192]{2,1,0:T(8,128)(2,1)S(1)} %get-tuple-element.72), channel_id=1, source_target_pairs={{2,4},{4,2},{6,8},{8,6},{10,12},{12,10},{3,5},{5,3},{7,9},{9,7},{1... | collective-permute-start | bytes 497672 | tf_op jit(solution)/shard_map/ppermute | solution.py:459

commit v3 on v2

--- a/solution.py
+++ b/solution.py
@@ -29,22 +29,22 @@
     return (6 - a) * 7 + (6 - b) if flipped else a * 7 + b
 
 
-def spread_taps(taps_ref, k0, k1, k2):
-    for layer in range(taps_ref.shape[0]):
+def spread_taps(taps_ref, k0, k1):
+    for layer in range(taps_ref.shape[2]):
+
+        def low(index):
+            return jnp.broadcast_to(taps_ref[index // 7, index % 7, layer : layer + 1, :128], (8, 128))
+
+        def high(index):
+            row = taps_ref[index // 7, index % 7, layer : layer + 1, 128:]
+            return jnp.broadcast_to(row, (8, row.shape[1]))
+
         for a in range(7):
-            rows = taps_ref[layer, a]
             for b in range(7):
-                row = rows[b : b + 1, :]
-                k0[layer, a * 7 + b] = jnp.broadcast_to(row[:, :128], (8, 128))
-                high = jnp.broadcast_to(row[:, 128:], (8, row.shape[1] - 128))
-                k1[layer, a * 7 + b] = jnp.concatenate([high, high], axis=1)
-        lane = lax.broadcasted_iota(jnp.int32, (8, 128), 1)
-        for a in range(3):
-            for b in range(7):
+                k0[layer, a * 7 + b] = low(a * 7 + b)
                 for flipped in (0, 1):
-                    low = k1[layer, tap_index(a, b, flipped)]
-                    high = k1[layer, tap_index(6 - a, b, flipped)]
-                    k2[layer, flipped, a * 7 + b] = jnp.where(lane < 64, low, high)
+                    pair = [high(tap_index(a, b, flipped)), high(tap_index(6 - a, b, flipped))]
+                    k1[layer, flipped, a * 7 + b] = jnp.concatenate(pair, axis=1)
 
 
 def fill_row(xs, index, mid, side):
@@ -58,21 +58,22 @@
     rows, cols, _ = out_ref.shape
     half = rows // 2
 
-    @pl.loop(0, half)
-    def _(r):
-        low, high = load_row(r), load_row(r + half)
-        low_side, high_side = lon_ref[r].astype(F32), lon_ref[r + half].astype(F32)
-        fill_row(xs0, r, low[:, :128], low_side[:, :128])
-        fill_row(xs0, r + half, high[:, :128], high_side[:, :128])
+    def fill(q, wide_too):
+        low, high = load_row(q), load_row(rows - 1 - q)
+        low_side, high_side = lon_ref[q].astype(F32), lon_ref[rows - 1 - q].astype(F32)
+        if wide_too:
+            fill_row(xs0, q, low[:, :128], low_side[:, :128])
+            fill_row(xs0, rows - 1 - q, high[:, :128], high_side[:, :128])
         mid = jnp.concatenate([low[:, 128:], high[:, 128:]], axis=1)
         side = jnp.concatenate([low_side[:, 128:], high_side[:, 128:]], axis=1)
-        fill_row(xs1, r + 3, mid, side)
-
-    lane = lax.broadcasted_iota(jnp.int32, (cols + 2 * MARGIN, 128), 1)
-    for q in range(3):
-        above, below = xs1[q + half], xs1[q + 3]
-        xs1[q] = jnp.where(lane < 64, 0.0, pltpu.roll(above, 64, 1))
-        xs1[q + half + 3] = jnp.where(lane < 64, pltpu.roll(below, 64, 1), 0.0)
+        fill_row(xs1, q, mid, side)
+
+    @pl.loop(0, half)
+    def _(q):
+        fill(q, True)
+
+    for q in range(half, half + 3):
+        fill(q, False)
 
     @pl.loop(0, cols // 8)
     def _(j):
@@ -91,17 +92,17 @@
             out_ref[o, pl.ds(base, 8), :128] = acc[o]
         acc = [None] * half
         for b in range(7):
-            taps = [k1[layer, tap_index(a, b, flipped)] for a in range(7)]
-            for q in range(half + 6):
+            taps = [k1[layer, int(flipped), a * 7 + b] for a in range(7)]
+            for q in range(half + 3):
                 x = xs1[q, pl.ds(base + (MARGIN - 3 + b), 8), :]
                 for a in range(7):
-                    o = q - a
+                    o = q + 3 - a
                     if 0 <= o < half:
                         term = taps[a] * x
                         acc[o] = term if acc[o] is None else acc[o] + term
         for o in range(half):
             out_ref[o, pl.ds(base, 8), 128:] = acc[o][:, :64]
-            out_ref[o + half, pl.ds(base, 8), 128:] = acc[o][:, 64:]
+            out_ref[rows - 1 - o, pl.ds(base, 8), 128:] = acc[o][:, 64:]
         if beside is not None:
             beside(j)
 
@@ -109,7 +110,7 @@
 def conv_scratch(rows, cols):
     return [
         pltpu.VMEM((rows, cols + 2 * MARGIN, 128), F32),
-        pltpu.VMEM((rows // 2 + 6, cols + 2 * MARGIN, 128), F32),
+        pltpu.VMEM((rows // 2 + 3, cols + 2 * MARGIN, 128), F32),
     ]
 
 
@@ -121,8 +122,7 @@
 
 
 def first_conv_kernel(
-    area_ref, f_ref, lon_ref, taps_ref, inv_ref, turned_ref, slope_hbm, out_ref, sum_ref, inv_out, normed_out,
-    k0, k1, k2, slope_out, xs0, xs1, sems,
+    area_ref, f_ref, lon_ref, k0, k1, turned_ref, slope_hbm, out_ref, sum_ref, normed_out, slope_out, xs0, xs1, sems
 ):
     rows, cols, _ = f_ref.shape
     start = lax.axis_index("lat") * rows
@@ -132,18 +132,15 @@
     ]
     for fetch in fetches:
         fetch.start()
-    spread_taps(taps_ref, k0, k1, k2)
     one = lax.broadcasted_iota(jnp.int32, (cols, cols), 0) == lax.broadcasted_iota(jnp.int32, (cols, cols), 1)
     eye = jnp.where(one, 1.0, 0.0).astype(BF16)
 
     def turn_row(r):
         x = f_ref[r]
         sum_ref[...] += area_ref[0, start + r] * jnp.sum(x * x, axis=0, keepdims=True)
-        for layer in range(inv_ref.shape[0]):
+        for layer in range(turned_ref.shape[0]):
             turned = lax.dot_general(eye, turned_ref[layer, r], ACROSS, preferred_element_type=F32)
             normed_out[layer, r] = turned.astype(BF16)
-            inv = inv_ref[layer, pl.ds(r, 1), :]
-            inv_out[layer, r] = jnp.transpose(jnp.broadcast_to(inv, (128, cols)))
 
     def load_row(r):
         return f_ref[r].astype(BF16).astype(F32)
@@ -181,7 +178,7 @@
         put(h1, e, jnp.concatenate([up, down], axis=1))
 
 
-def conv_halo(h0, h1, acc_ref, k0, k2, layer, edge, flipped):
+def conv_halo(h0, h1, acc_ref, k0, k1, layer, edge, flipped):
     rows, cols, _ = acc_ref.shape
     unroll = 2
 
@@ -208,7 +205,7 @@
                 edge[o, pl.ds(base, 8), :128] = acc_ref[own, pl.ds(base, 8), :128] + acc[i][o]
         acc = [[None] * 3 for _ in bases]
         for b in range(7):
-            taps = [k2[layer, int(flipped), a * 7 + b] for a in range(3)]
+            taps = [k1[layer, int(flipped), a * 7 + b] for a in range(3)]
             for i, base in enumerate(bases):
                 for e in range(3):
                     both = h1[e, pl.ds(base + (MARGIN - 3 + b), 8), :]
@@ -302,7 +299,7 @@
     ]
 
 
-def tangent_kernel(layer, last, area_ref, acc_ref, a_ref, b_ref, k0, k2, t_ref, *rest):
+def tangent_kernel(layer, last, area_ref, acc_ref, a_ref, b_ref, k0, k1, t_ref, *rest):
     net, rest = rest[:7], rest[7:]
     rows, cols, chans = acc_ref.shape
     lat = lax.axis_index("lat")
@@ -312,7 +309,7 @@
     else:
         t_out, lon_ref, sa_ref, sb_ref, h0, h1, edge = rest
     place_halo(lat % 2, a_ref, b_ref, h0, h1)
-    conv_halo(h0, h1, acc_ref, k0, k2, layer, edge, False)
+    conv_halo(h0, h1, acc_ref, k0, k1, layer, edge, False)
 
     def work(block, y):
         operands = net_operands(layer, block, net)
@@ -334,11 +331,11 @@
     send_rows(lat % 2, db_ref if last else t_out, lon_ref, sa_ref, sb_ref)
 
 
-def adjoint_kernel(layer, acc_ref, a_ref, b_ref, k0, k2, g_ref, *rest):
+def adjoint_kernel(layer, acc_ref, a_ref, b_ref, k0, k1, g_ref, *rest):
     net, (g_out, db_ref, lon_ref, sa_ref, sb_ref, h0, h1, edge) = rest[:7], rest[7:]
     parity = lax.axis_index("lat") % 2
     place_halo(parity, a_ref, b_ref, h0, h1)
-    conv_halo(h0, h1, acc_ref, k0, k2, layer + 1, edge, True)
+    conv_halo(h0, h1, acc_ref, k0, k1, layer + 1, edge, True)
 
     def work(block, y):
         g = block.get(g_ref) + y
@@ -350,12 +347,12 @@
 
 
 def final_kernel(
-    area_ref, acc_ref, a_ref, b_ref, k0, k2, g_ref, vv_ref, uu_ref, w_ref, tile_ref, h0, h1, edge, ww
+    area_ref, acc_ref, a_ref, b_ref, k0, k1, g_ref, vv_ref, uu_ref, w_ref, tile_ref, h0, h1, edge, ww
 ):
     rows = acc_ref.shape[0]
     lat = lax.axis_index("lat")
     place_halo(lat % 2, a_ref, b_ref, h0, h1)
-    conv_halo(h0, h1, acc_ref, k0, k2, 0, edge, True)
+    conv_halo(h0, h1, acc_ref, k0, k1, 0, edge, True)
     ww[...] = jnp.zeros_like(ww)
 
     def row(r, y):
@@ -371,7 +368,7 @@
     for r in range(3, rows - 3):
         row(r, acc_ref[r])
 
-    which = lax.broadcasted_iota(jnp.int32, (8, 128), 0)
+    which = lax.broadcasted_iota(jnp.int32, (1, 128), 1)
     vv, uu, wv = (jnp.sum(ref[...]) for ref in (vv_ref, uu_ref, ww))
     tile = jnp.where(which == 0, vv, jnp.where(which == 1, uu, jnp.where(which == 2, wv, 0.0)))
     for i in range(tile_ref.shape[0]):
@@ -380,7 +377,7 @@
 
 def scale_kernel(total, tile_ref, w_ref, out_hbm, growth_ref, scaled, sems):
     sums = jnp.sum(tile_ref[...], axis=0) * (1.0 / total)
-    vv, uu, ww = sums[0:1, :], sums[1:2, :], sums[2:3, :]
+    vv, uu, ww = (jnp.broadcast_to(sums[:, i : i + 1], (1, 128)) for i in range(3))
     growth_ref[...] = jnp.sqrt(uu / (vv + 1e-06))
     factor = 1.0 / jnp.sqrt(ww + 1e-06)
     copies = []
@@ -402,11 +399,24 @@
         sb_ref[e, cols:, :] = lon_ref[parity * (rows - 3) + e]
 
 
-def edges_kernel(turned_hbm, t_ref, lon_ref, sa_ref, sb_ref, turned, sems):
+def edges_kernel(
+    turned_hbm, taps_hbm, inv_hbm, t_ref, lon_ref, sa_ref, sb_ref, k0, k1, inv_out, turned, taps_ref, inv_ref, sems
+):
     rows = turned.shape[0]
     copies = [pltpu.make_async_copy(turned_hbm.at[r], turned.at[r], sems.at[r]) for r in range(rows)]
-    for copy in copies:
+    small = [
+        pltpu.make_async_copy(inv_hbm, inv_ref, sems.at[rows]),
+        pltpu.make_async_copy(taps_hbm, taps_ref, sems.at[rows + 1]),
+    ]
+    for copy in small + copies:
         copy.start()
+    for copy in small:
+        copy.wait()
+    spread_taps(taps_ref, k0, k1)
+    for layer in range(inv_ref.shape[0]):
+        for r in range(rows):
+            inv = jnp.broadcast_to(inv_ref[layer, r : r + 1, :], (128, inv_ref.shape[2]))
+            inv_out[layer, r] = jnp.transpose(inv)
     for r, copy in enumerate(copies):
         copy.wait()
         t_ref[r] = jnp.transpose(turned[r])
@@ -464,20 +474,25 @@
     kscr = conv_scratch(rows, cols)
     hscr = halo_scratch(cols, chans)
 
-    tangent, lon, send_a, send_b = call(
-        edges_kernel, [full32, lon_shape, send_shape, send_shape], [IN_HBM], (jnp.transpose(perturb, (0, 2, 1)),),
-        [pltpu.VMEM((rows, chans, cols), F32), pltpu.SemaphoreType.DMA((rows,))], name="edges",
+    tangent, lon, send_a, send_b, k0, k1, inv_cells = call(
+        edges_kernel,
+        [
+            full32, lon_shape, send_shape, send_shape, VMEM((layers, 49, 8, 128), F32),
+            VMEM((layers, 2, 49, 8, 128), F32), VMEM((layers, rows, cols, 128), F32),
+        ],
+        [IN_HBM] * 3, (jnp.transpose(perturb, (0, 2, 1)), jnp.transpose(kernels, (1, 2, 0, 3)), inv_std),
+        [
+            pltpu.VMEM((rows, chans, cols), F32), pltpu.VMEM((7, 7, layers, chans), F32),
+            pltpu.VMEM(inv_std.shape, F32), pltpu.SemaphoreType.DMA((rows + 2,)),
+        ],
+        name="edges",
     )
     side, halo_a, halo_b = exchange(lon, send_a, send_b)
-    acc, vv, inv_cells, normed_cells, k0, k1, k2, slope_cells = call(
+    acc, vv, normed_cells, slope_cells = call(
         first_conv_kernel,
-        [
-            full32, sums, VMEM((layers, rows, cols, 128), F32), VMEM((layers, rows, cols, chans), BF16),
-            VMEM((layers, 49, 8, 128), F32), VMEM((layers, 49, 8, 128), F32), VMEM((layers, 2, 21, 8, 128), F32),
-            VMEM(slope.shape, BF16),
-        ],
+        [full32, sums, VMEM((layers, rows, cols, chans), BF16), VMEM(slope.shape, BF16)],
         [IN_SMEM] + [IN_VMEM] * 5 + [IN_HBM],
-        (area, tangent, side, kernels, inv_std, jnp.transpose(normed, (0, 1, 3, 2)), slope),
+        (area, tangent, side, k0, k1, jnp.transpose(normed, (0, 1, 3, 2)), slope),
         kscr + [pltpu.SemaphoreType.DMA((layers,))], conv_flops, "conv_first",
     )
     net = (normed_cells, inv_cells, slope_cells, gains, w_in, across_cells, scales)
@@ -487,7 +502,7 @@
         outs = outs + [lon_shape, send_shape, send_shape]
         got = call(
             functools.partial(tangent_kernel, layer, last), outs, [IN_SMEM] + [IN_VMEM] * 13,
-            (area, acc, halo_a, halo_b, k0, k2, tangent) + net, hscr, net_flops, f"tangent{layer}",
+            (area, acc, halo_a, halo_b, k0, k1, tangent) + net, hscr, net_flops, f"tangent{layer}",
         )
         side, halo_a, halo_b = exchange(*got[-3:])
         if last:
@@ -506,13 +521,13 @@
         if layer > 0:
             grad, back, lon, send_a, send_b = call(
                 functools.partial(adjoint_kernel, layer - 1), [full32, full16, lon_shape, send_shape, send_shape],
-                [IN_VMEM] * 13, (acc, halo_a, halo_b, k0, k2, grad) + net, hscr, net_flops, f"adjoint{layer - 1}",
+                [IN_VMEM] * 13, (acc, halo_a, halo_b, k0, k1, grad) + net, hscr, net_flops, f"adjoint{layer - 1}",
             )
             side, halo_a, halo_b = exchange(lon, send_a, send_b)
     members = lat_size * lon_size
     w, tile = call(
-        final_kernel, [VMEM((rows, chans, cols), F32), VMEM((members, 8, 128), F32)], [IN_SMEM] + [IN_VMEM] * 8,
-        (area, acc, halo_a, halo_b, k0, k2, grad, vv, uu), hscr + [pltpu.VMEM((1, chans), F32)], 0, "final",
+        final_kernel, [VMEM((rows, chans, cols), F32), VMEM((members, 1, 128), F32)], [IN_SMEM] + [IN_VMEM] * 8,
+        (area, acc, halo_a, halo_b, k0, k1, grad, vv, uu), hscr + [pltpu.VMEM((1, chans), F32)], 0, "final",
     )
     tile = lax.all_to_all(tile, ("lat", "lon"), 0, 0, tiled=True)
     new_vec, growth = pl.pallas_call(

time: 94.4 us -> 93.3 us (0.988)
  waiting for transfers between devices: 11.2 us -> 13 us
  Pallas kernels: 53.3 us -> 51.7 us
    ppermute x4, waiting for transfers between devices: 6.24 us -> 7.95 us  [exchange(): halo_a = lax.ppermute(send_a, 'lat', swap_a)]
    pallas_call x13, Pallas kernels: 51.5 us -> 49.8 us  [call(): pl.pallas_call(kernel, out_shape=out_shape, in_specs=in_specs, out_specs=...]
  transfers between devices with their start and end apart: 12 -> 12, of which waited for: 7 -> 8; matrix products, arithmetic and copies ran while one was open for 0% -> 0% of each run, Pallas kernels for 33% -> 30%
where the time goes in v3:
time: 93.3 us; the launch traced here: 93.1 us
  Pallas kernels  51.7 us (55%)
  starting transfers between devices  15.3 us (16%)
  waiting for transfers between devices  13 us (14%)
  blocking collectives  12.1 us (13%)
  between operations  0.99 us (1%)
    pallas_call x13, Pallas kernels, call(): pl.pallas_call(kernel, out_shape=out_shape, in_specs=in_specs, out_specs=...  49.8 us
    all_to_all x1, blocking collectives, on_device(): tile = lax.all_to_all(tile, ('lat', 'lon'), 0, 0, tiled=True)  12.1 us
    ppermute x4, starting transfers between devices, exchange(): halo_a = lax.ppermute(send_a, 'lat', swap_a)  11.8 us
    ppermute x4, waiting for transfers between devices, exchange(): halo_a = lax.ppermute(send_a, 'lat', swap_a)  7.95 us
    ppermute x4, waiting for transfers between devices, exchange(): side = lax.ppermute(lon, 'lon', swap_lon)  4.99 us
    ppermute x4, starting transfers between devices, exchange(): halo_b = lax.ppermute(send_b, 'lat', swap_b)  2.83 us
    pallas_call x1, Pallas kernels, on_device(): pl.pallas_call(functools.partial(scale_kernel, total), out_shape=[jax.Sha...  1.88 us
  transfers between devices with their start and end apart: 12, of which 8 were waited for; matrix products, arithmetic and copies ran while one was open for 0% of the time, Pallas kernels for 30%

profile of v3, /device:TPU:0, one launch (start us, length us, event | category | flops | bytes accessed | tf_op | source)
XLA Modules:
  0.0 93.1 jit_solution(12089107495581331267)
XLA Ops:
  0.6 0.0 copy-start.5
  0.6 0.0 copy-start.2
  0.7 3.7 %edges.1 = (f32[16,128,192]{2,1,0:T(8,128)S(1)}, bf16[16,16,192]{2,1,0:T(8,128)(2,1)S(1)}, bf16[3,144,192]{2,1,0:T(8,128)(2,1)S(1)}, bf16[3,144,192]{2,1,0:T(8,1...) custom-call(f32[16,192,128]{2,1,0:T(8,128)} %bitcast.11, ...), custom_call_target="tpu_custom_call" | custom-call | bytes 4000000 | tf_op jit(solution)/shard_map/edges/pallas_call | solution.py:452
  4.4 0.5 collective-permute-start
  4.9 1.0 %collective-permute-done.lon_ref = bf16[16,16,192]{2,1,0:T(8,128)(2,1)S(1)} collective-permute-done((bf16[16,16,192]{2,1,0:T(8,128)(2,1)S(1)}, bf16[16,16,192]{2,1,0:T(8,128)(2,1)S(1)}, u32[]{:S(2)}, u32[]{:S(2)}) %collective-permute-start) | collective-permute-done | bytes 98336 | tf_op jit(solution)/shard_map/ppermute | solution.py:464
  5.9 2.9 %collective-permute-start.1 = (bf16[3,144,192]{2,1,0:T(8,128)(2,1)S(1)}, bf16[3,144,192]{2,1,0:T(8,128)(2,1)S(1)}, u32[]{:S(2)}, u32[]{:S(2)}) collective-permute-start(bf16[3,144,192]{2,1,0:T(8,128)(2,1)S(1)} %get-tuple-element.47), channel_id=1, source_target_pairs={{0,2},{2,0},{4,6},{6,4},{8,10},{10,8},{12,14},{14,12},{1,3},{3,1},... | collective-permute-start | bytes 497672 | tf_op jit(solution)/shard_map/ppermute | solution.py:468
  8.9 0.7 collective-permute-start.2
  9.5 0.0 copy-done.5
  9.5 0.0 copy-done.2
  9.6 0.0 copy-start
  9.6 0.0 copy-start.1
  9.6 0.0 copy-start.3
  9.6 0.0 copy-start.4
  9.6 8.4 %conv_first.1 = (f32[16,128,192]{2,1,0:T(8,128)S(1)}, f32[1,192]{1,0:T(1,128)S(1)}, bf16[2,16,128,192]{3,2,1,0:T(8,128)(2,1)S(1)}, bf16[2,16,128,768]{3,2,1,0:T(8,128)(2,1)S(1)}) custom-call(f32[2,128]{1,0:T(2,128)S(1)} %copy-done.5, f32[16,128,192]{2,1,0:T(8,128)S(1)} %get-tuple-element.40.f_ref.t_ref, ...), custom_call_target="tpu_custom_call" | custom-call | flops 38535168 | bytes 4000000 | tf_op jit(solution)/shard_map/conv_first/pallas_call | solution.py:452
  18.0 0.6 collective-permute-done.1.a_ref
  18.6 0.0 collective-permute-done.2.b_ref
  18.6 0.0 copy-done
  18.6 0.0 copy-done.1
  18.6 0.0 copy-done.3
  18.6 0.0 copy-done.4
  18.6 4.5 %tangent0.1 = (f32[16,128,192]{2,1,0:T(8,128)S(1)}, bf16[16,16,192]{2,1,0:T(8,128)(2,1)S(1)}, bf16[3,144,192]{2,1,0:T(8,128)(2,1)S(1)}, bf16[3,144,192]{2,1,0:T(8,128)(2,1)S(1)}) custom-call(f32[2,128]{1,0:T(2,128)S(1)} %copy-done.5, f32[16,128,192]{2,1,0:T(8,128)S(1)} %get-tuple-element.44.acc_ref, bf16[3,144,192]{2,1,0:T(8,128)(2,1)S(1)} %collective-permute-done.1.a_ref, ...), custom_call_target="tpu_custom_call" | custom-call | flops 1207959552 | bytes 4000000 | tf_op jit(solution)/shard_map/tangent0/pallas_call | solution.py:452
  23.1 0.1 collective-permute-start.3
  23.2 1.3 %collective-permute-done.3.lon_ref = bf16[16,16,192]{2,1,0:T(8,128)(2,1)S(1)} collective-permute-done((bf16[16,16,192]{2,1,0:T(8,128)(2,1)S(1)}, bf16[16,16,192]{2,1,0:T(8,128)(2,1)S(1)}, u32[]{:S(2)}, u32[]{:S(2)}) %collective-permute-start.3) | collective-permute-done | bytes 98336 | tf_op jit(solution)/shard_map/ppermute | solution.py:464
  24.6 3.8 %collective-permute-start.4 = (bf16[3,144,192]{2,1,0:T(8,128)(2,1)S(1)}, bf16[3,144,192]{2,1,0:T(8,128)(2,1)S(1)}, u32[]{:S(2)}, u32[]{:S(2)}) collective-permute-start(bf16[3,144,192]{2,1,0:T(8,128)(2,1)S(1)} %get-tuple-element.56), channel_id=1, source_target_pairs={{0,2},{2,0},{4,6},{6,4},{8,10},{10,8},{12,14},{14,12},{1,3},{3,1},... | collective-permute-start | bytes 497672 | tf_op jit(solution)/shard_map/ppermute | solution.py:468
  28.3 0.7 collective-permute-start.5
  29.0 6.6 %conv1.1.acc_ref = f32[16,128,192]{2,1,0:T(8,128)S(1)} custom-call(f32[16,128,192]{2,1,0:T(8,128)S(1)} %get-tuple-element.52.f_ref.t_ref, bf16[16,16,192]{2,1,0:T(8,128)(2,1)S(1)} %collective-permute-done.3.lon_ref, f32[2,49,8,128]{3,2,1,0:T(8,128)S(1)} %get-tuple-element.42.k0, f32[2,2,49,8,128]{4,3,2,1,0:T(8,128)S(1)} %get-tuple-element.43.k1), custom_call_target="tpu_custom_call" | custom-call | flops 38535168 | bytes 4000000 | tf_op jit(solution)/shard_map/conv1/pallas_call | solution.py:452
  35.6 2.5 %collective-permute-done.4.a_ref = bf16[3,144,192]{2,1,0:T(8,128)(2,1)S(1)} collective-permute-done((bf16[3,144,192]{2,1,0:T(8,128)(2,1)S(1)}, bf16[3,144,192]{2,1,0:T(8,128)(2,1)S(1)}, u32[]{:S(2)}, u32[]{:S(2)}) %collective-permute-start.4) | collective-permute-done | bytes 165920 | tf_op jit(solution)/shard_map/ppermute | solution.py:468
  38.1 0.0 collective-permute-done.5.b_ref
  38.1 6.9 %tangent1.1 = (f32[16,128,192]{2,1,0:T(8,128)S(1)}, bf16[16,128,192]{2,1,0:T(8,128)(2,1)S(1)}, f32[1,192]{1,0:T(1,128)S(1)}, bf16[16,16,192]{2,1,0:T(8,128)(2,1)...) custom-call(f32[2,128]{1,0:T(2,128)S(1)} %copy-done.5, f32[16,128,192]{2,1,0:T(8,128)S(1)} %conv1.1.acc_ref, ...), custom_call_target="tpu_custom_call" | custom-call | flops 1207959552 | bytes 4000000 | tf_op jit(solution)/shard_map/tangent1/pallas_call | solution.py:452
  44.9 0.1 collective-permute-start.6
  45.0 1.3 %collective-permute-done.6.lon_ref = bf16[16,16,192]{2,1,0:T(8,128)(2,1)S(1)} collective-permute-done((bf16[16,16,192]{2,1,0:T(8,128)(2,1)S(1)}, bf16[16,16,192]{2,1,0:T(8,128)(2,1)S(1)}, u32[]{:S(2)}, u32[]{:S(2)}) %collective-permute-start.6) | collective-permute-done | bytes 98336 | tf_op jit(solution)/shard_map/ppermute | solution.py:464
  46.4 2.5 %collective-permute-start.7 = (bf16[3,144,192]{2,1,0:T(8,128)(2,1)S(1)}, bf16[3,144,192]{2,1,0:T(8,128)(2,1)S(1)}, u32[]{:S(2)}, u32[]{:S(2)}) collective-permute-start(bf16[3,144,192]{2,1,0:T(8,128)(2,1)S(1)} %get-tuple-element.62), channel_id=1, source_target_pairs={{0,2},{2,0},{4,6},{6,4},{8,10},{10,8},{12,14},{14,12},{1,3},{3,1},... | collective-permute-start | bytes 497672 | tf_op jit(solution)/shard_map/ppermute | solution.py:468
  48.9 0.8 collective-permute-start.8
  49.8 6.5 %convt1.1.acc_ref = f32[16,128,192]{2,1,0:T(8,128)S(1)} custom-call(bf16[16,128,192]{2,1,0:T(8,128)(2,1)S(1)} %get-tuple-element.58.f_ref, bf16[16,16,192]{2,1,0:T(8,128)(2,1)S(1)} %collective-permute-done.6.lon_ref, f32[2,49,8,128]{3,2,1,0:T(8,128)S(1)} %get-tuple-element.42.k0, f32[2,2,49,8,128]{4,3,2,1,0:T(8,128)S(1)} %get-tuple-element.43.k1), custom_call_target="tpu_custom_call" | custom-call | flops 38535168 | bytes 4000000 | tf_op jit(solution)/shard_map/convt1/pallas_call | solution.py:452
  56.3 2.4 %collective-permute-done.7.a_ref = bf16[3,144,192]{2,1,0:T(8,128)(2,1)S(1)} collective-permute-done((bf16[3,144,192]{2,1,0:T(8,128)(2,1)S(1)}, bf16[3,144,192]{2,1,0:T(8,128)(2,1)S(1)}, u32[]{:S(2)}, u32[]{:S(2)}) %collective-permute-start.7) | collective-permute-done | bytes 165920 | tf_op jit(solution)/shard_map/ppermute | solution.py:468
  58.7 0.0 collective-permute-done.8.b_ref
  58.7 4.0 %adjoint0.1 = (f32[16,128,192]{2,1,0:T(8,128)S(1)}, bf16[16,128,192]{2,1,0:T(8,128)(2,1)S(1)}, bf16[16,16,192]{2,1,0:T(8,128)(2,1)S(1)}, bf16[3,144,192]{2,1,0:T(8,128)(2,1)S(1)}, bf16[3,144,192]{2,1,0:T(8,128)(2,1)S(1)}) custom-call(f32[16,128,192]{2,1,0:T(8,128)S(1)} %convt1.1.acc_ref, bf16[3,144,192]{2,1,0:T(8,128)(2,1)S(1)} %collective-permute-done.7.a_ref, ...), custom_call_target="tpu_custom_call" | custom-call | flops 1207959552 | bytes 4000000 | tf_op jit(solution)/shard_map/adjoint0/pallas_call | solution.py:452
  62.7 0.1 collective-permute-start.9
  62.8 1.3 %collective-permute-done.9.lon_ref = bf16[16,16,192]{2,1,0:T(8,128)(2,1)S(1)} collective-permute-done((bf16[16,16,192]{2,1,0:T(8,128)(2,1)S(1)}, bf16[16,16,192]{2,1,0:T(8,128)(2,1)S(1)}, u32[]{:S(2)}, u32[]{:S(2)}) %collective-permute-start.9) | collective-permute-done | bytes 98336 | tf_op jit(solution)/shard_map/ppermute | solution.py:464
  64.1 2.5 %collective-permute-start.10 = (bf16[3,144,192]{2,1,0:T(8,128)(2,1)S(1)}, bf16[3,144,192]{2,1,0:T(8,128)(2,1)S(1)}, u32[]{:S(2)}, u32[]{:S(2)}) collective-permute-start(bf16[3,144,192]{2,1,0:T(8,128)(2,1)S(1)} %get-tuple-element.69), channel_id=1, source_target_pairs={{0,2},{2,0},{4,6},{6,4},{8,10},{10,8},{12,14},{14,12},{1,3},{3,1},... | collective-permute-start | bytes 497672 | tf_op jit(solution)/shard_map/ppermute | solution.py:468
  66.7 0.7 collective-permute-start.11
  67.4 6.6 %convt0.1.acc_ref = f32[16,128,192]{2,1,0:T(8,128)S(1)} custom-call(bf16[16,128,192]{2,1,0:T(8,128)(2,1)S(1)} %get-tuple-element.65.f_ref, bf16[16,16,192]{2,1,0:T(8,128)(2,1)S(1)} %collective-permute-done.9.lon_ref, f32[2,49,8,128]{3,2,1,0:T(8,128)S(1)} %get-tuple-element.42.k0, f32[2,2,49,8,128]{4,3,2,1,0:T(8,128)S(1)} %get-tuple-element.43.k1), custom_call_target="tpu_custom_call" | custom-call | flops 38535168 | bytes 4000000 | tf_op jit(solution)/shard_map/convt0/pallas_call | solution.py:452
  73.9 2.5 %collective-permute-done.10.a_ref = bf16[3,144,192]{2,1,0:T(8,128)(2,1)S(1)} collective-permute-done((bf16[3,144,192]{2,1,0:T(8,128)(2,1)S(1)}, bf16[3,144,192]{2,1,0:T(8,128)(2,1)S(1)}, u32[]{:S(2)}, u32[]{:S(2)}) %collective-permute-start.10) | collective-permute-done | bytes 165920 | tf_op jit(solution)/shard_map/ppermute | solution.py:468
  76.4 0.0 collective-permute-done.11.b_ref
  76.4 2.5 %final.1 = (f32[16,192,128]{2,1,0:T(8,128)S(1)}, f32[16,1,128]{2,1,0:T(1,128)S(1)}) custom-call(f32[2,128]{1,0:T(2,128)S(1)} %copy-done.5, f32[16,128,192]{2,1,0:T(8,128)S(1)} %convt0.1.acc_ref, bf16[3,144,192]{2,1,0:T(8,128)(2,1)S(1)} %collective-permute-done.10.a_ref, bf16[3,144,192]{2,1,0:T(8,128)(2,1)S(1)} %collective-permute-done.11.b_ref, ...), custom_call_target="tpu_custom_call" | custom-call | bytes 4000000 | tf_op jit(solution)/shard_map/final/pallas_call | solution.py:452
  79.0 12.1 %all_to_all.5.tile_ref = f32[16,1,128]{2,1,0:T(1,128)S(1)} all-to-all(f32[16,1,128]{2,1,0:T(1,128)S(1)} %get-tuple-element.74), channel_id=1, replica_groups=mesh['grp'=2,'lat'=8,'lon'=2] {'lat','lon'}, dimensions={0} | all-to-all | bytes 16384 | tf_op jit(solution)/shard_map/all_to_all | solution.py:532
  91.1 1.9 %scale.1 = (f32[16,192,128]{2,1,0:T(8,128)}, f32[1,128]{1,0:T(1,128)}) custom-call(f32[16,1,128]{2,1,0:T(1,128)S(1)} %all_to_all.5.tile_ref, f32[16,192,128]{2,1,0:T(8,128)S(1)} %get-tuple-element.75.w_ref), custom_call_target="tpu_custom_call" | custom-call | tf_op jit(solution)/shard_map/scale/pallas_call | solution.py:533
  (4 shorter events, 0.1 us)
Async XLA Ops:
  0.6 8.9 %copy-start.5 = (f32[2,128]{1,0:T(2,128)S(1)}, f32[2,128]{1,0:T(2,128)}, u32[]{:S(2)}) copy-start(f32[2,128]{1,0:T(2,128)} %constant.2.clone.area_ref) | copy-start | bytes 3076
  0.6 8.9 %copy-start.2 = (bf16[2,16,128,192]{2,3,1,0:T(8,128)(2,1)S(1)}, bf16[2,16,128,192]{2,3,1,0:T(8,128)(2,1)}, u32[]{:S(2)}) copy-start(bf16[2,16,128,192]{2,3,1,0:T(8,128)(2,1)} %param.16) | copy-start | bytes 4718596
  4.4 1.5 %collective-permute-start = (bf16[16,16,192]{2,1,0:T(8,128)(2,1)S(1)}, bf16[16,16,192]{2,1,0:T(8,128)(2,1)S(1)}, u32[]{:S(2)}, u32[]{:S(2)}) collective-permute-start(bf16[16,16,192]{2,1,0:T(8,128)(2,1)S(1)} %get-tuple-element.41), channel_id=1, source_target_pairs={{0,1},{1,0},{2,3},{3,2},{4,5},{5,4},{6,7},{7,6},{8,9},{9,8},{10,11... | collective-permute-start | bytes 294920 | tf_op jit(solution)/shard_map/ppermute | solution.py:464
  5.9 12.7 %collective-permute-start.1 = (bf16[3,144,192]{2,1,0:T(8,128)(2,1)S(1)}, bf16[3,144,192]{2,1,0:T(8,128)(2,1)S(1)}, u32[]{:S(2)}, u32[]{:S(2)}) collective-permute-start(bf16[3,144,192]{2,1,0:T(8,128)(2,1)S(1)} %get-tuple-element.47), channel_id=1, source_target_pairs={{0,2},{2,0},{4,6},{6,4},{8,10},{10,8},{12,14},{14,12},{1,3},{3,1},... | collective-permute-start | bytes 497672 | tf_op jit(solution)/shard_map/ppermute | solution.py:468
  8.9 9.7 %collective-permute-start.2 = (bf16[3,144,192]{2,1,0:T(8,128)(2,1)S(1)}, bf16[3,144,192]{2,1,0:T(8,128)(2,1)S(1)}, u32[]{:S(2)}, u32[]{:S(2)}) collective-permute-start(bf16[3,144,192]{2,1,0:T(8,128)(2,1)S(1)} %get-tuple-element.48), channel_id=1, source_target_pairs={{2,4},{4,2},{6,8},{8,6},{10,12},{12,10},{3,5},{5,3},{7,9},{9,7},{1... | collective-permute-start | bytes 497672 | tf_op jit(solution)/shard_map/ppermute | solution.py:469
  9.6 9.1 %copy-start = (bf16[2,192,768]{2,1,0:T(8,128)(2,1)S(1)}, bf16[2,192,768]{2,1,0:T(8,128)(2,1)}, u32[]{:S(2)}) copy-start(bf16[2,192,768]{2,1,0:T(8,128)(2,1)} %rest_4_.5) | copy-start | bytes 1769476
  9.6 9.0 %copy-start.1 = (bf16[2,768,192]{1,2,0:T(8,128)(2,1)S(1)}, bf16[2,768,192]{1,2,0:T(8,128)(2,1)}, u32[]{:S(2)}) copy-start(bf16[2,768,192]{1,2,0:T(8,128)(2,1)} %param.14) | copy-start | bytes 1769476
  9.6 9.0 %copy-start.3 = (f32[2,192]{1,0:T(2,128)S(1)}, f32[2,192]{1,0:T(2,128)}, u32[]{:S(2)}) copy-start(f32[2,192]{1,0:T(2,128)} %rest_3_.5) | copy-start | bytes 4612
  9.6 9.0 %copy-start.4 = (f32[2,192]{1,0:T(2,128)S(1)}, f32[2,192]{1,0:T(2,128)}, u32[]{:S(2)}) copy-start(f32[2,192]{1,0:T(2,128)} %rest_6_.5) | copy-start | bytes 4612
  23.1 1.4 %collective-permute-start.3 = (bf16[16,16,192]{2,1,0:T(8,128)(2,1)S(1)}, bf16[16,16,192]{2,1,0:T(8,128)(2,1)S(1)}, u32[]{:S(2)}, u32[]{:S(2)}) collective-permute-start(bf16[16,16,192]{2,1,0:T(8,128)(2,1)S(1)} %get-tuple-element.53), channel_id=1, source_target_pairs={{0,1},{1,0},{2,3},{3,2},{4,5},{5,4},{6,7},{7,6},{8,9},{9,8},{10,11... | collective-permute-start | bytes 294920 | tf_op jit(solution)/shard_map/ppermute | solution.py:464
  24.6 13.5 %collective-permute-start.4 = (bf16[3,144,192]{2,1,0:T(8,128)(2,1)S(1)}, bf16[3,144,192]{2,1,0:T(8,128)(2,1)S(1)}, u32[]{:S(2)}, u32[]{:S(2)}) collective-permute-start(bf16[3,144,192]{2,1,0:T(8,128)(2,1)S(1)} %get-tuple-element.56), channel_id=1, source_target_pairs={{0,2},{2,0},{4,6},{6,4},{8,10},{10,8},{12,14},{14,12},{1,3},{3,1},... | collective-permute-start | bytes 497672 | tf_op jit(solution)/shard_map/ppermute | solution.py:468
  28.3 9.7 %collective-permute-start.5 = (bf16[3,144,192]{2,1,0:T(8,128)(2,1)S(1)}, bf16[3,144,192]{2,1,0:T(8,128)(2,1)S(1)}, u32[]{:S(2)}, u32[]{:S(2)}) collective-permute-start(bf16[3,144,192]{2,1,0:T(8,128)(2,1)S(1)} %get-tuple-element.57), channel_id=1, source_target_pairs={{2,4},{4,2},{6,8},{8,6},{10,12},{12,10},{3,5},{5,3},{7,9},{9,7},{1... | collective-permute-start | bytes 497672 | tf_op jit(solution)/shard_map/ppermute | solution.py:469
  44.9 1.4 %collective-permute-start.6 = (bf16[16,16,192]{2,1,0:T(8,128)(2,1)S(1)}, bf16[16,16,192]{2,1,0:T(8,128)(2,1)S(1)}, u32[]{:S(2)}, u32[]{:S(2)}) collective-permute-start(bf16[16,16,192]{2,1,0:T(8,128)(2,1)S(1)} %get-tuple-element.59), channel_id=1, source_target_pairs={{0,1},{1,0},{2,3},{3,2},{4,5},{5,4},{6,7},{7,6},{8,9},{9,8},{10,11... | collective-permute-start | bytes 294920 | tf_op jit(solution)/shard_map/ppermute | solution.py:464
  46.4 12.3 %collective-permute-start.7 = (bf16[3,144,192]{2,1,0:T(8,128)(2,1)S(1)}, bf16[3,144,192]{2,1,0:T(8,128)(2,1)S(1)}, u32[]{:S(2)}, u32[]{:S(2)}) collective-permute-start(bf16[3,144,192]{2,1,0:T(8,128)(2,1)S(1)} %get-tuple-element.62), channel_id=1, source_target_pairs={{0,2},{2,0},{4,6},{6,4},{8,10},{10,8},{12,14},{14,12},{1,3},{3,1},... | collective-permute-start | bytes 497672 | tf_op jit(solution)/shard_map/ppermute | solution.py:468
  48.9 9.7 %collective-permute-start.8 = (bf16[3,144,192]{2,1,0:T(8,128)(2,1)S(1)}, bf16[3,144,192]{2,1,0:T(8,128)(2,1)S(1)}, u32[]{:S(2)}, u32[]{:S(2)}) collective-permute-start(bf16[3,144,192]{2,1,0:T(8,128)(2,1)S(1)} %get-tuple-element.63), channel_id=1, source_target_pairs={{2,4},{4,2},{6,8},{8,6},{10,12},{12,10},{3,5},{5,3},{7,9},{9,7},{1... | collective-permute-start | bytes 497672 | tf_op jit(solution)/shard_map/ppermute | solution.py:469
  62.7 1.4 %collective-permute-start.9 = (bf16[16,16,192]{2,1,0:T(8,128)(2,1)S(1)}, bf16[16,16,192]{2,1,0:T(8,128)(2,1)S(1)}, u32[]{:S(2)}, u32[]{:S(2)}) collective-permute-start(bf16[16,16,192]{2,1,0:T(8,128)(2,1)S(1)} %get-tuple-element.66), channel_id=1, source_target_pairs={{0,1},{1,0},{2,3},{3,2},{4,5},{5,4},{6,7},{7,6},{8,9},{9,8},{10,11... | collective-permute-start | bytes 294920 | tf_op jit(solution)/shard_map/ppermute | solution.py:464
  64.1 12.3 %collective-permute-start.10 = (bf16[3,144,192]{2,1,0:T(8,128)(2,1)S(1)}, bf16[3,144,192]{2,1,0:T(8,128)(2,1)S(1)}, u32[]{:S(2)}, u32[]{:S(2)}) collective-permute-start(bf16[3,144,192]{2,1,0:T(8,128)(2,1)S(1)} %get-tuple-element.69), channel_id=1, source_target_pairs={{0,2},{2,0},{4,6},{6,4},{8,10},{10,8},{12,14},{14,12},{1,3},{3,1},... | collective-permute-start | bytes 497672 | tf_op jit(solution)/shard_map/ppermute | solution.py:468
  66.7 9.7 %collective-permute-start.11 = (bf16[3,144,192]{2,1,0:T(8,128)(2,1)S(1)}, bf16[3,144,192]{2,1,0:T(8,128)(2,1)S(1)}, u32[]{:S(2)}, u32[]{:S(2)}) collective-permute-start(bf16[3,144,192]{2,1,0:T(8,128)(2,1)S(1)} %get-tuple-element.70), channel_id=1, source_target_pairs={{2,4},{4,2},{6,8},{8,6},{10,12},{12,10},{3,5},{5,3},{7,9},{9,7},{1... | collective-permute-start | bytes 497672 | tf_op jit(solution)/shard_map/ppermute | solution.py:469

commit v4 on v3

--- a/solution.py
+++ b/solution.py
@@ -162,20 +162,25 @@
 
 
 def place_halo(parity, a_ref, b_ref, h0, h1):
-    cols = a_ref.shape[1] - EXT
-
-    def put(ref, index, row):
-        ref[index, :MARGIN, :] = row[cols : cols + MARGIN]
-        ref[index, MARGIN : MARGIN + cols, :] = row[:cols]
-        ref[index, MARGIN + cols :, :] = row[cols + MARGIN :]
-
+    width = h0.shape[1]
+    cols = width - EXT
+    middle = cols // 2
+    lane = lax.broadcasted_iota(jnp.int32, (width // 2, 128), 1)
     for e in range(3):
-        put(h0, (1 - parity) * 3 + e, a_ref[e, :, :128].astype(F32))
-        put(h0, parity * 3 + e, b_ref[e, :, :128].astype(F32))
-        a_up, a_down = a_ref[e, :, 128:].astype(F32), a_ref[2 - e, :, 128:].astype(F32)
-        b_up, b_down = b_ref[e, :, 128:].astype(F32), b_ref[2 - e, :, 128:].astype(F32)
+        for ref, first in ((a_ref, (1 - parity) * 3), (b_ref, parity * 3)):
+            row = ref[e, :width, :].astype(F32)
+            h0[first + e, :MARGIN, :] = row[cols : cols + MARGIN]
+            h0[first + e, MARGIN : MARGIN + cols, :] = row[:cols]
+            h0[first + e, MARGIN + cols :, :] = row[cols + MARGIN :]
+        a_up, a_down = a_ref[e, width:, :].astype(F32), a_ref[2 - e, width:, :].astype(F32)
+        b_up, b_down = b_ref[e, width:, :].astype(F32), b_ref[2 - e, width:, :].astype(F32)
         up, down = jnp.where(parity == 1, a_up, b_up), jnp.where(parity == 1, b_down, a_down)
-        put(h1, e, jnp.concatenate([up, down], axis=1))
+        first = jnp.where(lane < 64, up, pltpu.roll(down, 64, 1))
+        second = jnp.where(lane < 64, pltpu.roll(up, 64, 1), down)
+        h1[e, :MARGIN, :] = first[middle:]
+        h1[e, MARGIN : MARGIN + middle, :] = first[:middle]
+        h1[e, MARGIN + middle : MARGIN + cols, :] = second[:middle]
+        h1[e, MARGIN + cols :, :] = second[middle:]
 
 
 def conv_halo(h0, h1, acc_ref, k0, k1, layer, edge, flipped):
@@ -253,11 +258,18 @@
     return project(gain * back, normed, inv).astype(BF16)
 
 
+def fold(values):
+    count = values.shape[0] // 2
+    return jnp.concatenate([values[:count], values[count:]], axis=1)
+
+
 def send_rows(parity, field, lon_ref, a_ref, b_ref):
     rows, cols = field.shape[0], field.shape[1]
+    width = cols + EXT
     for e in range(3):
-        a_ref[e, :cols, :] = field[(1 - parity) * (rows - 3) + e].astype(BF16)
-        b_ref[e, :cols, :] = field[parity * (rows - 3) + e].astype(BF16)
+        for ref, row in ((a_ref, (1 - parity) * (rows - 3) + e), (b_ref, parity * (rows - 3) + e)):
+            ref[e, :cols, :] = field[row, :, :128].astype(BF16)
+            ref[e, width : width + cols // 2, :] = fold(field[row, :, 128:].astype(F32)).astype(BF16)
     for r in range(rows):
         lon_ref[r, :MARGIN, :] = field[r, cols - MARGIN :, :].astype(BF16)
         lon_ref[r, MARGIN:, :] = field[r, :MARGIN, :].astype(BF16)
@@ -390,13 +402,18 @@
 
 
 def extend_kernel(lon_ref, sa_in, sb_in, sa_ref, sb_ref):
-    rows, cols = lon_ref.shape[0], sa_ref.shape[1] - EXT
+    rows, width = lon_ref.shape[0], sa_ref.shape[1] // 3 * 2
+    cols = width - EXT
     parity = lax.axis_index("lat") % 2
     for e in range(3):
-        sa_ref[e, :cols, :] = sa_in[e, :cols, :]
-        sb_ref[e, :cols, :] = sb_in[e, :cols, :]
-        sa_ref[e, cols:, :] = lon_ref[(1 - parity) * (rows - 3) + e]
-        sb_ref[e, cols:, :] = lon_ref[parity * (rows - 3) + e]
+        for source, ref, row in (
+            (sa_in, sa_ref, (1 - parity) * (rows - 3) + e), (sb_in, sb_ref, parity * (rows - 3) + e)
+        ):
+            ref[e, :cols, :] = source[e, :cols, :]
+            ref[e, width : width + cols // 2, :] = source[e, width : width + cols // 2, :]
+            side = lon_ref[row]
+            ref[e, cols:width, :] = side[:, :128]
+            ref[e, width + cols // 2 :, :] = fold(side[:, 128:].astype(F32)).astype(BF16)
 
 
 def edges_kernel(
@@ -442,7 +459,7 @@
     swap_lon = [(i, (i + 1) % lon_size) for i in range(lon_size)]
 
     lon_shape = VMEM((rows, EXT, chans), BF16)
-    send_shape = VMEM((3, cols + EXT, chans), BF16)
+    send_shape = VMEM((3, (cols + EXT) // 2 * 3, 128), BF16)
     full32 = VMEM((rows, cols, chans), F32)
     full16 = VMEM((rows, cols, chans), BF16)
     sums = VMEM((1, chans), F32)

time: 93.3 us -> 88.9 us (0.953)
  waiting for transfers between devices: 13 us -> 5.31 us
  starting transfers between devices: 15.3 us -> 19.1 us
  blocking collectives: 12.1 us -> 11.1 us
    ppermute x4, waiting for transfers between devices: 7.95 us -> 0.31 us  [exchange(): halo_a = lax.ppermute(send_a, 'lat', swap_a)]
    ppermute x4, starting transfers between devices: 11.8 us -> 15.6 us  [exchange(): halo_a = lax.ppermute(send_a, 'lat', swap_a)]
    all_to_all x1, blocking collectives: 12.1 us -> 11.1 us  [on_device(): tile = lax.all_to_all(tile, ('lat', 'lon'), 0, 0, tiled=True)]
  transfers between devices with their start and end apart: 12 -> 12, of which waited for: 8 -> 6; matrix products, arithmetic and copies ran while one was open for 0% -> 0% of each run, Pallas kernels for 30% -> 32%
where the time goes in v4:
time: 88.9 us; the launch traced here: 88.6 us
  Pallas kernels  52 us (58%)
  starting transfers between devices  19.1 us (21%)
  blocking collectives  11.1 us (12%)
  waiting for transfers between devices  5.31 us (6%)
  between operations  1.02 us (1%)
    pallas_call x13, Pallas kernels, call(): pl.pallas_call(kernel, out_shape=out_shape, in_specs=in_specs, out_specs=...  50.1 us
    ppermute x4, starting transfers between devices, exchange(): halo_a = lax.ppermute(send_a, 'lat', swap_a)  15.6 us
    all_to_all x1, blocking collectives, on_device(): tile = lax.all_to_all(tile, ('lat', 'lon'), 0, 0, tiled=True)  11.1 us
    ppermute x4, waiting for transfers between devices, exchange(): side = lax.ppermute(lon, 'lon', swap_lon)  4.99 us
    ppermute x4, starting transfers between devices, exchange(): halo_b = lax.ppermute(send_b, 'lat', swap_b)  2.82 us
    pallas_call x1, Pallas kernels, on_device(): pl.pallas_call(functools.partial(scale_kernel, total), out_shape=[jax.Sha...  1.88 us
  transfers between devices with their start and end apart: 12, of which 6 were waited for; matrix products, arithmetic and copies ran while one was open for 0% of the time, Pallas kernels for 32%

profile of v4, /device:TPU:0, one launch (start us, length us, event | category | flops | bytes accessed | tf_op | source)
XLA Modules:
  0.0 88.6 jit_solution(16372765388748704055)
XLA Ops:
  0.6 0.0 copy-start.5
  0.6 0.0 copy-start.2
  0.7 3.8 %edges.1 = (f32[16,128,192]{2,1,0:T(8,128)S(1)}, bf16[16,16,192]{2,1,0:T(8,128)(2,1)S(1)}, bf16[3,216,128]{2,1,0:T(8,128)(2,1)S(1)}, bf16[3,216,128]{2,1,0:T(8,1...) custom-call(f32[16,192,128]{2,1,0:T(8,128)} %bitcast.11, ...), custom_call_target="tpu_custom_call" | custom-call | bytes 4000000 | tf_op jit(solution)/shard_map/edges/pallas_call | solution.py:469
  4.4 0.5 collective-permute-start
  5.0 1.0 %collective-permute-done.lon_ref = bf16[16,16,192]{2,1,0:T(8,128)(2,1)S(1)} collective-permute-done((bf16[16,16,192]{2,1,0:T(8,128)(2,1)S(1)}, bf16[16,16,192]{2,1,0:T(8,128)(2,1)S(1)}, u32[]{:S(2)}, u32[]{:S(2)}) %collective-permute-start) | collective-permute-done | bytes 98336 | tf_op jit(solution)/shard_map/ppermute | solution.py:481
  5.9 0.1 extend.4
  6.0 2.9 %collective-permute-start.1 = (bf16[3,216,128]{2,1,0:T(8,128)(2,1)S(1)}, bf16[3,216,128]{2,1,0:T(8,128)(2,1)S(1)}, u32[]{:S(2)}, u32[]{:S(2)}) collective-permute-start(bf16[3,216,128]{2,1,0:T(8,128)(2,1)S(1)} %get-tuple-element.47), channel_id=1, source_target_pairs={{0,2},{2,0},{4,6},{6,4},{8,10},{10,8},{12,14},{14,12},{1,3},{3,1},... | collective-permute-start | bytes 497672 | tf_op jit(solution)/shard_map/ppermute | solution.py:485
  8.9 0.7 collective-permute-start.2
  9.6 0.0 copy-done.5
  9.6 0.0 copy-done.2
  9.6 0.0 copy-start
  9.6 0.0 copy-start.1
  9.6 0.0 copy-start.3
  9.6 0.0 copy-start.4
  9.7 8.4 %conv_first.1 = (f32[16,128,192]{2,1,0:T(8,128)S(1)}, f32[1,192]{1,0:T(1,128)S(1)}, bf16[2,16,128,192]{3,2,1,0:T(8,128)(2,1)S(1)}, bf16[2,16,128,768]{3,2,1,0:T(8,128)(2,1)S(1)}) custom-call(f32[2,128]{1,0:T(2,128)S(1)} %copy-done.5, f32[16,128,192]{2,1,0:T(8,128)S(1)} %get-tuple-element.40.f_ref.t_ref, ...), custom_call_target="tpu_custom_call" | custom-call | flops 38535168 | bytes 4000000 | tf_op jit(solution)/shard_map/conv_first/pallas_call | solution.py:469
  18.0 0.0 collective-permute-done.1.a_ref
  18.0 0.0 collective-permute-done.2.b_ref
  18.1 0.0 copy-done
  18.1 4.5 %tangent0.1 = (f32[16,128,192]{2,1,0:T(8,128)S(1)}, bf16[16,16,192]{2,1,0:T(8,128)(2,1)S(1)}, bf16[3,216,128]{2,1,0:T(8,128)(2,1)S(1)}, bf16[3,216,128]{2,1,0:T(8,128)(2,1)S(1)}) custom-call(f32[2,128]{1,0:T(2,128)S(1)} %copy-done.5, f32[16,128,192]{2,1,0:T(8,128)S(1)} %get-tuple-element.44.acc_ref, bf16[3,216,128]{2,1,0:T(8,128)(2,1)S(1)} %collective-permute-done.1.a_ref, ...), custom_call_target="tpu_custom_call" | custom-call | flops 1207959552 | bytes 4000000 | tf_op jit(solution)/shard_map/tangent0/pallas_call | solution.py:469
  22.6 0.1 collective-permute-start.3
  22.7 1.3 %collective-permute-done.3.lon_ref = bf16[16,16,192]{2,1,0:T(8,128)(2,1)S(1)} collective-permute-done((bf16[16,16,192]{2,1,0:T(8,128)(2,1)S(1)}, bf16[16,16,192]{2,1,0:T(8,128)(2,1)S(1)}, u32[]{:S(2)}, u32[]{:S(2)}) %collective-permute-start.3) | collective-permute-done | bytes 98336 | tf_op jit(solution)/shard_map/ppermute | solution.py:481
  24.0 0.1 extend.5
  24.1 4.3 %collective-permute-start.4 = (bf16[3,216,128]{2,1,0:T(8,128)(2,1)S(1)}, bf16[3,216,128]{2,1,0:T(8,128)(2,1)S(1)}, u32[]{:S(2)}, u32[]{:S(2)}) collective-permute-start(bf16[3,216,128]{2,1,0:T(8,128)(2,1)S(1)} %get-tuple-element.56), channel_id=1, source_target_pairs={{0,2},{2,0},{4,6},{6,4},{8,10},{10,8},{12,14},{14,12},{1,3},{3,1},... | collective-permute-start | bytes 497672 | tf_op jit(solution)/shard_map/ppermute | solution.py:485
  28.4 0.7 collective-permute-start.5
  29.0 6.6 %conv1.1.acc_ref = f32[16,128,192]{2,1,0:T(8,128)S(1)} custom-call(f32[16,128,192]{2,1,0:T(8,128)S(1)} %get-tuple-element.52.f_ref.t_ref, bf16[16,16,192]{2,1,0:T(8,128)(2,1)S(1)} %collective-permute-done.3.lon_ref, f32[2,49,8,128]{3,2,1,0:T(8,128)S(1)} %get-tuple-element.42.k0, f32[2,2,49,8,128]{4,3,2,1,0:T(8,128)S(1)} %get-tuple-element.43.k1), custom_call_target="tpu_custom_call" | custom-call | flops 38535168 | bytes 4000000 | tf_op jit(solution)/shard_map/conv1/pallas_call | solution.py:469
  35.6 0.2 collective-permute-done.4.a_ref
  35.8 0.0 collective-permute-done.5.b_ref
  35.8 6.9 %tangent1.1 = (f32[16,128,192]{2,1,0:T(8,128)S(1)}, bf16[16,128,192]{2,1,0:T(8,128)(2,1)S(1)}, f32[1,192]{1,0:T(1,128)S(1)}, bf16[16,16,192]{2,1,0:T(8,128)(2,1)...) custom-call(f32[2,128]{1,0:T(2,128)S(1)} %copy-done.5, f32[16,128,192]{2,1,0:T(8,128)S(1)} %conv1.1.acc_ref, ...), custom_call_target="tpu_custom_call" | custom-call | flops 1207959552 | bytes 4000000 | tf_op jit(solution)/shard_map/tangent1/pallas_call | solution.py:469
  42.7 0.1 collective-permute-start.6
  42.8 1.3 %collective-permute-done.6.lon_ref = bf16[16,16,192]{2,1,0:T(8,128)(2,1)S(1)} collective-permute-done((bf16[16,16,192]{2,1,0:T(8,128)(2,1)S(1)}, bf16[16,16,192]{2,1,0:T(8,128)(2,1)S(1)}, u32[]{:S(2)}, u32[]{:S(2)}) %collective-permute-start.6) | collective-permute-done | bytes 98336 | tf_op jit(solution)/shard_map/ppermute | solution.py:481
  44.1 0.1 extend.6
  44.2 4.2 %collective-permute-start.7 = (bf16[3,216,128]{2,1,0:T(8,128)(2,1)S(1)}, bf16[3,216,128]{2,1,0:T(8,128)(2,1)S(1)}, u32[]{:S(2)}, u32[]{:S(2)}) collective-permute-start(bf16[3,216,128]{2,1,0:T(8,128)(2,1)S(1)} %get-tuple-element.62), channel_id=1, source_target_pairs={{0,2},{2,0},{4,6},{6,4},{8,10},{10,8},{12,14},{14,12},{1,3},{3,1},... | collective-permute-start | bytes 497672 | tf_op jit(solution)/shard_map/ppermute | solution.py:485
  48.3 0.8 collective-permute-start.8
  49.2 6.5 %convt1.1.acc_ref = f32[16,128,192]{2,1,0:T(8,128)S(1)} custom-call(bf16[16,128,192]{2,1,0:T(8,128)(2,1)S(1)} %get-tuple-element.58.f_ref, bf16[16,16,192]{2,1,0:T(8,128)(2,1)S(1)} %collective-permute-done.6.lon_ref, f32[2,49,8,128]{3,2,1,0:T(8,128)S(1)} %get-tuple-element.42.k0, f32[2,2,49,8,128]{4,3,2,1,0:T(8,128)S(1)} %get-tuple-element.43.k1), custom_call_target="tpu_custom_call" | custom-call | flops 38535168 | bytes 4000000 | tf_op jit(solution)/shard_map/convt1/pallas_call | solution.py:469
  55.7 0.0 collective-permute-done.7.a_ref
  55.8 0.0 collective-permute-done.8.b_ref
  55.8 4.0 %adjoint0.1 = (f32[16,128,192]{2,1,0:T(8,128)S(1)}, bf16[16,128,192]{2,1,0:T(8,128)(2,1)S(1)}, bf16[16,16,192]{2,1,0:T(8,128)(2,1)S(1)}, bf16[3,216,128]{2,1,0:T(8,128)(2,1)S(1)}, bf16[3,216,128]{2,1,0:T(8,128)(2,1)S(1)}) custom-call(f32[16,128,192]{2,1,0:T(8,128)S(1)} %convt1.1.acc_ref, bf16[3,216,128]{2,1,0:T(8,128)(2,1)S(1)} %collective-permute-done.7.a_ref, ...), custom_call_target="tpu_custom_call" | custom-call | flops 1207959552 | bytes 4000000 | tf_op jit(solution)/shard_map/adjoint0/pallas_call | solution.py:469
  59.8 0.1 collective-permute-start.9
  59.9 1.3 %collective-permute-done.9.lon_ref = bf16[16,16,192]{2,1,0:T(8,128)(2,1)S(1)} collective-permute-done((bf16[16,16,192]{2,1,0:T(8,128)(2,1)S(1)}, bf16[16,16,192]{2,1,0:T(8,128)(2,1)S(1)}, u32[]{:S(2)}, u32[]{:S(2)}) %collective-permute-start.9) | collective-permute-done | bytes 98336 | tf_op jit(solution)/shard_map/ppermute | solution.py:481
  61.2 0.1 extend.7
  61.3 4.3 %collective-permute-start.10 = (bf16[3,216,128]{2,1,0:T(8,128)(2,1)S(1)}, bf16[3,216,128]{2,1,0:T(8,128)(2,1)S(1)}, u32[]{:S(2)}, u32[]{:S(2)}) collective-permute-start(bf16[3,216,128]{2,1,0:T(8,128)(2,1)S(1)} %get-tuple-element.69), channel_id=1, source_target_pairs={{0,2},{2,0},{4,6},{6,4},{8,10},{10,8},{12,14},{14,12},{1,3},{3,1},... | collective-permute-start | bytes 497672 | tf_op jit(solution)/shard_map/ppermute | solution.py:485
  65.6 0.7 collective-permute-start.11
  66.2 6.6 %convt0.1.acc_ref = f32[16,128,192]{2,1,0:T(8,128)S(1)} custom-call(bf16[16,128,192]{2,1,0:T(8,128)(2,1)S(1)} %get-tuple-element.65.f_ref, bf16[16,16,192]{2,1,0:T(8,128)(2,1)S(1)} %collective-permute-done.9.lon_ref, f32[2,49,8,128]{3,2,1,0:T(8,128)S(1)} %get-tuple-element.42.k0, f32[2,2,49,8,128]{4,3,2,1,0:T(8,128)S(1)} %get-tuple-element.43.k1), custom_call_target="tpu_custom_call" | custom-call | flops 38535168 | bytes 4000000 | tf_op jit(solution)/shard_map/convt0/pallas_call | solution.py:469
  72.8 0.1 collective-permute-done.10.a_ref
  73.0 0.0 collective-permute-done.11.b_ref
  73.0 2.5 %final.1 = (f32[16,192,128]{2,1,0:T(8,128)S(1)}, f32[16,1,128]{2,1,0:T(1,128)S(1)}) custom-call(f32[2,128]{1,0:T(2,128)S(1)} %copy-done.5, f32[16,128,192]{2,1,0:T(8,128)S(1)} %convt0.1.acc_ref, bf16[3,216,128]{2,1,0:T(8,128)(2,1)S(1)} %collective-permute-done.10.a_ref, bf16[3,216,128]{2,1,0:T(8,128)(2,1)S(1)} %collective-permute-done.11.b_ref, ...), custom_call_target="tpu_custom_call" | custom-call | bytes 4000000 | tf_op jit(solution)/shard_map/final/pallas_call | solution.py:469
  75.5 11.1 %all_to_all.5.tile_ref = f32[16,1,128]{2,1,0:T(1,128)S(1)} all-to-all(f32[16,1,128]{2,1,0:T(1,128)S(1)} %get-tuple-element.74), channel_id=1, replica_groups=mesh['grp'=2,'lat'=8,'lon'=2] {'lat','lon'}, dimensions={0} | all-to-all | bytes 16384 | tf_op jit(solution)/shard_map/all_to_all | solution.py:549
  86.6 1.9 %scale.1 = (f32[16,192,128]{2,1,0:T(8,128)}, f32[1,128]{1,0:T(1,128)}) custom-call(f32[16,1,128]{2,1,0:T(1,128)S(1)} %all_to_all.5.tile_ref, f32[16,192,128]{2,1,0:T(8,128)S(1)} %get-tuple-element.75.w_ref), custom_call_target="tpu_custom_call" | custom-call | tf_op jit(solution)/shard_map/scale/pallas_call | solution.py:550
  (3 shorter events, 0.0 us)
Async XLA Ops:
  0.6 9.0 %copy-start.5 = (f32[2,128]{1,0:T(2,128)S(1)}, f32[2,128]{1,0:T(2,128)}, u32[]{:S(2)}) copy-start(f32[2,128]{1,0:T(2,128)} %constant.2.clone.area_ref) | copy-start | bytes 3076
  0.6 9.0 %copy-start.2 = (bf16[2,16,128,192]{2,3,1,0:T(8,128)(2,1)S(1)}, bf16[2,16,128,192]{2,3,1,0:T(8,128)(2,1)}, u32[]{:S(2)}) copy-start(bf16[2,16,128,192]{2,3,1,0:T(8,128)(2,1)} %param.16) | copy-start | bytes 4718596
  4.4 1.5 %collective-permute-start = (bf16[16,16,192]{2,1,0:T(8,128)(2,1)S(1)}, bf16[16,16,192]{2,1,0:T(8,128)(2,1)S(1)}, u32[]{:S(2)}, u32[]{:S(2)}) collective-permute-start(bf16[16,16,192]{2,1,0:T(8,128)(2,1)S(1)} %get-tuple-element.41), channel_id=1, source_target_pairs={{0,1},{1,0},{2,3},{3,2},{4,5},{5,4},{6,7},{7,6},{8,9},{9,8},{10,11... | collective-permute-start | bytes 294920 | tf_op jit(solution)/shard_map/ppermute | solution.py:481
  6.0 12.0 %collective-permute-start.1 = (bf16[3,216,128]{2,1,0:T(8,128)(2,1)S(1)}, bf16[3,216,128]{2,1,0:T(8,128)(2,1)S(1)}, u32[]{:S(2)}, u32[]{:S(2)}) collective-permute-start(bf16[3,216,128]{2,1,0:T(8,128)(2,1)S(1)} %get-tuple-element.47), channel_id=1, source_target_pairs={{0,2},{2,0},{4,6},{6,4},{8,10},{10,8},{12,14},{14,12},{1,3},{3,1},... | collective-permute-start | bytes 497672 | tf_op jit(solution)/shard_map/ppermute | solution.py:485
  8.9 9.1 %collective-permute-start.2 = (bf16[3,216,128]{2,1,0:T(8,128)(2,1)S(1)}, bf16[3,216,128]{2,1,0:T(8,128)(2,1)S(1)}, u32[]{:S(2)}, u32[]{:S(2)}) collective-permute-start(bf16[3,216,128]{2,1,0:T(8,128)(2,1)S(1)} %get-tuple-element.48), channel_id=1, source_target_pairs={{2,4},{4,2},{6,8},{8,6},{10,12},{12,10},{3,5},{5,3},{7,9},{9,7},{1... | collective-permute-start | bytes 497672 | tf_op jit(solution)/shard_map/ppermute | solution.py:486
  9.6 8.4 %copy-start = (bf16[2,192,768]{2,1,0:T(8,128)(2,1)S(1)}, bf16[2,192,768]{2,1,0:T(8,128)(2,1)}, u32[]{:S(2)}) copy-start(bf16[2,192,768]{2,1,0:T(8,128)(2,1)} %rest_4_.5) | copy-start | bytes 1769476
  9.6 8.4 %copy-start.1 = (bf16[2,768,192]{1,2,0:T(8,128)(2,1)S(1)}, bf16[2,768,192]{1,2,0:T(8,128)(2,1)}, u32[]{:S(2)}) copy-start(bf16[2,768,192]{1,2,0:T(8,128)(2,1)} %param.14) | copy-start | bytes 1769476
  9.6 8.4 %copy-start.3 = (f32[2,192]{1,0:T(2,128)S(1)}, f32[2,192]{1,0:T(2,128)}, u32[]{:S(2)}) copy-start(f32[2,192]{1,0:T(2,128)} %rest_3_.5) | copy-start | bytes 4612
  9.6 8.4 %copy-start.4 = (f32[2,192]{1,0:T(2,128)S(1)}, f32[2,192]{1,0:T(2,128)}, u32[]{:S(2)}) copy-start(f32[2,192]{1,0:T(2,128)} %rest_6_.5) | copy-start | bytes 4612
  22.6 1.4 %collective-permute-start.3 = (bf16[16,16,192]{2,1,0:T(8,128)(2,1)S(1)}, bf16[16,16,192]{2,1,0:T(8,128)(2,1)S(1)}, u32[]{:S(2)}, u32[]{:S(2)}) collective-permute-start(bf16[16,16,192]{2,1,0:T(8,128)(2,1)S(1)} %get-tuple-element.53), channel_id=1, source_target_pairs={{0,1},{1,0},{2,3},{3,2},{4,5},{5,4},{6,7},{7,6},{8,9},{9,8},{10,11... | collective-permute-start | bytes 294920 | tf_op jit(solution)/shard_map/ppermute | solution.py:481
  24.1 11.7 %collective-permute-start.4 = (bf16[3,216,128]{2,1,0:T(8,128)(2,1)S(1)}, bf16[3,216,128]{2,1,0:T(8,128)(2,1)S(1)}, u32[]{:S(2)}, u32[]{:S(2)}) collective-permute-start(bf16[3,216,128]{2,1,0:T(8,128)(2,1)S(1)} %get-tuple-element.56), channel_id=1, source_target_pairs={{0,2},{2,0},{4,6},{6,4},{8,10},{10,8},{12,14},{14,12},{1,3},{3,1},... | collective-permute-start | bytes 497672 | tf_op jit(solution)/shard_map/ppermute | solution.py:485
  28.4 7.4 %collective-permute-start.5 = (bf16[3,216,128]{2,1,0:T(8,128)(2,1)S(1)}, bf16[3,216,128]{2,1,0:T(8,128)(2,1)S(1)}, u32[]{:S(2)}, u32[]{:S(2)}) collective-permute-start(bf16[3,216,128]{2,1,0:T(8,128)(2,1)S(1)} %get-tuple-element.57), channel_id=1, source_target_pairs={{2,4},{4,2},{6,8},{8,6},{10,12},{12,10},{3,5},{5,3},{7,9},{9,7},{1... | collective-permute-start | bytes 497672 | tf_op jit(solution)/shard_map/ppermute | solution.py:486
  42.7 1.4 %collective-permute-start.6 = (bf16[16,16,192]{2,1,0:T(8,128)(2,1)S(1)}, bf16[16,16,192]{2,1,0:T(8,128)(2,1)S(1)}, u32[]{:S(2)}, u32[]{:S(2)}) collective-permute-start(bf16[16,16,192]{2,1,0:T(8,128)(2,1)S(1)} %get-tuple-element.59), channel_id=1, source_target_pairs={{0,1},{1,0},{2,3},{3,2},{4,5},{5,4},{6,7},{7,6},{8,9},{9,8},{10,11... | collective-permute-start | bytes 294920 | tf_op jit(solution)/shard_map/ppermute | solution.py:481
  44.2 11.6 %collective-permute-start.7 = (bf16[3,216,128]{2,1,0:T(8,128)(2,1)S(1)}, bf16[3,216,128]{2,1,0:T(8,128)(2,1)S(1)}, u32[]{:S(2)}, u32[]{:S(2)}) collective-permute-start(bf16[3,216,128]{2,1,0:T(8,128)(2,1)S(1)} %get-tuple-element.62), channel_id=1, source_target_pairs={{0,2},{2,0},{4,6},{6,4},{8,10},{10,8},{12,14},{14,12},{1,3},{3,1},... | collective-permute-start | bytes 497672 | tf_op jit(solution)/shard_map/ppermute | solution.py:485
  48.3 7.4 %collective-permute-start.8 = (bf16[3,216,128]{2,1,0:T(8,128)(2,1)S(1)}, bf16[3,216,128]{2,1,0:T(8,128)(2,1)S(1)}, u32[]{:S(2)}, u32[]{:S(2)}) collective-permute-start(bf16[3,216,128]{2,1,0:T(8,128)(2,1)S(1)} %get-tuple-element.63), channel_id=1, source_target_pairs={{2,4},{4,2},{6,8},{8,6},{10,12},{12,10},{3,5},{5,3},{7,9},{9,7},{1... | collective-permute-start | bytes 497672 | tf_op jit(solution)/shard_map/ppermute | solution.py:486
  59.8 1.4 %collective-permute-start.9 = (bf16[16,16,192]{2,1,0:T(8,128)(2,1)S(1)}, bf16[16,16,192]{2,1,0:T(8,128)(2,1)S(1)}, u32[]{:S(2)}, u32[]{:S(2)}) collective-permute-start(bf16[16,16,192]{2,1,0:T(8,128)(2,1)S(1)} %get-tuple-element.66), channel_id=1, source_target_pairs={{0,1},{1,0},{2,3},{3,2},{4,5},{5,4},{6,7},{7,6},{8,9},{9,8},{10,11... | collective-permute-start | bytes 294920 | tf_op jit(solution)/shard_map/ppermute | solution.py:481
  61.3 11.6 %collective-permute-start.10 = (bf16[3,216,128]{2,1,0:T(8,128)(2,1)S(1)}, bf16[3,216,128]{2,1,0:T(8,128)(2,1)S(1)}, u32[]{:S(2)}, u32[]{:S(2)}) collective-permute-start(bf16[3,216,128]{2,1,0:T(8,128)(2,1)S(1)} %get-tuple-element.69), channel_id=1, source_target_pairs={{0,2},{2,0},{4,6},{6,4},{8,10},{10,8},{12,14},{14,12},{1,3},{3,1},... | collective-permute-start | bytes 497672 | tf_op jit(solution)/shard_map/ppermute | solution.py:485
  65.6 7.4 %collective-permute-start.11 = (bf16[3,216,128]{2,1,0:T(8,128)(2,1)S(1)}, bf16[3,216,128]{2,1,0:T(8,128)(2,1)S(1)}, u32[]{:S(2)}, u32[]{:S(2)}) collective-permute-start(bf16[3,216,128]{2,1,0:T(8,128)(2,1)S(1)} %get-tuple-element.70), channel_id=1, source_target_pairs={{2,4},{4,2},{6,8},{8,6},{10,12},{12,10},{3,5},{5,3},{7,9},{9,7},{1... | collective-permute-start | bytes 497672 | tf_op jit(solution)/shard_map/ppermute | solution.py:486

commit v5 on v4

--- a/solution.py
+++ b/solution.py
@@ -47,42 +47,43 @@
                     k1[layer, flipped, a * 7 + b] = jnp.concatenate(pair, axis=1)
 
 
-def fill_row(xs, index, mid, side):
-    cols = mid.shape[0]
-    xs[index, :MARGIN, :] = side[:MARGIN]
-    xs[index, MARGIN : MARGIN + cols, :] = mid
-    xs[index, MARGIN + cols :, :] = side[MARGIN:]
-
-
-def conv_local(load_row, lon_ref, k0, k1, layer, out_ref, xs0, xs1, flipped, beside=None):
+def planes_kernel(f_ref, x0, x1):
+    rows = f_ref.shape[0]
+    half = rows // 2
+
+    def load_row(r):
+        return f_ref[r].astype(BF16).astype(F32)
+
+    for q in range(half + 3):
+        low, high = load_row(q), load_row(rows - 1 - q)
+        if q < half:
+            x0[q] = low[:, :128]
+            x0[rows - 1 - q] = high[:, :128]
+        x1[q] = jnp.concatenate([low[:, 128:], high[:, 128:]], axis=1)
+
+
+def conv_local(x0, x1, lon_ref, k0, k1, layer, out_ref, e0, e1, flipped, beside=None):
     rows, cols, _ = out_ref.shape
     half = rows // 2
 
-    def fill(q, wide_too):
-        low, high = load_row(q), load_row(rows - 1 - q)
-        low_side, high_side = lon_ref[q].astype(F32), lon_ref[rows - 1 - q].astype(F32)
-        if wide_too:
-            fill_row(xs0, q, low[:, :128], low_side[:, :128])
-            fill_row(xs0, rows - 1 - q, high[:, :128], high_side[:, :128])
-        mid = jnp.concatenate([low[:, 128:], high[:, 128:]], axis=1)
-        side = jnp.concatenate([low_side[:, 128:], high_side[:, 128:]], axis=1)
-        fill_row(xs1, q, mid, side)
-
-    @pl.loop(0, half)
-    def _(q):
-        fill(q, True)
-
-    for q in range(half, half + 3):
-        fill(q, False)
-
-    @pl.loop(0, cols // 8)
-    def _(j):
-        base = pl.multiple_of(j * 8, 8)
+    def ends(ref, index, x, side):
+        ref[0, index, :MARGIN, :] = side[:MARGIN]
+        ref[0, index, MARGIN:, :] = x[index, : 2 * MARGIN, :]
+        ref[1, index, : 2 * MARGIN, :] = x[index, cols - 2 * MARGIN :, :]
+        ref[1, index, 2 * MARGIN :, :] = side[MARGIN:]
+
+    for r in range(rows):
+        ends(e0, r, x0, lon_ref[r, :, :128].astype(F32))
+    for q in range(half + 3):
+        low, high = lon_ref[q, :, 128:].astype(F32), lon_ref[rows - 1 - q, :, 128:].astype(F32)
+        ends(e1, q, x1, jnp.concatenate([low, high], axis=1))
+
+    def tile(base, low_window, high_window):
         acc = [None] * rows
         for b in range(7):
             taps = [k0[layer, tap_index(a, b, flipped)] for a in range(7)]
             for r in range(rows):
-                x = xs0[r, pl.ds(base + (MARGIN - 3 + b), 8), :]
+                x = low_window(r, b)
                 for a in range(7):
                     o = r + 3 - a
                     if 0 <= o < rows:
@@ -94,7 +95,7 @@
         for b in range(7):
             taps = [k1[layer, int(flipped), a * 7 + b] for a in range(7)]
             for q in range(half + 3):
-                x = xs1[q, pl.ds(base + (MARGIN - 3 + b), 8), :]
+                x = high_window(q, b)
                 for a in range(7):
                     o = q + 3 - a
                     if 0 <= o < half:
@@ -103,26 +104,43 @@
         for o in range(half):
             out_ref[o, pl.ds(base, 8), 128:] = acc[o][:, :64]
             out_ref[rows - 1 - o, pl.ds(base, 8), 128:] = acc[o][:, 64:]
+
+    def both(j, *windows):
+        tile(pl.multiple_of(j * 8, 8), *windows)
         if beside is not None:
             beside(j)
 
-
-def conv_scratch(rows, cols):
+    last = cols // 8 - 1
+
+    @pl.loop(0, 2)
+    def _(s):
+        both(
+            s * last,
+            lambda r, b: e0[s, r, MARGIN - 3 + b : 2 * MARGIN - 3 + b, :],
+            lambda q, b: e1[s, q, MARGIN - 3 + b : 2 * MARGIN - 3 + b, :],
+        )
+
+    @pl.loop(1, last)
+    def _(j):
+        base = pl.multiple_of(j * 8, 8)
+        both(
+            j, lambda r, b: x0[r, pl.ds(base + (b - 3), 8), :], lambda q, b: x1[q, pl.ds(base + (b - 3), 8), :]
+        )
+
+
+def conv_scratch(rows):
     return [
-        pltpu.VMEM((rows, cols + 2 * MARGIN, 128), F32),
-        pltpu.VMEM((rows // 2 + 3, cols + 2 * MARGIN, 128), F32),
+        pltpu.VMEM((2, rows, 3 * MARGIN, 128), F32),
+        pltpu.VMEM((2, rows // 2 + 3, 3 * MARGIN, 128), F32),
     ]
 
 
-def conv_kernel(layer, flipped, f_ref, lon_ref, k0, k1, out_ref, *scratch):
-    def load_row(r):
-        return f_ref[r].astype(BF16).astype(F32)
-
-    conv_local(load_row, lon_ref, k0, k1, layer, out_ref, *scratch, flipped)
+def conv_kernel(layer, flipped, x0, x1, lon_ref, k0, k1, out_ref, *scratch):
+    conv_local(x0, x1, lon_ref, k0, k1, layer, out_ref, *scratch, flipped)
 
 
 def first_conv_kernel(
-    area_ref, f_ref, lon_ref, k0, k1, turned_ref, slope_hbm, out_ref, sum_ref, normed_out, slope_out, xs0, xs1, sems
+    area_ref, f_ref, x0, x1, lon_ref, k0, k1, turned_ref, slope_hbm, out_ref, sum_ref, normed_out, slope_out, e0, e1, sems
 ):
     rows, cols, _ = f_ref.shape
     start = lax.axis_index("lat") * rows
@@ -142,9 +160,6 @@
             turned = lax.dot_general(eye, turned_ref[layer, r], ACROSS, preferred_element_type=F32)
             normed_out[layer, r] = turned.astype(BF16)
 
-    def load_row(r):
-        return f_ref[r].astype(BF16).astype(F32)
-
     sum_ref[...] = jnp.zeros_like(sum_ref)
     steps = cols // 8
     for j in range(steps, rows):
@@ -156,7 +171,7 @@
         else:
             pl.when(j < rows)(lambda: turn_row(j))
 
-    conv_local(load_row, lon_ref, k0, k1, 0, out_ref, xs0, xs1, False, beside)
+    conv_local(x0, x1, lon_ref, k0, k1, 0, out_ref, e0, e1, False, beside)
     for fetch in fetches:
         fetch.wait()
 
@@ -401,7 +416,7 @@
         copy.wait()
 
 
-def extend_kernel(lon_ref, sa_in, sb_in, sa_ref, sb_ref):
+def extend_kernel(after_ref, lon_ref, sa_in, sb_in, sa_ref, sb_ref):
     rows, width = lon_ref.shape[0], sa_ref.shape[1] // 3 * 2
     cols = width - EXT
     parity = lax.axis_index("lat") % 2
@@ -477,18 +492,22 @@
             name=name,
         )(*args)
 
-    def exchange(lon, send_a, send_b):
+    def exchange(field, lon, send_a, send_b):
         side = lax.ppermute(lon, "lon", swap_lon)
+        planes = call(
+            planes_kernel, [VMEM((rows, cols, 128), F32), VMEM((rows // 2 + 3, cols, 128), F32)], [IN_VMEM], (field,),
+            flops=conv_flops // 8, name="planes",
+        )
         send_a, send_b = call(
-            extend_kernel, [send_shape] * 2, [IN_VMEM] * 3, (side, send_a, send_b), name="extend"
+            extend_kernel, [send_shape] * 2, [IN_VMEM] * 4, (planes[1], side, send_a, send_b), name="extend"
         )
+        halo_b = lax.ppermute(send_b, "lat", swap_b)
         halo_a = lax.ppermute(send_a, "lat", swap_a)
-        halo_b = lax.ppermute(send_b, "lat", swap_b)
-        return side, halo_a, halo_b
+        return (*planes, side), halo_a, halo_b
 
     conv_flops = 2 * 49 * rows * cols * chans
     net_flops = 4 * rows * cols * chans * hidden
-    kscr = conv_scratch(rows, cols)
+    kscr = conv_scratch(rows)
     hscr = halo_scratch(cols, chans)
 
     tangent, lon, send_a, send_b, k0, k1, inv_cells = call(
@@ -504,12 +523,12 @@
         ],
         name="edges",
     )
-    side, halo_a, halo_b = exchange(lon, send_a, send_b)
+    taken, halo_a, halo_b = exchange(tangent, lon, send_a, send_b)
     acc, vv, normed_cells, slope_cells = call(
         first_conv_kernel,
         [full32, sums, VMEM((layers, rows, cols, chans), BF16), VMEM(slope.shape, BF16)],
-        [IN_SMEM] + [IN_VMEM] * 5 + [IN_HBM],
-        (area, tangent, side, k0, k1, jnp.transpose(normed, (0, 1, 3, 2)), slope),
+        [IN_SMEM] + [IN_VMEM] * 7 + [IN_HBM],
+        (area, tangent, *taken, k0, k1, jnp.transpose(normed, (0, 1, 3, 2)), slope),
         kscr + [pltpu.SemaphoreType.DMA((layers,))], conv_flops, "conv_first",
     )
     net = (normed_cells, inv_cells, slope_cells, gains, w_in, across_cells, scales)
@@ -521,18 +540,19 @@
             functools.partial(tangent_kernel, layer, last), outs, [IN_SMEM] + [IN_VMEM] * 13,
             (area, acc, halo_a, halo_b, k0, k1, tangent) + net, hscr, net_flops, f"tangent{layer}",
         )
-        side, halo_a, halo_b = exchange(*got[-3:])
         if last:
             grad, back, uu = got[:3]
         else:
             tangent = got[0]
+        taken, halo_a, halo_b = exchange(back if last else tangent, *got[-3:])
+        if not last:
             (acc,) = call(
-                functools.partial(conv_kernel, layer + 1, False), [full32], [IN_VMEM] * 4, (tangent, side, k0, k1),
+                functools.partial(conv_kernel, layer + 1, False), [full32], [IN_VMEM] * 5, (*taken, k0, k1),
                 kscr, conv_flops, f"conv{layer + 1}",
             )
     for layer in range(layers - 1, -1, -1):
         (acc,) = call(
-            functools.partial(conv_kernel, layer, True), [full32], [IN_VMEM] * 4, (back, side, k0, k1),
+            functools.partial(conv_kernel, layer, True), [full32], [IN_VMEM] * 5, (*taken, k0, k1),
             kscr, conv_flops, f"convt{layer}",
         )
         if layer > 0:
@@ -540,7 +560,7 @@
                 functools.partial(adjoint_kernel, layer - 1), [full32, full16, lon_shape, send_shape, send_shape],
                 [IN_VMEM] * 13, (acc, halo_a, halo_b, k0, k1, grad) + net, hscr, net_flops, f"adjoint{layer - 1}",
             )
-            side, halo_a, halo_b = exchange(lon, send_a, send_b)
+            taken, halo_a, halo_b = exchange(back, lon, send_a, send_b)
     members = lat_size * lon_size
     w, tile = call(
         final_kernel, [VMEM((rows, chans, cols), F32), VMEM((members, 1, 128), F32)], [IN_SMEM] + [IN_VMEM] * 8,

time: 88.9 us -> 86.2 us (0.970)
  Pallas kernels: 52 us -> 50.2 us
  starting transfers between devices: 19.1 us -> 17.9 us
  waiting for transfers between devices: 5.31 us -> 6.32 us
    ppermute x4, waiting for transfers between devices: 0.31 us -> 2.17 us  [exchange(): halo_a = lax.ppermute(send_a, 'lat', swap_a)]
    pallas_call x13 -> x17, Pallas kernels: 50.1 us -> 48.3 us  [call(): pl.pallas_call(kernel, out_shape=out_shape, in_specs=in_specs, out_specs=...]
    ppermute x4, starting transfers between devices: 15.6 us -> 14.4 us  [exchange(): halo_a = lax.ppermute(send_a, 'lat', swap_a)]
  transfers between devices with their start and end apart: 12 -> 12, of which waited for: 6 -> 7; matrix products, arithmetic and copies ran while one was open for 0% -> 0% of each run, Pallas kernels for 32% -> 31%
where the time goes in v5:
time: 86.2 us; the launch traced here: 86 us
  Pallas kernels  50.2 us (58%)
  starting transfers between devices  17.9 us (21%)
  blocking collectives  10.5 us (12%)
  waiting for transfers between devices  6.32 us (7%)
  between operations  1.03 us (1%)
    pallas_call x17, Pallas kernels, call(): pl.pallas_call(kernel, out_shape=out_shape, in_specs=in_specs, out_specs=...  48.3 us
    ppermute x4, starting transfers between devices, exchange(): halo_a = lax.ppermute(send_a, 'lat', swap_a)  14.4 us
    all_to_all x1, blocking collectives, on_device(): tile = lax.all_to_all(tile, ('lat', 'lon'), 0, 0, tiled=True)  10.5 us
    ppermute x4, waiting for transfers between devices, exchange(): side = lax.ppermute(lon, 'lon', swap_lon)  4.14 us
    ppermute x4, starting transfers between devices, exchange(): halo_b = lax.ppermute(send_b, 'lat', swap_b)  2.82 us
    ppermute x4, waiting for transfers between devices, exchange(): halo_a = lax.ppermute(send_a, 'lat', swap_a)  2.17 us
    pallas_call x1, Pallas kernels, on_device(): pl.pallas_call(functools.partial(scale_kernel, total), out_shape=[jax.Sha...  1.88 us
  transfers between devices with their start and end apart: 12, of which 7 were waited for; matrix products, arithmetic and copies ran while one was open for 0% of the time, Pallas kernels for 31%

profile of v5, /device:TPU:0, one launch (start us, length us, event | category | flops | bytes accessed | tf_op | source)
XLA Modules:
  0.0 86.0 jit_solution(17499343094345987761)
XLA Ops:
  0.6 0.0 copy-start.5
  0.7 3.8 %edges.1 = (f32[16,128,192]{2,1,0:T(8,128)S(1)}, bf16[16,16,192]{2,1,0:T(8,128)(2,1)S(1)}, bf16[3,216,128]{2,1,0:T(8,128)(2,1)S(1)}, bf16[3,216,128]{2,1,0:T(8,1...) custom-call(f32[16,192,128]{2,1,0:T(8,128)} %bitcast.11, ...), custom_call_target="tpu_custom_call" | custom-call | bytes 4000000 | tf_op jit(solution)/shard_map/edges/pallas_call | solution.py:484
  4.4 0.5 collective-permute-start
  5.0 0.2 planes.4
  5.2 0.7 collective-permute-done.lon_ref
  5.9 0.1 extend.4
  6.0 2.9 %collective-permute-start.1 = (bf16[3,216,128]{2,1,0:T(8,128)(2,1)S(1)}, bf16[3,216,128]{2,1,0:T(8,128)(2,1)S(1)}, u32[]{:S(2)}, u32[]{:S(2)}) collective-permute-start(bf16[3,216,128]{2,1,0:T(8,128)(2,1)S(1)} %get-tuple-element.57), channel_id=1, source_target_pairs={{0,2},{2,0},{4,6},{6,4},{8,10},{10,8},{12,14},{14,12},{1,3},{3,1},... | collective-permute-start | bytes 497672 | tf_op jit(solution)/shard_map/ppermute | solution.py:505
  8.9 0.7 collective-permute-start.2
  9.6 0.0 copy-start
  9.6 0.0 copy-start.1
  9.6 0.0 copy-start.3
  9.6 0.0 copy-start.4
  9.7 7.7 %conv_first.1 = (f32[16,128,192]{2,1,0:T(8,128)S(1)}, f32[1,192]{1,0:T(1,128)S(1)}, bf16[2,16,128,192]{3,2,1,0:T(8,128)(2,1)S(1)}, bf16[2,16,128,768]{3,2,1,0:T(8,128)(2,1)S(1)}) custom-call(f32[2,128]{1,0:T(2,128)S(1)} %copy-done.5, f32[16,128,192]{2,1,0:T(8,128)S(1)} %get-tuple-element.48.f_ref.t_ref, f32[16,128,128]{2,1,0:T(8,128)S(1)} %get-tuple-element.49.x0, ...), custom_call_target="tpu_custom_call" | custom-call | flops 38535168 | bytes 4000000 | tf_op jit(solution)/shard_map/conv_first/pallas_call | solution.py:484
  17.3 0.0 collective-permute-done.1.a_ref
  17.3 0.0 collective-permute-done.2.b_ref
  17.4 4.4 %tangent0.1 = (f32[16,128,192]{2,1,0:T(8,128)S(1)}, bf16[16,16,192]{2,1,0:T(8,128)(2,1)S(1)}, bf16[3,216,128]{2,1,0:T(8,128)(2,1)S(1)}, bf16[3,216,128]{2,1,0:T(8,128)(2,1)S(1)}) custom-call(f32[2,128]{1,0:T(2,128)S(1)} %copy-done.5, f32[16,128,192]{2,1,0:T(8,128)S(1)} %get-tuple-element.54.acc_ref, bf16[3,216,128]{2,1,0:T(8,128)(2,1)S(1)} %collective-permute-done.1.a_ref, ...), custom_call_target="tpu_custom_call" | custom-call | flops 1207959552 | bytes 4000000 | tf_op jit(solution)/shard_map/tangent0/pallas_call | solution.py:484
  21.8 0.1 collective-permute-start.3
  21.9 0.2 planes.5
  22.2 1.1 %collective-permute-done.3.lon_ref = bf16[16,16,192]{2,1,0:T(8,128)(2,1)S(1)} collective-permute-done((bf16[16,16,192]{2,1,0:T(8,128)(2,1)S(1)}, bf16[16,16,192]{2,1,0:T(8,128)(2,1)S(1)}, u32[]{:S(2)}, u32[]{:S(2)}) %collective-permute-start.3) | collective-permute-done | bytes 98336 | tf_op jit(solution)/shard_map/ppermute | solution.py:496
  23.2 0.1 extend.5
  23.3 4.3 %collective-permute-start.4 = (bf16[3,216,128]{2,1,0:T(8,128)(2,1)S(1)}, bf16[3,216,128]{2,1,0:T(8,128)(2,1)S(1)}, u32[]{:S(2)}, u32[]{:S(2)}) collective-permute-start(bf16[3,216,128]{2,1,0:T(8,128)(2,1)S(1)} %get-tuple-element.68), channel_id=1, source_target_pairs={{0,2},{2,0},{4,6},{6,4},{8,10},{10,8},{12,14},{14,12},{1,3},{3,1},... | collective-permute-start | bytes 497672 | tf_op jit(solution)/shard_map/ppermute | solution.py:505
  27.6 0.8 collective-permute-start.5
  28.5 6.0 %conv1.1.acc_ref = f32[16,128,192]{2,1,0:T(8,128)S(1)} custom-call(f32[16,128,128]{2,1,0:T(8,128)S(1)} %get-tuple-element.63.x0, f32[11,128,128]{2,1,0:T(8,128)S(1)} %get-tuple-element.64.x1.after_ref, bf16[16,16,192]{2,1,0:T(8,128)(2,1)S(1)} %collective-permute-done.3.lon_ref, f32[2,49,8,128]{3,2,1,0:T(8,128)S(1)} %get-tuple-element.52.k0, ...), custom_call_target="tpu_custom_call" | custom-call | flops 38535168 | bytes 4000000 | tf_op jit(solution)/shard_map/conv1/pallas_call | solution.py:484
  34.5 0.6 collective-permute-done.4.a_ref
  35.0 0.0 collective-permute-done.5.b_ref
  35.0 6.9 %tangent1.1 = (f32[16,128,192]{2,1,0:T(8,128)S(1)}, bf16[16,128,192]{2,1,0:T(8,128)(2,1)S(1)}, f32[1,192]{1,0:T(1,128)S(1)}, bf16[16,16,192]{2,1,0:T(8,128)(2,1)...) custom-call(f32[2,128]{1,0:T(2,128)S(1)} %copy-done.5, f32[16,128,192]{2,1,0:T(8,128)S(1)} %conv1.1.acc_ref, ...), custom_call_target="tpu_custom_call" | custom-call | flops 1207959552 | bytes 4000000 | tf_op jit(solution)/shard_map/tangent1/pallas_call | solution.py:484
  41.9 0.1 collective-permute-start.6
  42.0 0.2 planes.6
  42.2 1.1 %collective-permute-done.6.lon_ref = bf16[16,16,192]{2,1,0:T(8,128)(2,1)S(1)} collective-permute-done((bf16[16,16,192]{2,1,0:T(8,128)(2,1)S(1)}, bf16[16,16,192]{2,1,0:T(8,128)(2,1)S(1)}, u32[]{:S(2)}, u32[]{:S(2)}) %collective-permute-start.6) | collective-permute-done | bytes 98336 | tf_op jit(solution)/shard_map/ppermute | solution.py:496
  43.3 0.1 extend.6
  43.4 3.7 %collective-permute-start.7 = (bf16[3,216,128]{2,1,0:T(8,128)(2,1)S(1)}, bf16[3,216,128]{2,1,0:T(8,128)(2,1)S(1)}, u32[]{:S(2)}, u32[]{:S(2)}) collective-permute-start(bf16[3,216,128]{2,1,0:T(8,128)(2,1)S(1)} %get-tuple-element.76), channel_id=1, source_target_pairs={{0,2},{2,0},{4,6},{6,4},{8,10},{10,8},{12,14},{14,12},{1,3},{3,1},... | collective-permute-start | bytes 497672 | tf_op jit(solution)/shard_map/ppermute | solution.py:505
  47.2 0.7 collective-permute-start.8
  47.8 5.9 %convt1.1.acc_ref = f32[16,128,192]{2,1,0:T(8,128)S(1)} custom-call(f32[16,128,128]{2,1,0:T(8,128)S(1)} %get-tuple-element.71.x0, f32[11,128,128]{2,1,0:T(8,128)S(1)} %get-tuple-element.72.x1.after_ref, bf16[16,16,192]{2,1,0:T(8,128)(2,1)S(1)} %collective-permute-done.6.lon_ref, f32[2,49,8,128]{3,2,1,0:T(8,128)S(1)} %get-tuple-element.52.k0, ...), custom_call_target="tpu_custom_call" | custom-call | flops 38535168 | bytes 4000000 | tf_op jit(solution)/shard_map/convt1/pallas_call | solution.py:484
  53.7 0.8 collective-permute-done.7.a_ref
  54.6 0.0 collective-permute-done.8.b_ref
  54.6 4.0 %adjoint0.1 = (f32[16,128,192]{2,1,0:T(8,128)S(1)}, bf16[16,128,192]{2,1,0:T(8,128)(2,1)S(1)}, bf16[16,16,192]{2,1,0:T(8,128)(2,1)S(1)}, bf16[3,216,128]{2,1,0:T(8,128)(2,1)S(1)}, bf16[3,216,128]{2,1,0:T(8,128)(2,1)S(1)}) custom-call(f32[16,128,192]{2,1,0:T(8,128)S(1)} %convt1.1.acc_ref, bf16[3,216,128]{2,1,0:T(8,128)(2,1)S(1)} %collective-permute-done.7.a_ref, ...), custom_call_target="tpu_custom_call" | custom-call | flops 1207959552 | bytes 4000000 | tf_op jit(solution)/shard_map/adjoint0/pallas_call | solution.py:484
  58.6 0.1 collective-permute-start.9
  58.6 0.2 planes.7
  58.8 1.1 %collective-permute-done.9.lon_ref = bf16[16,16,192]{2,1,0:T(8,128)(2,1)S(1)} collective-permute-done((bf16[16,16,192]{2,1,0:T(8,128)(2,1)S(1)}, bf16[16,16,192]{2,1,0:T(8,128)(2,1)S(1)}, u32[]{:S(2)}, u32[]{:S(2)}) %collective-permute-start.9) | collective-permute-done | bytes 98336 | tf_op jit(solution)/shard_map/ppermute | solution.py:496
  60.0 0.1 extend.7
  60.1 3.5 %collective-permute-start.10 = (bf16[3,216,128]{2,1,0:T(8,128)(2,1)S(1)}, bf16[3,216,128]{2,1,0:T(8,128)(2,1)S(1)}, u32[]{:S(2)}, u32[]{:S(2)}) collective-permute-start(bf16[3,216,128]{2,1,0:T(8,128)(2,1)S(1)} %get-tuple-element.85), channel_id=1, source_target_pairs={{0,2},{2,0},{4,6},{6,4},{8,10},{10,8},{12,14},{14,12},{1,3},{3,1},... | collective-permute-start | bytes 497672 | tf_op jit(solution)/shard_map/ppermute | solution.py:505
  63.5 0.7 collective-permute-start.11
  64.2 5.9 %convt0.1.acc_ref = f32[16,128,192]{2,1,0:T(8,128)S(1)} custom-call(f32[16,128,128]{2,1,0:T(8,128)S(1)} %get-tuple-element.80.x0, f32[11,128,128]{2,1,0:T(8,128)S(1)} %get-tuple-element.81.x1.after_ref, bf16[16,16,192]{2,1,0:T(8,128)(2,1)S(1)} %collective-permute-done.9.lon_ref, f32[2,49,8,128]{3,2,1,0:T(8,128)S(1)} %get-tuple-element.52.k0, ...), custom_call_target="tpu_custom_call" | custom-call | flops 38535168 | bytes 4000000 | tf_op jit(solution)/shard_map/convt0/pallas_call | solution.py:484
  70.1 0.8 collective-permute-done.10.a_ref
  70.9 0.0 collective-permute-done.11.b_ref
  70.9 2.5 %final.1 = (f32[16,192,128]{2,1,0:T(8,128)S(1)}, f32[16,1,128]{2,1,0:T(1,128)S(1)}) custom-call(f32[2,128]{1,0:T(2,128)S(1)} %copy-done.5, f32[16,128,192]{2,1,0:T(8,128)S(1)} %convt0.1.acc_ref, bf16[3,216,128]{2,1,0:T(8,128)(2,1)S(1)} %collective-permute-done.10.a_ref, bf16[3,216,128]{2,1,0:T(8,128)(2,1)S(1)} %collective-permute-done.11.b_ref, ...), custom_call_target="tpu_custom_call" | custom-call | bytes 4000000 | tf_op jit(solution)/shard_map/final/pallas_call | solution.py:484
  73.4 10.5 %all_to_all.5.tile_ref = f32[16,1,128]{2,1,0:T(1,128)S(1)} all-to-all(f32[16,1,128]{2,1,0:T(1,128)S(1)} %get-tuple-element.90), channel_id=1, replica_groups=mesh['grp'=2,'lat'=8,'lon'=2] {'lat','lon'}, dimensions={0} | all-to-all | bytes 16384 | tf_op jit(solution)/shard_map/all_to_all | solution.py:569
  83.9 1.9 %scale.1 = (f32[16,192,128]{2,1,0:T(8,128)}, f32[1,128]{1,0:T(1,128)}) custom-call(f32[16,1,128]{2,1,0:T(1,128)S(1)} %all_to_all.5.tile_ref, f32[16,192,128]{2,1,0:T(8,128)S(1)} %get-tuple-element.91.w_ref), custom_call_target="tpu_custom_call" | custom-call | tf_op jit(solution)/shard_map/scale/pallas_call | solution.py:570
  (7 shorter events, 0.0 us)
Async XLA Ops:
  0.6 9.0 %copy-start.2 = (bf16[2,16,128,192]{2,3,1,0:T(8,128)(2,1)S(1)}, bf16[2,16,128,192]{2,3,1,0:T(8,128)(2,1)}, u32[]{:S(2)}) copy-start(bf16[2,16,128,192]{2,3,1,0:T(8,128)(2,1)} %param.16) | copy-start | bytes 4718596
  0.6 9.0 %copy-start.5 = (f32[2,128]{1,0:T(2,128)S(1)}, f32[2,128]{1,0:T(2,128)}, u32[]{:S(2)}) copy-start(f32[2,128]{1,0:T(2,128)} %constant.2.clone.area_ref) | copy-start | bytes 3076
  4.4 1.5 %collective-permute-start = (bf16[16,16,192]{2,1,0:T(8,128)(2,1)S(1)}, bf16[16,16,192]{2,1,0:T(8,128)(2,1)S(1)}, u32[]{:S(2)}, u32[]{:S(2)}) collective-permute-start(bf16[16,16,192]{2,1,0:T(8,128)(2,1)S(1)} %get-tuple-element.51), channel_id=1, source_target_pairs={{0,1},{1,0},{2,3},{3,2},{4,5},{5,4},{6,7},{7,6},{8,9},{9,8},{10,11... | collective-permute-start | bytes 294920 | tf_op jit(solution)/shard_map/ppermute | solution.py:496
  6.0 11.3 %collective-permute-start.1 = (bf16[3,216,128]{2,1,0:T(8,128)(2,1)S(1)}, bf16[3,216,128]{2,1,0:T(8,128)(2,1)S(1)}, u32[]{:S(2)}, u32[]{:S(2)}) collective-permute-start(bf16[3,216,128]{2,1,0:T(8,128)(2,1)S(1)} %get-tuple-element.57), channel_id=1, source_target_pairs={{0,2},{2,0},{4,6},{6,4},{8,10},{10,8},{12,14},{14,12},{1,3},{3,1},... | collective-permute-start | bytes 497672 | tf_op jit(solution)/shard_map/ppermute | solution.py:505
  8.9 8.4 %collective-permute-start.2 = (bf16[3,216,128]{2,1,0:T(8,128)(2,1)S(1)}, bf16[3,216,128]{2,1,0:T(8,128)(2,1)S(1)}, u32[]{:S(2)}, u32[]{:S(2)}) collective-permute-start(bf16[3,216,128]{2,1,0:T(8,128)(2,1)S(1)} %get-tuple-element.58), channel_id=1, source_target_pairs={{2,4},{4,2},{6,8},{8,6},{10,12},{12,10},{3,5},{5,3},{7,9},{9,7},{1... | collective-permute-start | bytes 497672 | tf_op jit(solution)/shard_map/ppermute | solution.py:504
  9.6 7.7 %copy-start = (bf16[2,192,768]{2,1,0:T(8,128)(2,1)S(1)}, bf16[2,192,768]{2,1,0:T(8,128)(2,1)}, u32[]{:S(2)}) copy-start(bf16[2,192,768]{2,1,0:T(8,128)(2,1)} %rest_4_.5) | copy-start | bytes 1769476
  9.6 7.7 %copy-start.1 = (bf16[2,768,192]{1,2,0:T(8,128)(2,1)S(1)}, bf16[2,768,192]{1,2,0:T(8,128)(2,1)}, u32[]{:S(2)}) copy-start(bf16[2,768,192]{1,2,0:T(8,128)(2,1)} %param.14) | copy-start | bytes 1769476
  9.6 7.7 %copy-start.3 = (f32[2,192]{1,0:T(2,128)S(1)}, f32[2,192]{1,0:T(2,128)}, u32[]{:S(2)}) copy-start(f32[2,192]{1,0:T(2,128)} %rest_3_.5) | copy-start | bytes 4612
  9.6 7.7 %copy-start.4 = (f32[2,192]{1,0:T(2,128)S(1)}, f32[2,192]{1,0:T(2,128)}, u32[]{:S(2)}) copy-start(f32[2,192]{1,0:T(2,128)} %rest_6_.5) | copy-start | bytes 4612
  21.8 1.4 %collective-permute-start.3 = (bf16[16,16,192]{2,1,0:T(8,128)(2,1)S(1)}, bf16[16,16,192]{2,1,0:T(8,128)(2,1)S(1)}, u32[]{:S(2)}, u32[]{:S(2)}) collective-permute-start(bf16[16,16,192]{2,1,0:T(8,128)(2,1)S(1)} %get-tuple-element.65), channel_id=1, source_target_pairs={{0,1},{1,0},{2,3},{3,2},{4,5},{5,4},{6,7},{7,6},{8,9},{9,8},{10,11... | collective-permute-start | bytes 294920 | tf_op jit(solution)/shard_map/ppermute | solution.py:496
  23.3 11.7 %collective-permute-start.4 = (bf16[3,216,128]{2,1,0:T(8,128)(2,1)S(1)}, bf16[3,216,128]{2,1,0:T(8,128)(2,1)S(1)}, u32[]{:S(2)}, u32[]{:S(2)}) collective-permute-start(bf16[3,216,128]{2,1,0:T(8,128)(2,1)S(1)} %get-tuple-element.68), channel_id=1, source_target_pairs={{0,2},{2,0},{4,6},{6,4},{8,10},{10,8},{12,14},{14,12},{1,3},{3,1},... | collective-permute-start | bytes 497672 | tf_op jit(solution)/shard_map/ppermute | solution.py:505
  27.6 7.4 %collective-permute-start.5 = (bf16[3,216,128]{2,1,0:T(8,128)(2,1)S(1)}, bf16[3,216,128]{2,1,0:T(8,128)(2,1)S(1)}, u32[]{:S(2)}, u32[]{:S(2)}) collective-permute-start(bf16[3,216,128]{2,1,0:T(8,128)(2,1)S(1)} %get-tuple-element.69), channel_id=1, source_target_pairs={{2,4},{4,2},{6,8},{8,6},{10,12},{12,10},{3,5},{5,3},{7,9},{9,7},{1... | collective-permute-start | bytes 497672 | tf_op jit(solution)/shard_map/ppermute | solution.py:504
  41.9 1.4 %collective-permute-start.6 = (bf16[16,16,192]{2,1,0:T(8,128)(2,1)S(1)}, bf16[16,16,192]{2,1,0:T(8,128)(2,1)S(1)}, u32[]{:S(2)}, u32[]{:S(2)}) collective-permute-start(bf16[16,16,192]{2,1,0:T(8,128)(2,1)S(1)} %get-tuple-element.73), channel_id=1, source_target_pairs={{0,1},{1,0},{2,3},{3,2},{4,5},{5,4},{6,7},{7,6},{8,9},{9,8},{10,11... | collective-permute-start | bytes 294920 | tf_op jit(solution)/shard_map/ppermute | solution.py:496
  43.4 11.1 %collective-permute-start.7 = (bf16[3,216,128]{2,1,0:T(8,128)(2,1)S(1)}, bf16[3,216,128]{2,1,0:T(8,128)(2,1)S(1)}, u32[]{:S(2)}, u32[]{:S(2)}) collective-permute-start(bf16[3,216,128]{2,1,0:T(8,128)(2,1)S(1)} %get-tuple-element.76), channel_id=1, source_target_pairs={{0,2},{2,0},{4,6},{6,4},{8,10},{10,8},{12,14},{14,12},{1,3},{3,1},... | collective-permute-start | bytes 497672 | tf_op jit(solution)/shard_map/ppermute | solution.py:505
  47.2 7.4 %collective-permute-start.8 = (bf16[3,216,128]{2,1,0:T(8,128)(2,1)S(1)}, bf16[3,216,128]{2,1,0:T(8,128)(2,1)S(1)}, u32[]{:S(2)}, u32[]{:S(2)}) collective-permute-start(bf16[3,216,128]{2,1,0:T(8,128)(2,1)S(1)} %get-tuple-element.77), channel_id=1, source_target_pairs={{2,4},{4,2},{6,8},{8,6},{10,12},{12,10},{3,5},{5,3},{7,9},{9,7},{1... | collective-permute-start | bytes 497672 | tf_op jit(solution)/shard_map/ppermute | solution.py:504
  58.6 1.4 %collective-permute-start.9 = (bf16[16,16,192]{2,1,0:T(8,128)(2,1)S(1)}, bf16[16,16,192]{2,1,0:T(8,128)(2,1)S(1)}, u32[]{:S(2)}, u32[]{:S(2)}) collective-permute-start(bf16[16,16,192]{2,1,0:T(8,128)(2,1)S(1)} %get-tuple-element.82), channel_id=1, source_target_pairs={{0,1},{1,0},{2,3},{3,2},{4,5},{5,4},{6,7},{7,6},{8,9},{9,8},{10,11... | collective-permute-start | bytes 294920 | tf_op jit(solution)/shard_map/ppermute | solution.py:496
  60.1 10.8 %collective-permute-start.10 = (bf16[3,216,128]{2,1,0:T(8,128)(2,1)S(1)}, bf16[3,216,128]{2,1,0:T(8,128)(2,1)S(1)}, u32[]{:S(2)}, u32[]{:S(2)}) collective-permute-start(bf16[3,216,128]{2,1,0:T(8,128)(2,1)S(1)} %get-tuple-element.85), channel_id=1, source_target_pairs={{0,2},{2,0},{4,6},{6,4},{8,10},{10,8},{12,14},{14,12},{1,3},{3,1},... | collective-permute-start | bytes 497672 | tf_op jit(solution)/shard_map/ppermute | solution.py:505
  63.5 7.4 %collective-permute-start.11 = (bf16[3,216,128]{2,1,0:T(8,128)(2,1)S(1)}, bf16[3,216,128]{2,1,0:T(8,128)(2,1)S(1)}, u32[]{:S(2)}, u32[]{:S(2)}) collective-permute-start(bf16[3,216,128]{2,1,0:T(8,128)(2,1)S(1)} %get-tuple-element.86), channel_id=1, source_target_pairs={{2,4},{4,2},{6,8},{8,6},{10,12},{12,10},{3,5},{5,3},{7,9},{9,7},{1... | collective-permute-start | bytes 497672 | tf_op jit(solution)/shard_map/ppermute | solution.py:504

commit v6 on v5

--- a/solution.py
+++ b/solution.py
@@ -13,6 +13,7 @@
 BF16 = jnp.bfloat16
 LAT_SPAN = 70.0 * math.pi / 180.0
 MARGIN = 8
+EARLY = 2
 EXT = 16
 VMEM = pltpu.VMEM
 ACROSS = (((1,), (1,)), ((), ()))
@@ -47,7 +48,43 @@
                     k1[layer, flipped, a * 7 + b] = jnp.concatenate(pair, axis=1)
 
 
-def planes_kernel(f_ref, x0, x1):
+def tap_tile(k0, k1, layer, flipped, rows, out_ref, base, low_window, high_window):
+    half = rows // 2
+    acc = [None] * rows
+    for b in range(7):
+        taps = [k0[layer, tap_index(a, b, flipped)] for a in range(7)]
+        for r in range(rows):
+            x = low_window(r, b)
+            for a in range(7):
+                o = r + 3 - a
+                if 0 <= o < rows:
+                    term = taps[a] * x
+                    acc[o] = term if acc[o] is None else acc[o] + term
+    for o in range(rows):
+        out_ref[o, pl.ds(base, 8), :128] = acc[o]
+    acc = [None] * half
+    for b in range(7):
+        taps = [k1[layer, int(flipped), a * 7 + b] for a in range(7)]
+        for q in range(half + 3):
+            x = high_window(q, b)
+            for a in range(7):
+                o = q + 3 - a
+                if 0 <= o < half:
+                    term = taps[a] * x
+                    acc[o] = term if acc[o] is None else acc[o] + term
+    for o in range(half):
+        out_ref[o, pl.ds(base, 8), 128:] = acc[o][:, :64]
+        out_ref[rows - 1 - o, pl.ds(base, 8), 128:] = acc[o][:, 64:]
+
+
+def plane_windows(x0, x1, base):
+    return (
+        lambda r, b: x0[r, pl.ds(base + (b - 3), 8), :],
+        lambda q, b: x1[q, pl.ds(base + (b - 3), 8), :],
+    )
+
+
+def planes_kernel(layer, flipped, f_ref, k0, k1, x0, x1, early_ref):
     rows = f_ref.shape[0]
     half = rows // 2
 
@@ -61,8 +98,13 @@
             x0[rows - 1 - q] = high[:, :128]
         x1[q] = jnp.concatenate([low[:, 128:], high[:, 128:]], axis=1)
 
-
-def conv_local(x0, x1, lon_ref, k0, k1, layer, out_ref, e0, e1, flipped, beside=None):
+    @pl.loop(0, EARLY)
+    def _(j):
+        base = pl.multiple_of(j * 8, 8)
+        tap_tile(k0, k1, layer, flipped, rows, early_ref, base, *plane_windows(x0, x1, base + 8))
+
+
+def conv_local(x0, x1, early_ref, lon_ref, k0, k1, layer, out_ref, e0, e1, flipped, beside=None):
     rows, cols, _ = out_ref.shape
     half = rows // 2
 
@@ -78,35 +120,8 @@
         low, high = lon_ref[q, :, 128:].astype(F32), lon_ref[rows - 1 - q, :, 128:].astype(F32)
         ends(e1, q, x1, jnp.concatenate([low, high], axis=1))
 
-    def tile(base, low_window, high_window):
-        acc = [None] * rows
-        for b in range(7):
-            taps = [k0[layer, tap_index(a, b, flipped)] for a in range(7)]
-            for r in range(rows):
-                x = low_window(r, b)
-                for a in range(7):
-                    o = r + 3 - a
-                    if 0 <= o < rows:
-                        term = taps[a] * x
-                        acc[o] = term if acc[o] is None else acc[o] + term
-        for o in range(rows):
-            out_ref[o, pl.ds(base, 8), :128] = acc[o]
-        acc = [None] * half
-        for b in range(7):
-            taps = [k1[layer, int(flipped), a * 7 + b] for a in range(7)]
-            for q in range(half + 3):
-                x = high_window(q, b)
-                for a in range(7):
-                    o = q + 3 - a
-                    if 0 <= o < half:
-                        term = taps[a] * x
-                        acc[o] = term if acc[o] is None else acc[o] + term
-        for o in range(half):
-            out_ref[o, pl.ds(base, 8), 128:] = acc[o][:, :64]
-            out_ref[rows - 1 - o, pl.ds(base, 8), 128:] = acc[o][:, 64:]
-
     def both(j, *windows):
-        tile(pl.multiple_of(j * 8, 8), *windows)
+        tap_tile(k0, k1, layer, flipped, rows, out_ref, pl.multiple_of(j * 8, 8), *windows)
         if beside is not None:
             beside(j)
 
@@ -120,12 +135,15 @@
             lambda q, b: e1[s, q, MARGIN - 3 + b : 2 * MARGIN - 3 + b, :],
         )
 
-    @pl.loop(1, last)
+    for r in range(rows):
+        out_ref[r, 8 : 8 + 8 * EARLY, :] = early_ref[r]
+    if beside is not None:
+        for j in range(1, 1 + EARLY):
+            beside(j)
+
+    @pl.loop(1 + EARLY, last)
     def _(j):
-        base = pl.multiple_of(j * 8, 8)
-        both(
-            j, lambda r, b: x0[r, pl.ds(base + (b - 3), 8), :], lambda q, b: x1[q, pl.ds(base + (b - 3), 8), :]
-        )
+        both(j, *plane_windows(x0, x1, pl.multiple_of(j * 8, 8)))
 
 
 def conv_scratch(rows):
@@ -135,12 +153,12 @@
     ]
 
 
-def conv_kernel(layer, flipped, x0, x1, lon_ref, k0, k1, out_ref, *scratch):
-    conv_local(x0, x1, lon_ref, k0, k1, layer, out_ref, *scratch, flipped)
+def conv_kernel(layer, flipped, x0, x1, early_ref, lon_ref, k0, k1, out_ref, *scratch):
+    conv_local(x0, x1, early_ref, lon_ref, k0, k1, layer, out_ref, *scratch, flipped)
 
 
 def first_conv_kernel(
-    area_ref, f_ref, x0, x1, lon_ref, k0, k1, turned_ref, slope_hbm, out_ref, sum_ref, normed_out, slope_out, e0, e1, sems
+    area_ref, f_ref, x0, x1, early_ref, lon_ref, k0, k1, turned_ref, slope_hbm, out_ref, sum_ref, normed_out, slope_out, e0, e1, sems
 ):
     rows, cols, _ = f_ref.shape
     start = lax.axis_index("lat") * rows
@@ -171,7 +189,7 @@
         else:
             pl.when(j < rows)(lambda: turn_row(j))
 
-    conv_local(x0, x1, lon_ref, k0, k1, 0, out_ref, e0, e1, False, beside)
+    conv_local(x0, x1, early_ref, lon_ref, k0, k1, 0, out_ref, e0, e1, False, beside)
     for fetch in fetches:
         fetch.wait()
 
@@ -492,14 +510,19 @@
             name=name,
         )(*args)
 
-    def exchange(field, lon, send_a, send_b):
+    def exchange(layer, flipped, field, lon, send_a, send_b):
         side = lax.ppermute(lon, "lon", swap_lon)
         planes = call(
-            planes_kernel, [VMEM((rows, cols, 128), F32), VMEM((rows // 2 + 3, cols, 128), F32)], [IN_VMEM], (field,),
+            functools.partial(planes_kernel, layer, flipped),
+            [
+                VMEM((rows, cols, 128), F32), VMEM((rows // 2 + 3, cols, 128), F32),
+                VMEM((rows, 8 * EARLY, chans), F32),
+            ],
+            [IN_VMEM] * 3, (field, k0, k1),
             flops=conv_flops // 8, name="planes",
         )
         send_a, send_b = call(
-            extend_kernel, [send_shape] * 2, [IN_VMEM] * 4, (planes[1], side, send_a, send_b), name="extend"
+            extend_kernel, [send_shape] * 2, [IN_VMEM] * 4, (planes[2], side, send_a, send_b), name="extend"
         )
         halo_b = lax.ppermute(send_b, "lat", swap_b)
         halo_a = lax.ppermute(send_a, "lat", swap_a)
@@ -523,11 +546,11 @@
         ],
         name="edges",
     )
-    taken, halo_a, halo_b = exchange(tangent, lon, send_a, send_b)
+    taken, halo_a, halo_b = exchange(0, False, tangent, lon, send_a, send_b)
     acc, vv, normed_cells, slope_cells = call(
         first_conv_kernel,
         [full32, sums, VMEM((layers, rows, cols, chans), BF16), VMEM(slope.shape, BF16)],
-        [IN_SMEM] + [IN_VMEM] * 7 + [IN_HBM],
+        [IN_SMEM] + [IN_VMEM] * 8 + [IN_HBM],
         (area, tangent, *taken, k0, k1, jnp.transpose(normed, (0, 1, 3, 2)), slope),
         kscr + [pltpu.SemaphoreType.DMA((layers,))], conv_flops, "conv_first",
     )
@@ -544,15 +567,15 @@
             grad, back, uu = got[:3]
         else:
             tangent = got[0]
-        taken, halo_a, halo_b = exchange(back if last else tangent, *got[-3:])
+        taken, halo_a, halo_b = exchange(layer + (not last), last, back if last else tangent, *got[-3:])
         if not last:
             (acc,) = call(
-                functools.partial(conv_kernel, layer + 1, False), [full32], [IN_VMEM] * 5, (*taken, k0, k1),
+                functools.partial(conv_kernel, layer + 1, False), [full32], [IN_VMEM] * 6, (*taken, k0, k1),
                 kscr, conv_flops, f"conv{layer + 1}",
             )
     for layer in range(layers - 1, -1, -1):
         (acc,) = call(
-            functools.partial(conv_kernel, layer, True), [full32], [IN_VMEM] * 5, (*taken, k0, k1),
+            functools.partial(conv_kernel, layer, True), [full32], [IN_VMEM] * 6, (*taken, k0, k1),
             kscr, conv_flops, f"convt{layer}",
         )
         if layer > 0:
@@ -560,7 +583,7 @@
                 functools.partial(adjoint_kernel, layer - 1), [full32, full16, lon_shape, send_shape, send_shape],
                 [IN_VMEM] * 13, (acc, halo_a, halo_b, k0, k1, grad) + net, hscr, net_flops, f"adjoint{layer - 1}",
             )
-            taken, halo_a, halo_b = exchange(back, lon, send_a, send_b)
+            taken, halo_a, halo_b = exchange(layer - 1, True, back, lon, send_a, send_b)
     members = lat_size * lon_size
     w, tile = call(
         final_kernel, [VMEM((rows, chans, cols), F32), VMEM((members, 1, 128), F32)], [IN_SMEM] + [IN_VMEM] * 8,

time: 86.2 us -> 84.4 us (0.979)
  starting transfers between devices: 17.9 us -> 16.5 us
    ppermute x4, waiting for transfers between devices: 4.14 us -> 1.23 us  [exchange(): side = lax.ppermute(lon, 'lon', swap_lon)]
    ppermute x4, waiting for transfers between devices: 2.17 us -> 4.22 us  [exchange(): halo_a = lax.ppermute(send_a, 'lat', swap_a)]
    ppermute x4, starting transfers between devices: 14.4 us -> 13 us  [exchange(): halo_a = lax.ppermute(send_a, 'lat', swap_a)]
  transfers between devices with their start and end apart: 12 -> 12, of which waited for: 7 -> 6; matrix products, arithmetic and copies ran while one was open for 0% -> 0% of each run, Pallas kernels for 31% -> 32%
where the time goes in v6:
time: 84.4 us; the launch traced here: 84.1 us
  Pallas kernels  49.8 us (59%)
  starting transfers between devices  16.5 us (20%)
  blocking collectives  11.2 us (13%)
  waiting for transfers between devices  5.46 us (6%)
  between operations  1.04 us (1%)
    pallas_call x17, Pallas kernels, call(): pl.pallas_call(kernel, out_shape=out_shape, in_specs=in_specs, out_specs=...  47.9 us
    ppermute x4, starting transfers between devices, exchange(): halo_a = lax.ppermute(send_a, 'lat', swap_a)  13 us
    all_to_all x1, blocking collectives, on_device(): tile = lax.all_to_all(tile, ('lat', 'lon'), 0, 0, tiled=True)  11.2 us
    ppermute x4, waiting for transfers between devices, exchange(): halo_a = lax.ppermute(send_a, 'lat', swap_a)  4.22 us
    ppermute x4, starting transfers between devices, exchange(): halo_b = lax.ppermute(send_b, 'lat', swap_b)  2.82 us
    pallas_call x1, Pallas kernels, on_device(): pl.pallas_call(functools.partial(scale_kernel, total), out_shape=[jax.Sha...  1.88 us
  transfers between devices with their start and end apart: 12, of which 6 were waited for; matrix products, arithmetic and copies ran while one was open for 0% of the time, Pallas kernels for 32%

profile of v6, /device:TPU:0, one launch (start us, length us, event | category | flops | bytes accessed | tf_op | source)
XLA Modules:
  0.0 84.1 jit_solution(4401247447682670760)
XLA Ops:
  0.6 3.7 %edges.1 = (f32[16,128,192]{2,1,0:T(8,128)S(1)}, bf16[16,16,192]{2,1,0:T(8,128)(2,1)S(1)}, bf16[3,216,128]{2,1,0:T(8,128)(2,1)S(1)}, bf16[3,216,128]{2,1,0:T(8,1...) custom-call(f32[16,192,128]{2,1,0:T(8,128)} %bitcast.11, ...), custom_call_target="tpu_custom_call" | custom-call | bytes 4000000 | tf_op jit(solution)/shard_map/edges/pallas_call | solution.py:502
  4.3 0.0 copy-start.2
  4.3 0.0 copy-start.5
  4.3 0.5 collective-permute-start
  4.8 1.0 %planes.4 = (f32[16,128,128]{2,1,0:T(8,128)S(1)}, f32[11,128,128]{2,1,0:T(8,128)S(1)}, f32[16,16,192]{2,1,0:T(8,128)S(1)}) custom-call(f32[16,128,192]{2,1,0:T(8,128)S(1)} %get-tuple-element.52.f_ref.t_ref, f32[2,49,8,128]{3,2,1,0:T(8,128)S(1)} %get-tuple-element.53.k0, f32[2,2,49,8,128]{4,3,2,1,0:T(8,128)S(1)} %get-tuple-element.54.k1), custom_call_target="tpu_custom_call" | custom-call | flops 4816896 | bytes 4000000 | tf_op jit(solution)/shard_map/planes/pallas_call | solution.py:502
  5.8 0.0 collective-permute-done.lon_ref
  5.8 0.1 extend.4
  5.9 2.9 %collective-permute-start.1 = (bf16[3,216,128]{2,1,0:T(8,128)(2,1)S(1)}, bf16[3,216,128]{2,1,0:T(8,128)(2,1)S(1)}, u32[]{:S(2)}, u32[]{:S(2)}) collective-permute-start(bf16[3,216,128]{2,1,0:T(8,128)(2,1)S(1)} %get-tuple-element.62), channel_id=1, source_target_pairs={{0,2},{2,0},{4,6},{6,4},{8,10},{10,8},{12,14},{14,12},{1,3},{3,1},... | collective-permute-start | bytes 497672 | tf_op jit(solution)/shard_map/ppermute | solution.py:528
  8.8 0.7 collective-permute-start.2
  9.5 0.0 copy-start
  9.5 0.0 copy-start.1
  9.5 0.0 copy-start.3
  9.5 0.0 copy-start.4
  9.5 7.1 %conv_first.1 = (f32[16,128,192]{2,1,0:T(8,128)S(1)}, f32[1,192]{1,0:T(1,128)S(1)}, bf16[2,16,128,192]{3,2,1,0:T(8,128)(2,1)S(1)}, bf16[2,16,128,768]{3,2,1,0:T(8,128)(2,1)S(1)}) custom-call(f32[2,128]{1,0:T(2,128)S(1)} %copy-done.5, f32[16,128,192]{2,1,0:T(8,128)S(1)} %get-tuple-element.52.f_ref.t_ref, f32[16,128,128]{2,1,0:T(8,128)S(1)} %get-tuple-element.55.x0, ...), custom_call_target="tpu_custom_call" | custom-call | flops 38535168 | bytes 4000000 | tf_op jit(solution)/shard_map/conv_first/pallas_call | solution.py:502
  16.7 0.0 collective-permute-done.1.a_ref
  16.7 0.0 collective-permute-done.2.b_ref
  16.7 4.3 %tangent0.1 = (f32[16,128,192]{2,1,0:T(8,128)S(1)}, bf16[16,16,192]{2,1,0:T(8,128)(2,1)S(1)}, bf16[3,216,128]{2,1,0:T(8,128)(2,1)S(1)}, bf16[3,216,128]{2,1,0:T(8,128)(2,1)S(1)}) custom-call(f32[2,128]{1,0:T(2,128)S(1)} %copy-done.5, f32[16,128,192]{2,1,0:T(8,128)S(1)} %get-tuple-element.59.acc_ref, bf16[3,216,128]{2,1,0:T(8,128)(2,1)S(1)} %collective-permute-done.1.a_ref, ...), custom_call_target="tpu_custom_call" | custom-call | flops 1207959552 | bytes 4000000 | tf_op jit(solution)/shard_map/tangent0/pallas_call | solution.py:502
  21.0 0.1 collective-permute-start.3
  21.1 1.0 %planes.5 = (f32[16,128,128]{2,1,0:T(8,128)S(1)}, f32[11,128,128]{2,1,0:T(8,128)S(1)}, f32[16,16,192]{2,1,0:T(8,128)S(1)}) custom-call(f32[16,128,192]{2,1,0:T(8,128)S(1)} %get-tuple-element.67.f_ref.t_ref, f32[2,49,8,128]{3,2,1,0:T(8,128)S(1)} %get-tuple-element.53.k0, f32[2,2,49,8,128]{4,3,2,1,0:T(8,128)S(1)} %get-tuple-element.54.k1), custom_call_target="tpu_custom_call" | custom-call | flops 4816896 | bytes 4000000 | tf_op jit(solution)/shard_map/planes/pallas_call | solution.py:502
  22.0 0.4 collective-permute-done.3.lon_ref
  22.4 0.1 extend.5
  22.5 4.3 %collective-permute-start.4 = (bf16[3,216,128]{2,1,0:T(8,128)(2,1)S(1)}, bf16[3,216,128]{2,1,0:T(8,128)(2,1)S(1)}, u32[]{:S(2)}, u32[]{:S(2)}) collective-permute-start(bf16[3,216,128]{2,1,0:T(8,128)(2,1)S(1)} %get-tuple-element.74), channel_id=1, source_target_pairs={{0,2},{2,0},{4,6},{6,4},{8,10},{10,8},{12,14},{14,12},{1,3},{3,1},... | collective-permute-start | bytes 497672 | tf_op jit(solution)/shard_map/ppermute | solution.py:528
  26.8 0.8 collective-permute-start.5
  27.6 5.2 %conv1.1.acc_ref = f32[16,128,192]{2,1,0:T(8,128)S(1)} custom-call(f32[16,128,128]{2,1,0:T(8,128)S(1)} %get-tuple-element.68.x0, f32[11,128,128]{2,1,0:T(8,128)S(1)} %get-tuple-element.69.x1, f32[16,16,192]{2,1,0:T(8,128)S(1)} %get-tuple-element.70.early_ref.after_ref, bf16[16,16,192]{2,1,0:T(8,128)(2,1)S(1)} %collective-permute-done.3.lon_ref, ...), custom_call_target="tpu_custom_call" | custom-call | flops 38535168 | bytes 4000000 | tf_op jit(solution)/shard_map/conv1/pallas_call | solution.py:502
  32.9 1.3 %collective-permute-done.4.a_ref = bf16[3,216,128]{2,1,0:T(8,128)(2,1)S(1)} collective-permute-done((bf16[3,216,128]{2,1,0:T(8,128)(2,1)S(1)}, bf16[3,216,128]{2,1,0:T(8,128)(2,1)S(1)}, u32[]{:S(2)}, u32[]{:S(2)}) %collective-permute-start.4) | collective-permute-done | bytes 165920 | tf_op jit(solution)/shard_map/ppermute | solution.py:528
  34.2 0.0 collective-permute-done.5.b_ref
  34.2 6.6 %tangent1.1 = (f32[16,128,192]{2,1,0:T(8,128)S(1)}, bf16[16,128,192]{2,1,0:T(8,128)(2,1)S(1)}, f32[1,192]{1,0:T(1,128)S(1)}, bf16[16,16,192]{2,1,0:T(8,128)(2,1)...) custom-call(f32[2,128]{1,0:T(2,128)S(1)} %copy-done.5, f32[16,128,192]{2,1,0:T(8,128)S(1)} %conv1.1.acc_ref, ...), custom_call_target="tpu_custom_call" | custom-call | flops 1207959552 | bytes 4000000 | tf_op jit(solution)/shard_map/tangent1/pallas_call | solution.py:502
  40.8 0.1 collective-permute-start.6
  40.9 0.9 %planes.6 = (f32[16,128,128]{2,1,0:T(8,128)S(1)}, f32[11,128,128]{2,1,0:T(8,128)S(1)}, f32[16,16,192]{2,1,0:T(8,128)S(1)}) custom-call(bf16[16,128,192]{2,1,0:T(8,128)(2,1)S(1)} %get-tuple-element.76.f_ref, f32[2,49,8,128]{3,2,1,0:T(8,128)S(1)} %get-tuple-element.53.k0, f32[2,2,49,8,128]{4,3,2,1,0:T(8,128)S(1)} %get-tuple-element.54.k1), custom_call_target="tpu_custom_call" | custom-call | flops 4816896 | bytes 4000000 | tf_op jit(solution)/shard_map/planes/pallas_call | solution.py:502
  41.8 0.4 collective-permute-done.6.lon_ref
  42.2 0.1 extend.6
  42.3 3.0 %collective-permute-start.7 = (bf16[3,216,128]{2,1,0:T(8,128)(2,1)S(1)}, bf16[3,216,128]{2,1,0:T(8,128)(2,1)S(1)}, u32[]{:S(2)}, u32[]{:S(2)}) collective-permute-start(bf16[3,216,128]{2,1,0:T(8,128)(2,1)S(1)} %get-tuple-element.83), channel_id=1, source_target_pairs={{0,2},{2,0},{4,6},{6,4},{8,10},{10,8},{12,14},{14,12},{1,3},{3,1},... | collective-permute-start | bytes 497672 | tf_op jit(solution)/shard_map/ppermute | solution.py:528
  45.3 0.7 collective-permute-start.8
  46.0 5.3 %convt1.1.acc_ref = f32[16,128,192]{2,1,0:T(8,128)S(1)} custom-call(f32[16,128,128]{2,1,0:T(8,128)S(1)} %get-tuple-element.77.x0, f32[11,128,128]{2,1,0:T(8,128)S(1)} %get-tuple-element.78.x1, f32[16,16,192]{2,1,0:T(8,128)S(1)} %get-tuple-element.79.early_ref.after_ref, bf16[16,16,192]{2,1,0:T(8,128)(2,1)S(1)} %collective-permute-done.6.lon_ref, ...), custom_call_target="tpu_custom_call" | custom-call | flops 38535168 | bytes 4000000 | tf_op jit(solution)/shard_map/convt1/pallas_call | solution.py:502
  51.2 1.5 %collective-permute-done.7.a_ref = bf16[3,216,128]{2,1,0:T(8,128)(2,1)S(1)} collective-permute-done((bf16[3,216,128]{2,1,0:T(8,128)(2,1)S(1)}, bf16[3,216,128]{2,1,0:T(8,128)(2,1)S(1)}, u32[]{:S(2)}, u32[]{:S(2)}) %collective-permute-start.7) | collective-permute-done | bytes 165920 | tf_op jit(solution)/shard_map/ppermute | solution.py:528
  52.7 0.0 collective-permute-done.8.b_ref
  52.7 3.9 %adjoint0.1 = (f32[16,128,192]{2,1,0:T(8,128)S(1)}, bf16[16,128,192]{2,1,0:T(8,128)(2,1)S(1)}, bf16[16,16,192]{2,1,0:T(8,128)(2,1)S(1)}, bf16[3,216,128]{2,1,0:T(8,128)(2,1)S(1)}, bf16[3,216,128]{2,1,0:T(8,128)(2,1)S(1)}) custom-call(f32[16,128,192]{2,1,0:T(8,128)S(1)} %convt1.1.acc_ref, bf16[3,216,128]{2,1,0:T(8,128)(2,1)S(1)} %collective-permute-done.7.a_ref, ...), custom_call_target="tpu_custom_call" | custom-call | flops 1207959552 | bytes 4000000 | tf_op jit(solution)/shard_map/adjoint0/pallas_call | solution.py:502
  56.6 0.1 collective-permute-start.9
  56.7 0.9 %planes.7 = (f32[16,128,128]{2,1,0:T(8,128)S(1)}, f32[11,128,128]{2,1,0:T(8,128)S(1)}, f32[16,16,192]{2,1,0:T(8,128)S(1)}) custom-call(bf16[16,128,192]{2,1,0:T(8,128)(2,1)S(1)} %get-tuple-element.86.f_ref, f32[2,49,8,128]{3,2,1,0:T(8,128)S(1)} %get-tuple-element.53.k0, f32[2,2,49,8,128]{4,3,2,1,0:T(8,128)S(1)} %get-tuple-element.54.k1), custom_call_target="tpu_custom_call" | custom-call | flops 4816896 | bytes 4000000 | tf_op jit(solution)/shard_map/planes/pallas_call | solution.py:502
  57.6 0.4 collective-permute-done.9.lon_ref
  58.0 0.1 extend.7
  58.1 2.8 %collective-permute-start.10 = (bf16[3,216,128]{2,1,0:T(8,128)(2,1)S(1)}, bf16[3,216,128]{2,1,0:T(8,128)(2,1)S(1)}, u32[]{:S(2)}, u32[]{:S(2)}) collective-permute-start(bf16[3,216,128]{2,1,0:T(8,128)(2,1)S(1)} %get-tuple-element.93), channel_id=1, source_target_pairs={{0,2},{2,0},{4,6},{6,4},{8,10},{10,8},{12,14},{14,12},{1,3},{3,1},... | collective-permute-start | bytes 497672 | tf_op jit(solution)/shard_map/ppermute | solution.py:528
  61.0 0.7 collective-permute-start.11
  61.6 5.2 %convt0.1.acc_ref = f32[16,128,192]{2,1,0:T(8,128)S(1)} custom-call(f32[16,128,128]{2,1,0:T(8,128)S(1)} %get-tuple-element.87.x0, f32[11,128,128]{2,1,0:T(8,128)S(1)} %get-tuple-element.88.x1, f32[16,16,192]{2,1,0:T(8,128)S(1)} %get-tuple-element.89.early_ref.after_ref, bf16[16,16,192]{2,1,0:T(8,128)(2,1)S(1)} %collective-permute-done.9.lon_ref, ...), custom_call_target="tpu_custom_call" | custom-call | flops 38535168 | bytes 4000000 | tf_op jit(solution)/shard_map/convt0/pallas_call | solution.py:502
  66.9 1.5 %collective-permute-done.10.a_ref = bf16[3,216,128]{2,1,0:T(8,128)(2,1)S(1)} collective-permute-done((bf16[3,216,128]{2,1,0:T(8,128)(2,1)S(1)}, bf16[3,216,128]{2,1,0:T(8,128)(2,1)S(1)}, u32[]{:S(2)}, u32[]{:S(2)}) %collective-permute-start.10) | collective-permute-done | bytes 165920 | tf_op jit(solution)/shard_map/ppermute | solution.py:528
  68.3 2.5 %final.1 = (f32[16,192,128]{2,1,0:T(8,128)S(1)}, f32[16,1,128]{2,1,0:T(1,128)S(1)}) custom-call(f32[2,128]{1,0:T(2,128)S(1)} %copy-done.5, f32[16,128,192]{2,1,0:T(8,128)S(1)} %convt0.1.acc_ref, bf16[3,216,128]{2,1,0:T(8,128)(2,1)S(1)} %collective-permute-done.10.a_ref, bf16[3,216,128]{2,1,0:T(8,128)(2,1)S(1)} %collective-permute-done.11.b_ref, ...), custom_call_target="tpu_custom_call" | custom-call | bytes 4000000 | tf_op jit(solution)/shard_map/final/pallas_call | solution.py:502
  70.9 11.2 %all_to_all.5.tile_ref = f32[16,1,128]{2,1,0:T(1,128)S(1)} all-to-all(f32[16,1,128]{2,1,0:T(1,128)S(1)} %get-tuple-element.98), channel_id=1, replica_groups=mesh['grp'=2,'lat'=8,'lon'=2] {'lat','lon'}, dimensions={0} | all-to-all | bytes 16384 | tf_op jit(solution)/shard_map/all_to_all | solution.py:592
  82.0 1.9 %scale.1 = (f32[16,192,128]{2,1,0:T(8,128)}, f32[1,128]{1,0:T(1,128)}) custom-call(f32[16,1,128]{2,1,0:T(1,128)S(1)} %all_to_all.5.tile_ref, f32[16,192,128]{2,1,0:T(8,128)S(1)} %get-tuple-element.99.w_ref), custom_call_target="tpu_custom_call" | custom-call | tf_op jit(solution)/shard_map/scale/pallas_call | solution.py:593
  (7 shorter events, 0.0 us)
Async XLA Ops:
  4.3 5.2 %copy-start.2 = (bf16[2,16,128,192]{2,3,1,0:T(8,128)(2,1)S(1)}, bf16[2,16,128,192]{2,3,1,0:T(8,128)(2,1)}, u32[]{:S(2)}) copy-start(bf16[2,16,128,192]{2,3,1,0:T(8,128)(2,1)} %param.16) | copy-start | bytes 4718596
  4.3 5.2 %copy-start.5 = (f32[2,128]{1,0:T(2,128)S(1)}, f32[2,128]{1,0:T(2,128)}, u32[]{:S(2)}) copy-start(f32[2,128]{1,0:T(2,128)} %constant.2.clone.area_ref) | copy-start | bytes 3076
  4.3 1.5 %collective-permute-start = (bf16[16,16,192]{2,1,0:T(8,128)(2,1)S(1)}, bf16[16,16,192]{2,1,0:T(8,128)(2,1)S(1)}, u32[]{:S(2)}, u32[]{:S(2)}) collective-permute-start(bf16[16,16,192]{2,1,0:T(8,128)(2,1)S(1)} %get-tuple-element.58), channel_id=1, source_target_pairs={{0,1},{1,0},{2,3},{3,2},{4,5},{5,4},{6,7},{7,6},{8,9},{9,8},{10,11... | collective-permute-start | bytes 294920 | tf_op jit(solution)/shard_map/ppermute | solution.py:514
  5.9 10.7 %collective-permute-start.1 = (bf16[3,216,128]{2,1,0:T(8,128)(2,1)S(1)}, bf16[3,216,128]{2,1,0:T(8,128)(2,1)S(1)}, u32[]{:S(2)}, u32[]{:S(2)}) collective-permute-start(bf16[3,216,128]{2,1,0:T(8,128)(2,1)S(1)} %get-tuple-element.62), channel_id=1, source_target_pairs={{0,2},{2,0},{4,6},{6,4},{8,10},{10,8},{12,14},{14,12},{1,3},{3,1},... | collective-permute-start | bytes 497672 | tf_op jit(solution)/shard_map/ppermute | solution.py:528
  8.8 7.9 %collective-permute-start.2 = (bf16[3,216,128]{2,1,0:T(8,128)(2,1)S(1)}, bf16[3,216,128]{2,1,0:T(8,128)(2,1)S(1)}, u32[]{:S(2)}, u32[]{:S(2)}) collective-permute-start(bf16[3,216,128]{2,1,0:T(8,128)(2,1)S(1)} %get-tuple-element.63), channel_id=1, source_target_pairs={{2,4},{4,2},{6,8},{8,6},{10,12},{12,10},{3,5},{5,3},{7,9},{9,7},{1... | collective-permute-start | bytes 497672 | tf_op jit(solution)/shard_map/ppermute | solution.py:527
  9.5 7.2 %copy-start = (bf16[2,192,768]{2,1,0:T(8,128)(2,1)S(1)}, bf16[2,192,768]{2,1,0:T(8,128)(2,1)}, u32[]{:S(2)}) copy-start(bf16[2,192,768]{2,1,0:T(8,128)(2,1)} %rest_4_.5) | copy-start | bytes 1769476
  9.5 7.2 %copy-start.1 = (bf16[2,768,192]{1,2,0:T(8,128)(2,1)S(1)}, bf16[2,768,192]{1,2,0:T(8,128)(2,1)}, u32[]{:S(2)}) copy-start(bf16[2,768,192]{1,2,0:T(8,128)(2,1)} %param.14) | copy-start | bytes 1769476
  9.5 7.2 %copy-start.3 = (f32[2,192]{1,0:T(2,128)S(1)}, f32[2,192]{1,0:T(2,128)}, u32[]{:S(2)}) copy-start(f32[2,192]{1,0:T(2,128)} %rest_3_.5) | copy-start | bytes 4612
  9.5 7.2 %copy-start.4 = (f32[2,192]{1,0:T(2,128)S(1)}, f32[2,192]{1,0:T(2,128)}, u32[]{:S(2)}) copy-start(f32[2,192]{1,0:T(2,128)} %rest_6_.5) | copy-start | bytes 4612
  21.0 1.4 %collective-permute-start.3 = (bf16[16,16,192]{2,1,0:T(8,128)(2,1)S(1)}, bf16[16,16,192]{2,1,0:T(8,128)(2,1)S(1)}, u32[]{:S(2)}, u32[]{:S(2)}) collective-permute-start(bf16[16,16,192]{2,1,0:T(8,128)(2,1)S(1)} %get-tuple-element.71), channel_id=1, source_target_pairs={{0,1},{1,0},{2,3},{3,2},{4,5},{5,4},{6,7},{7,6},{8,9},{9,8},{10,11... | collective-permute-start | bytes 294920 | tf_op jit(solution)/shard_map/ppermute | solution.py:514
  22.5 11.7 %collective-permute-start.4 = (bf16[3,216,128]{2,1,0:T(8,128)(2,1)S(1)}, bf16[3,216,128]{2,1,0:T(8,128)(2,1)S(1)}, u32[]{:S(2)}, u32[]{:S(2)}) collective-permute-start(bf16[3,216,128]{2,1,0:T(8,128)(2,1)S(1)} %get-tuple-element.74), channel_id=1, source_target_pairs={{0,2},{2,0},{4,6},{6,4},{8,10},{10,8},{12,14},{14,12},{1,3},{3,1},... | collective-permute-start | bytes 497672 | tf_op jit(solution)/shard_map/ppermute | solution.py:528
  26.8 7.4 %collective-permute-start.5 = (bf16[3,216,128]{2,1,0:T(8,128)(2,1)S(1)}, bf16[3,216,128]{2,1,0:T(8,128)(2,1)S(1)}, u32[]{:S(2)}, u32[]{:S(2)}) collective-permute-start(bf16[3,216,128]{2,1,0:T(8,128)(2,1)S(1)} %get-tuple-element.75), channel_id=1, source_target_pairs={{2,4},{4,2},{6,8},{8,6},{10,12},{12,10},{3,5},{5,3},{7,9},{9,7},{1... | collective-permute-start | bytes 497672 | tf_op jit(solution)/shard_map/ppermute | solution.py:527
  40.8 1.4 %collective-permute-start.6 = (bf16[16,16,192]{2,1,0:T(8,128)(2,1)S(1)}, bf16[16,16,192]{2,1,0:T(8,128)(2,1)S(1)}, u32[]{:S(2)}, u32[]{:S(2)}) collective-permute-start(bf16[16,16,192]{2,1,0:T(8,128)(2,1)S(1)} %get-tuple-element.80), channel_id=1, source_target_pairs={{0,1},{1,0},{2,3},{3,2},{4,5},{5,4},{6,7},{7,6},{8,9},{9,8},{10,11... | collective-permute-start | bytes 294920 | tf_op jit(solution)/shard_map/ppermute | solution.py:514
  42.3 10.4 %collective-permute-start.7 = (bf16[3,216,128]{2,1,0:T(8,128)(2,1)S(1)}, bf16[3,216,128]{2,1,0:T(8,128)(2,1)S(1)}, u32[]{:S(2)}, u32[]{:S(2)}) collective-permute-start(bf16[3,216,128]{2,1,0:T(8,128)(2,1)S(1)} %get-tuple-element.83), channel_id=1, source_target_pairs={{0,2},{2,0},{4,6},{6,4},{8,10},{10,8},{12,14},{14,12},{1,3},{3,1},... | collective-permute-start | bytes 497672 | tf_op jit(solution)/shard_map/ppermute | solution.py:528
  45.3 7.4 %collective-permute-start.8 = (bf16[3,216,128]{2,1,0:T(8,128)(2,1)S(1)}, bf16[3,216,128]{2,1,0:T(8,128)(2,1)S(1)}, u32[]{:S(2)}, u32[]{:S(2)}) collective-permute-start(bf16[3,216,128]{2,1,0:T(8,128)(2,1)S(1)} %get-tuple-element.84), channel_id=1, source_target_pairs={{2,4},{4,2},{6,8},{8,6},{10,12},{12,10},{3,5},{5,3},{7,9},{9,7},{1... | collective-permute-start | bytes 497672 | tf_op jit(solution)/shard_map/ppermute | solution.py:527
  56.6 1.4 %collective-permute-start.9 = (bf16[16,16,192]{2,1,0:T(8,128)(2,1)S(1)}, bf16[16,16,192]{2,1,0:T(8,128)(2,1)S(1)}, u32[]{:S(2)}, u32[]{:S(2)}) collective-permute-start(bf16[16,16,192]{2,1,0:T(8,128)(2,1)S(1)} %get-tuple-element.90), channel_id=1, source_target_pairs={{0,1},{1,0},{2,3},{3,2},{4,5},{5,4},{6,7},{7,6},{8,9},{9,8},{10,11... | collective-permute-start | bytes 294920 | tf_op jit(solution)/shard_map/ppermute | solution.py:514
  58.1 10.2 %collective-permute-start.10 = (bf16[3,216,128]{2,1,0:T(8,128)(2,1)S(1)}, bf16[3,216,128]{2,1,0:T(8,128)(2,1)S(1)}, u32[]{:S(2)}, u32[]{:S(2)}) collective-permute-start(bf16[3,216,128]{2,1,0:T(8,128)(2,1)S(1)} %get-tuple-element.93), channel_id=1, source_target_pairs={{0,2},{2,0},{4,6},{6,4},{8,10},{10,8},{12,14},{14,12},{1,3},{3,1},... | collective-permute-start | bytes 497672 | tf_op jit(solution)/shard_map/ppermute | solution.py:528
  61.0 7.4 %collective-permute-start.11 = (bf16[3,216,128]{2,1,0:T(8,128)(2,1)S(1)}, bf16[3,216,128]{2,1,0:T(8,128)(2,1)S(1)}, u32[]{:S(2)}, u32[]{:S(2)}) collective-permute-start(bf16[3,216,128]{2,1,0:T(8,128)(2,1)S(1)} %get-tuple-element.94), channel_id=1, source_target_pairs={{2,4},{4,2},{6,8},{8,6},{10,12},{12,10},{3,5},{5,3},{7,9},{9,7},{1... | collective-permute-start | bytes 497672 | tf_op jit(solution)/shard_map/ppermute | solution.py:527

commit v7 on v6

--- a/solution.py
+++ b/solution.py
@@ -141,7 +141,7 @@
         for j in range(1, 1 + EARLY):
             beside(j)
 
-    @pl.loop(1 + EARLY, last)
+    @pl.loop(1 + EARLY, last, unroll=2)
     def _(j):
         both(j, *plane_windows(x0, x1, pl.multiple_of(j * 8, 8)))
 

time: 84.4 us -> 83.8 us (level)
  transfers between devices with their start and end apart: 12 -> 12, of which waited for: 6 -> 7; matrix products, arithmetic and copies ran while one was open for 0% -> 0% of each run, Pallas kernels for 32% -> 31%
where the time goes in v7:
time: 83.8 us; the launch traced here: 83.5 us
  Pallas kernels  49.3 us (59%)
  starting transfers between devices  16.7 us (20%)
  blocking collectives  11.1 us (13%)
  waiting for transfers between devices  5.36 us (6%)
  between operations  1.02 us (1%)
    pallas_call x17, Pallas kernels, call(): pl.pallas_call(kernel, out_shape=out_shape, in_specs=in_specs, out_specs=...  47.4 us
    ppermute x4, starting transfers between devices, exchange(): halo_a = lax.ppermute(send_a, 'lat', swap_a)  12.9 us
    all_to_all x1, blocking collectives, on_device(): tile = lax.all_to_all(tile, ('lat', 'lon'), 0, 0, tiled=True)  11.1 us
    ppermute x4, waiting for transfers between devices, exchange(): halo_a = lax.ppermute(send_a, 'lat', swap_a)  4.12 us
    ppermute x4, starting transfers between devices, exchange(): halo_b = lax.ppermute(send_b, 'lat', swap_b)  3.04 us
    pallas_call x1, Pallas kernels, on_device(): pl.pallas_call(functools.partial(scale_kernel, total), out_shape=[jax.Sha...  1.88 us
  transfers between devices with their start and end apart: 12, of which 7 were waited for; matrix products, arithmetic and copies ran while one was open for 0% of the time, Pallas kernels for 31%

profile of v7, /device:TPU:0, one launch (start us, length us, event | category | flops | bytes accessed | tf_op | source)
XLA Modules:
  0.0 83.5 jit_solution(15086158286394506399)
XLA Ops:
  0.6 3.7 %edges.1 = (f32[16,128,192]{2,1,0:T(8,128)S(1)}, bf16[16,16,192]{2,1,0:T(8,128)(2,1)S(1)}, bf16[3,216,128]{2,1,0:T(8,128)(2,1)S(1)}, bf16[3,216,128]{2,1,0:T(8,1...) custom-call(f32[16,192,128]{2,1,0:T(8,128)} %bitcast.11, ...), custom_call_target="tpu_custom_call" | custom-call | bytes 4000000 | tf_op jit(solution)/shard_map/edges/pallas_call | solution.py:502
  4.3 0.0 copy-start.2
  4.3 0.0 copy-start.5
  4.3 0.5 collective-permute-start
  4.8 1.0 %planes.4 = (f32[16,128,128]{2,1,0:T(8,128)S(1)}, f32[11,128,128]{2,1,0:T(8,128)S(1)}, f32[16,16,192]{2,1,0:T(8,128)S(1)}) custom-call(f32[16,128,192]{2,1,0:T(8,128)S(1)} %get-tuple-element.52.f_ref.t_ref, f32[2,49,8,128]{3,2,1,0:T(8,128)S(1)} %get-tuple-element.53.k0, f32[2,2,49,8,128]{4,3,2,1,0:T(8,128)S(1)} %get-tuple-element.54.k1), custom_call_target="tpu_custom_call" | custom-call | flops 4816896 | bytes 4000000 | tf_op jit(solution)/shard_map/planes/pallas_call | solution.py:502
  5.8 0.0 collective-permute-done.lon_ref
  5.8 0.1 extend.4
  5.9 2.9 %collective-permute-start.1 = (bf16[3,216,128]{2,1,0:T(8,128)(2,1)S(1)}, bf16[3,216,128]{2,1,0:T(8,128)(2,1)S(1)}, u32[]{:S(2)}, u32[]{:S(2)}) collective-permute-start(bf16[3,216,128]{2,1,0:T(8,128)(2,1)S(1)} %get-tuple-element.62), channel_id=1, source_target_pairs={{0,2},{2,0},{4,6},{6,4},{8,10},{10,8},{12,14},{14,12},{1,3},{3,1},... | collective-permute-start | bytes 497672 | tf_op jit(solution)/shard_map/ppermute | solution.py:528
  8.8 0.7 collective-permute-start.2
  9.5 0.0 copy-start
  9.5 0.0 copy-start.1
  9.5 0.0 copy-start.3
  9.5 0.0 copy-start.4
  9.5 6.5 %conv_first.1 = (f32[16,128,192]{2,1,0:T(8,128)S(1)}, f32[1,192]{1,0:T(1,128)S(1)}, bf16[2,16,128,192]{3,2,1,0:T(8,128)(2,1)S(1)}, bf16[2,16,128,768]{3,2,1,0:T(8,128)(2,1)S(1)}) custom-call(f32[2,128]{1,0:T(2,128)S(1)} %copy-done.5, f32[16,128,192]{2,1,0:T(8,128)S(1)} %get-tuple-element.52.f_ref.t_ref, f32[16,128,128]{2,1,0:T(8,128)S(1)} %get-tuple-element.55.x0, ...), custom_call_target="tpu_custom_call" | custom-call | flops 38535168 | bytes 4000000 | tf_op jit(solution)/shard_map/conv_first/pallas_call | solution.py:502
  16.1 0.1 collective-permute-done.1.a_ref
  16.2 0.0 collective-permute-done.2.b_ref
  16.2 4.3 %tangent0.1 = (f32[16,128,192]{2,1,0:T(8,128)S(1)}, bf16[16,16,192]{2,1,0:T(8,128)(2,1)S(1)}, bf16[3,216,128]{2,1,0:T(8,128)(2,1)S(1)}, bf16[3,216,128]{2,1,0:T(8,128)(2,1)S(1)}) custom-call(f32[2,128]{1,0:T(2,128)S(1)} %copy-done.5, f32[16,128,192]{2,1,0:T(8,128)S(1)} %get-tuple-element.59.acc_ref, bf16[3,216,128]{2,1,0:T(8,128)(2,1)S(1)} %collective-permute-done.1.a_ref, ...), custom_call_target="tpu_custom_call" | custom-call | flops 1207959552 | bytes 4000000 | tf_op jit(solution)/shard_map/tangent0/pallas_call | solution.py:502
  20.5 0.1 collective-permute-start.3
  20.6 1.0 %planes.5 = (f32[16,128,128]{2,1,0:T(8,128)S(1)}, f32[11,128,128]{2,1,0:T(8,128)S(1)}, f32[16,16,192]{2,1,0:T(8,128)S(1)}) custom-call(f32[16,128,192]{2,1,0:T(8,128)S(1)} %get-tuple-element.67.f_ref.t_ref, f32[2,49,8,128]{3,2,1,0:T(8,128)S(1)} %get-tuple-element.53.k0, f32[2,2,49,8,128]{4,3,2,1,0:T(8,128)S(1)} %get-tuple-element.54.k1), custom_call_target="tpu_custom_call" | custom-call | flops 4816896 | bytes 4000000 | tf_op jit(solution)/shard_map/planes/pallas_call | solution.py:502
  21.6 0.4 collective-permute-done.3.lon_ref
  21.9 0.1 extend.5
  22.0 4.2 %collective-permute-start.4 = (bf16[3,216,128]{2,1,0:T(8,128)(2,1)S(1)}, bf16[3,216,128]{2,1,0:T(8,128)(2,1)S(1)}, u32[]{:S(2)}, u32[]{:S(2)}) collective-permute-start(bf16[3,216,128]{2,1,0:T(8,128)(2,1)S(1)} %get-tuple-element.74), channel_id=1, source_target_pairs={{0,2},{2,0},{4,6},{6,4},{8,10},{10,8},{12,14},{14,12},{1,3},{3,1},... | collective-permute-start | bytes 497672 | tf_op jit(solution)/shard_map/ppermute | solution.py:528
  26.2 0.8 %collective-permute-start.5 = (bf16[3,216,128]{2,1,0:T(8,128)(2,1)S(1)}, bf16[3,216,128]{2,1,0:T(8,128)(2,1)S(1)}, u32[]{:S(2)}, u32[]{:S(2)}) collective-permute-start(bf16[3,216,128]{2,1,0:T(8,128)(2,1)S(1)} %get-tuple-element.75), channel_id=1, source_target_pairs={{2,4},{4,2},{6,8},{8,6},{10,12},{12,10},{3,5},{5,3},{7,9},{9,7},{1... | collective-permute-start | bytes 497672 | tf_op jit(solution)/shard_map/ppermute | solution.py:527
  27.1 5.3 %conv1.1.acc_ref = f32[16,128,192]{2,1,0:T(8,128)S(1)} custom-call(f32[16,128,128]{2,1,0:T(8,128)S(1)} %get-tuple-element.68.x0, f32[11,128,128]{2,1,0:T(8,128)S(1)} %get-tuple-element.69.x1, f32[16,16,192]{2,1,0:T(8,128)S(1)} %get-tuple-element.70.early_ref.after_ref, bf16[16,16,192]{2,1,0:T(8,128)(2,1)S(1)} %collective-permute-done.3.lon_ref, ...), custom_call_target="tpu_custom_call" | custom-call | flops 38535168 | bytes 4000000 | tf_op jit(solution)/shard_map/conv1/pallas_call | solution.py:502
  32.3 1.3 %collective-permute-done.4.a_ref = bf16[3,216,128]{2,1,0:T(8,128)(2,1)S(1)} collective-permute-done((bf16[3,216,128]{2,1,0:T(8,128)(2,1)S(1)}, bf16[3,216,128]{2,1,0:T(8,128)(2,1)S(1)}, u32[]{:S(2)}, u32[]{:S(2)}) %collective-permute-start.4) | collective-permute-done | bytes 165920 | tf_op jit(solution)/shard_map/ppermute | solution.py:528
  33.6 0.0 collective-permute-done.5.b_ref
  33.6 6.6 %tangent1.1 = (f32[16,128,192]{2,1,0:T(8,128)S(1)}, bf16[16,128,192]{2,1,0:T(8,128)(2,1)S(1)}, f32[1,192]{1,0:T(1,128)S(1)}, bf16[16,16,192]{2,1,0:T(8,128)(2,1)...) custom-call(f32[2,128]{1,0:T(2,128)S(1)} %copy-done.5, f32[16,128,192]{2,1,0:T(8,128)S(1)} %conv1.1.acc_ref, ...), custom_call_target="tpu_custom_call" | custom-call | flops 1207959552 | bytes 4000000 | tf_op jit(solution)/shard_map/tangent1/pallas_call | solution.py:502
  40.2 0.1 collective-permute-start.6
  40.3 0.9 %planes.6 = (f32[16,128,128]{2,1,0:T(8,128)S(1)}, f32[11,128,128]{2,1,0:T(8,128)S(1)}, f32[16,16,192]{2,1,0:T(8,128)S(1)}) custom-call(bf16[16,128,192]{2,1,0:T(8,128)(2,1)S(1)} %get-tuple-element.76.f_ref, f32[2,49,8,128]{3,2,1,0:T(8,128)S(1)} %get-tuple-element.53.k0, f32[2,2,49,8,128]{4,3,2,1,0:T(8,128)S(1)} %get-tuple-element.54.k1), custom_call_target="tpu_custom_call" | custom-call | flops 4816896 | bytes 4000000 | tf_op jit(solution)/shard_map/planes/pallas_call | solution.py:502
  41.2 0.4 collective-permute-done.6.lon_ref
  41.6 0.1 extend.6
  41.7 3.0 %collective-permute-start.7 = (bf16[3,216,128]{2,1,0:T(8,128)(2,1)S(1)}, bf16[3,216,128]{2,1,0:T(8,128)(2,1)S(1)}, u32[]{:S(2)}, u32[]{:S(2)}) collective-permute-start(bf16[3,216,128]{2,1,0:T(8,128)(2,1)S(1)} %get-tuple-element.83), channel_id=1, source_target_pairs={{0,2},{2,0},{4,6},{6,4},{8,10},{10,8},{12,14},{14,12},{1,3},{3,1},... | collective-permute-start | bytes 497672 | tf_op jit(solution)/shard_map/ppermute | solution.py:528
  44.8 0.7 collective-permute-start.8
  45.4 5.2 %convt1.1.acc_ref = f32[16,128,192]{2,1,0:T(8,128)S(1)} custom-call(f32[16,128,128]{2,1,0:T(8,128)S(1)} %get-tuple-element.77.x0, f32[11,128,128]{2,1,0:T(8,128)S(1)} %get-tuple-element.78.x1, f32[16,16,192]{2,1,0:T(8,128)S(1)} %get-tuple-element.79.early_ref.after_ref, bf16[16,16,192]{2,1,0:T(8,128)(2,1)S(1)} %collective-permute-done.6.lon_ref, ...), custom_call_target="tpu_custom_call" | custom-call | flops 38535168 | bytes 4000000 | tf_op jit(solution)/shard_map/convt1/pallas_call | solution.py:502
  50.7 1.5 %collective-permute-done.7.a_ref = bf16[3,216,128]{2,1,0:T(8,128)(2,1)S(1)} collective-permute-done((bf16[3,216,128]{2,1,0:T(8,128)(2,1)S(1)}, bf16[3,216,128]{2,1,0:T(8,128)(2,1)S(1)}, u32[]{:S(2)}, u32[]{:S(2)}) %collective-permute-start.7) | collective-permute-done | bytes 165920 | tf_op jit(solution)/shard_map/ppermute | solution.py:528
  52.2 0.0 collective-permute-done.8.b_ref
  52.2 3.9 %adjoint0.1 = (f32[16,128,192]{2,1,0:T(8,128)S(1)}, bf16[16,128,192]{2,1,0:T(8,128)(2,1)S(1)}, bf16[16,16,192]{2,1,0:T(8,128)(2,1)S(1)}, bf16[3,216,128]{2,1,0:T(8,128)(2,1)S(1)}, bf16[3,216,128]{2,1,0:T(8,128)(2,1)S(1)}) custom-call(f32[16,128,192]{2,1,0:T(8,128)S(1)} %convt1.1.acc_ref, bf16[3,216,128]{2,1,0:T(8,128)(2,1)S(1)} %collective-permute-done.7.a_ref, ...), custom_call_target="tpu_custom_call" | custom-call | flops 1207959552 | bytes 4000000 | tf_op jit(solution)/shard_map/adjoint0/pallas_call | solution.py:502
  56.1 0.1 collective-permute-start.9
  56.2 0.9 %planes.7 = (f32[16,128,128]{2,1,0:T(8,128)S(1)}, f32[11,128,128]{2,1,0:T(8,128)S(1)}, f32[16,16,192]{2,1,0:T(8,128)S(1)}) custom-call(bf16[16,128,192]{2,1,0:T(8,128)(2,1)S(1)} %get-tuple-element.86.f_ref, f32[2,49,8,128]{3,2,1,0:T(8,128)S(1)} %get-tuple-element.53.k0, f32[2,2,49,8,128]{4,3,2,1,0:T(8,128)S(1)} %get-tuple-element.54.k1), custom_call_target="tpu_custom_call" | custom-call | flops 4816896 | bytes 4000000 | tf_op jit(solution)/shard_map/planes/pallas_call | solution.py:502
  57.1 0.4 collective-permute-done.9.lon_ref
  57.5 0.1 extend.7
  57.6 2.8 %collective-permute-start.10 = (bf16[3,216,128]{2,1,0:T(8,128)(2,1)S(1)}, bf16[3,216,128]{2,1,0:T(8,128)(2,1)S(1)}, u32[]{:S(2)}, u32[]{:S(2)}) collective-permute-start(bf16[3,216,128]{2,1,0:T(8,128)(2,1)S(1)} %get-tuple-element.93), channel_id=1, source_target_pairs={{0,2},{2,0},{4,6},{6,4},{8,10},{10,8},{12,14},{14,12},{1,3},{3,1},... | collective-permute-start | bytes 497672 | tf_op jit(solution)/shard_map/ppermute | solution.py:528
  60.4 0.9 %collective-permute-start.11 = (bf16[3,216,128]{2,1,0:T(8,128)(2,1)S(1)}, bf16[3,216,128]{2,1,0:T(8,128)(2,1)S(1)}, u32[]{:S(2)}, u32[]{:S(2)}) collective-permute-start(bf16[3,216,128]{2,1,0:T(8,128)(2,1)S(1)} %get-tuple-element.94), channel_id=1, source_target_pairs={{2,4},{4,2},{6,8},{8,6},{10,12},{12,10},{3,5},{5,3},{7,9},{9,7},{1... | collective-permute-start | bytes 497672 | tf_op jit(solution)/shard_map/ppermute | solution.py:527
  61.3 5.2 %convt0.1.acc_ref = f32[16,128,192]{2,1,0:T(8,128)S(1)} custom-call(f32[16,128,128]{2,1,0:T(8,128)S(1)} %get-tuple-element.87.x0, f32[11,128,128]{2,1,0:T(8,128)S(1)} %get-tuple-element.88.x1, f32[16,16,192]{2,1,0:T(8,128)S(1)} %get-tuple-element.89.early_ref.after_ref, bf16[16,16,192]{2,1,0:T(8,128)(2,1)S(1)} %collective-permute-done.9.lon_ref, ...), custom_call_target="tpu_custom_call" | custom-call | flops 38535168 | bytes 4000000 | tf_op jit(solution)/shard_map/convt0/pallas_call | solution.py:502
  66.5 1.2 %collective-permute-done.10.a_ref = bf16[3,216,128]{2,1,0:T(8,128)(2,1)S(1)} collective-permute-done((bf16[3,216,128]{2,1,0:T(8,128)(2,1)S(1)}, bf16[3,216,128]{2,1,0:T(8,128)(2,1)S(1)}, u32[]{:S(2)}, u32[]{:S(2)}) %collective-permute-start.10) | collective-permute-done | bytes 165920 | tf_op jit(solution)/shard_map/ppermute | solution.py:528
  67.8 2.5 %final.1 = (f32[16,192,128]{2,1,0:T(8,128)S(1)}, f32[16,1,128]{2,1,0:T(1,128)S(1)}) custom-call(f32[2,128]{1,0:T(2,128)S(1)} %copy-done.5, f32[16,128,192]{2,1,0:T(8,128)S(1)} %convt0.1.acc_ref, bf16[3,216,128]{2,1,0:T(8,128)(2,1)S(1)} %collective-permute-done.10.a_ref, bf16[3,216,128]{2,1,0:T(8,128)(2,1)S(1)} %collective-permute-done.11.b_ref, ...), custom_call_target="tpu_custom_call" | custom-call | bytes 4000000 | tf_op jit(solution)/shard_map/final/pallas_call | solution.py:502
  70.3 11.1 %all_to_all.5.tile_ref = f32[16,1,128]{2,1,0:T(1,128)S(1)} all-to-all(f32[16,1,128]{2,1,0:T(1,128)S(1)} %get-tuple-element.98), channel_id=1, replica_groups=mesh['grp'=2,'lat'=8,'lon'=2] {'lat','lon'}, dimensions={0} | all-to-all | bytes 16384 | tf_op jit(solution)/shard_map/all_to_all | solution.py:592
  81.4 1.9 %scale.1 = (f32[16,192,128]{2,1,0:T(8,128)}, f32[1,128]{1,0:T(1,128)}) custom-call(f32[16,1,128]{2,1,0:T(1,128)S(1)} %all_to_all.5.tile_ref, f32[16,192,128]{2,1,0:T(8,128)S(1)} %get-tuple-element.99.w_ref), custom_call_target="tpu_custom_call" | custom-call | tf_op jit(solution)/shard_map/scale/pallas_call | solution.py:593
  (7 shorter events, 0.0 us)
Async XLA Ops:
  4.3 5.2 %copy-start.2 = (bf16[2,16,128,192]{2,3,1,0:T(8,128)(2,1)S(1)}, bf16[2,16,128,192]{2,3,1,0:T(8,128)(2,1)}, u32[]{:S(2)}) copy-start(bf16[2,16,128,192]{2,3,1,0:T(8,128)(2,1)} %param.16) | copy-start | bytes 4718596
  4.3 5.2 %copy-start.5 = (f32[2,128]{1,0:T(2,128)S(1)}, f32[2,128]{1,0:T(2,128)}, u32[]{:S(2)}) copy-start(f32[2,128]{1,0:T(2,128)} %constant.2.clone.area_ref) | copy-start | bytes 3076
  4.3 1.5 %collective-permute-start = (bf16[16,16,192]{2,1,0:T(8,128)(2,1)S(1)}, bf16[16,16,192]{2,1,0:T(8,128)(2,1)S(1)}, u32[]{:S(2)}, u32[]{:S(2)}) collective-permute-start(bf16[16,16,192]{2,1,0:T(8,128)(2,1)S(1)} %get-tuple-element.58), channel_id=1, source_target_pairs={{0,1},{1,0},{2,3},{3,2},{4,5},{5,4},{6,7},{7,6},{8,9},{9,8},{10,11... | collective-permute-start | bytes 294920 | tf_op jit(solution)/shard_map/ppermute | solution.py:514
  5.9 10.3 %collective-permute-start.1 = (bf16[3,216,128]{2,1,0:T(8,128)(2,1)S(1)}, bf16[3,216,128]{2,1,0:T(8,128)(2,1)S(1)}, u32[]{:S(2)}, u32[]{:S(2)}) collective-permute-start(bf16[3,216,128]{2,1,0:T(8,128)(2,1)S(1)} %get-tuple-element.62), channel_id=1, source_target_pairs={{0,2},{2,0},{4,6},{6,4},{8,10},{10,8},{12,14},{14,12},{1,3},{3,1},... | collective-permute-start | bytes 497672 | tf_op jit(solution)/shard_map/ppermute | solution.py:528
  8.8 7.4 %collective-permute-start.2 = (bf16[3,216,128]{2,1,0:T(8,128)(2,1)S(1)}, bf16[3,216,128]{2,1,0:T(8,128)(2,1)S(1)}, u32[]{:S(2)}, u32[]{:S(2)}) collective-permute-start(bf16[3,216,128]{2,1,0:T(8,128)(2,1)S(1)} %get-tuple-element.63), channel_id=1, source_target_pairs={{2,4},{4,2},{6,8},{8,6},{10,12},{12,10},{3,5},{5,3},{7,9},{9,7},{1... | collective-permute-start | bytes 497672 | tf_op jit(solution)/shard_map/ppermute | solution.py:527
  9.5 6.7 %copy-start = (bf16[2,192,768]{2,1,0:T(8,128)(2,1)S(1)}, bf16[2,192,768]{2,1,0:T(8,128)(2,1)}, u32[]{:S(2)}) copy-start(bf16[2,192,768]{2,1,0:T(8,128)(2,1)} %rest_4_.5) | copy-start | bytes 1769476
  9.5 6.7 %copy-start.1 = (bf16[2,768,192]{1,2,0:T(8,128)(2,1)S(1)}, bf16[2,768,192]{1,2,0:T(8,128)(2,1)}, u32[]{:S(2)}) copy-start(bf16[2,768,192]{1,2,0:T(8,128)(2,1)} %param.14) | copy-start | bytes 1769476
  9.5 6.7 %copy-start.3 = (f32[2,192]{1,0:T(2,128)S(1)}, f32[2,192]{1,0:T(2,128)}, u32[]{:S(2)}) copy-start(f32[2,192]{1,0:T(2,128)} %rest_3_.5) | copy-start | bytes 4612
  9.5 6.7 %copy-start.4 = (f32[2,192]{1,0:T(2,128)S(1)}, f32[2,192]{1,0:T(2,128)}, u32[]{:S(2)}) copy-start(f32[2,192]{1,0:T(2,128)} %rest_6_.5) | copy-start | bytes 4612
  20.5 1.4 %collective-permute-start.3 = (bf16[16,16,192]{2,1,0:T(8,128)(2,1)S(1)}, bf16[16,16,192]{2,1,0:T(8,128)(2,1)S(1)}, u32[]{:S(2)}, u32[]{:S(2)}) collective-permute-start(bf16[16,16,192]{2,1,0:T(8,128)(2,1)S(1)} %get-tuple-element.71), channel_id=1, source_target_pairs={{0,1},{1,0},{2,3},{3,2},{4,5},{5,4},{6,7},{7,6},{8,9},{9,8},{10,11... | collective-permute-start | bytes 294920 | tf_op jit(solution)/shard_map/ppermute | solution.py:514
  22.0 11.6 %collective-permute-start.4 = (bf16[3,216,128]{2,1,0:T(8,128)(2,1)S(1)}, bf16[3,216,128]{2,1,0:T(8,128)(2,1)S(1)}, u32[]{:S(2)}, u32[]{:S(2)}) collective-permute-start(bf16[3,216,128]{2,1,0:T(8,128)(2,1)S(1)} %get-tuple-element.74), channel_id=1, source_target_pairs={{0,2},{2,0},{4,6},{6,4},{8,10},{10,8},{12,14},{14,12},{1,3},{3,1},... | collective-permute-start | bytes 497672 | tf_op jit(solution)/shard_map/ppermute | solution.py:528
  26.2 7.4 %collective-permute-start.5 = (bf16[3,216,128]{2,1,0:T(8,128)(2,1)S(1)}, bf16[3,216,128]{2,1,0:T(8,128)(2,1)S(1)}, u32[]{:S(2)}, u32[]{:S(2)}) collective-permute-start(bf16[3,216,128]{2,1,0:T(8,128)(2,1)S(1)} %get-tuple-element.75), channel_id=1, source_target_pairs={{2,4},{4,2},{6,8},{8,6},{10,12},{12,10},{3,5},{5,3},{7,9},{9,7},{1... | collective-permute-start | bytes 497672 | tf_op jit(solution)/shard_map/ppermute | solution.py:527
  40.2 1.4 %collective-permute-start.6 = (bf16[16,16,192]{2,1,0:T(8,128)(2,1)S(1)}, bf16[16,16,192]{2,1,0:T(8,128)(2,1)S(1)}, u32[]{:S(2)}, u32[]{:S(2)}) collective-permute-start(bf16[16,16,192]{2,1,0:T(8,128)(2,1)S(1)} %get-tuple-element.80), channel_id=1, source_target_pairs={{0,1},{1,0},{2,3},{3,2},{4,5},{5,4},{6,7},{7,6},{8,9},{9,8},{10,11... | collective-permute-start | bytes 294920 | tf_op jit(solution)/shard_map/ppermute | solution.py:514
  41.7 10.4 %collective-permute-start.7 = (bf16[3,216,128]{2,1,0:T(8,128)(2,1)S(1)}, bf16[3,216,128]{2,1,0:T(8,128)(2,1)S(1)}, u32[]{:S(2)}, u32[]{:S(2)}) collective-permute-start(bf16[3,216,128]{2,1,0:T(8,128)(2,1)S(1)} %get-tuple-element.83), channel_id=1, source_target_pairs={{0,2},{2,0},{4,6},{6,4},{8,10},{10,8},{12,14},{14,12},{1,3},{3,1},... | collective-permute-start | bytes 497672 | tf_op jit(solution)/shard_map/ppermute | solution.py:528
  44.8 7.4 %collective-permute-start.8 = (bf16[3,216,128]{2,1,0:T(8,128)(2,1)S(1)}, bf16[3,216,128]{2,1,0:T(8,128)(2,1)S(1)}, u32[]{:S(2)}, u32[]{:S(2)}) collective-permute-start(bf16[3,216,128]{2,1,0:T(8,128)(2,1)S(1)} %get-tuple-element.84), channel_id=1, source_target_pairs={{2,4},{4,2},{6,8},{8,6},{10,12},{12,10},{3,5},{5,3},{7,9},{9,7},{1... | collective-permute-start | bytes 497672 | tf_op jit(solution)/shard_map/ppermute | solution.py:527
  56.1 1.4 %collective-permute-start.9 = (bf16[16,16,192]{2,1,0:T(8,128)(2,1)S(1)}, bf16[16,16,192]{2,1,0:T(8,128)(2,1)S(1)}, u32[]{:S(2)}, u32[]{:S(2)}) collective-permute-start(bf16[16,16,192]{2,1,0:T(8,128)(2,1)S(1)} %get-tuple-element.90), channel_id=1, source_target_pairs={{0,1},{1,0},{2,3},{3,2},{4,5},{5,4},{6,7},{7,6},{8,9},{9,8},{10,11... | collective-permute-start | bytes 294920 | tf_op jit(solution)/shard_map/ppermute | solution.py:514
  57.6 10.2 %collective-permute-start.10 = (bf16[3,216,128]{2,1,0:T(8,128)(2,1)S(1)}, bf16[3,216,128]{2,1,0:T(8,128)(2,1)S(1)}, u32[]{:S(2)}, u32[]{:S(2)}) collective-permute-start(bf16[3,216,128]{2,1,0:T(8,128)(2,1)S(1)} %get-tuple-element.93), channel_id=1, source_target_pairs={{0,2},{2,0},{4,6},{6,4},{8,10},{10,8},{12,14},{14,12},{1,3},{3,1},... | collective-permute-start | bytes 497672 | tf_op jit(solution)/shard_map/ppermute | solution.py:528
  60.4 7.4 %collective-permute-start.11 = (bf16[3,216,128]{2,1,0:T(8,128)(2,1)S(1)}, bf16[3,216,128]{2,1,0:T(8,128)(2,1)S(1)}, u32[]{:S(2)}, u32[]{:S(2)}) collective-permute-start(bf16[3,216,128]{2,1,0:T(8,128)(2,1)S(1)} %get-tuple-element.94), channel_id=1, source_target_pairs={{2,4},{4,2},{6,8},{8,6},{10,12},{12,10},{3,5},{5,3},{7,9},{9,7},{1... | collective-permute-start | bytes 497672 | tf_op jit(solution)/shard_map/ppermute | solution.py:527
